TPU v7x, 256 devices: a whole 4x4x8 slice. The times are simulated.
256 devices in a mesh: src: 2 (over y_lo), tx: 8 (over y_hi, x), ty: 16 (over z, core).
Axes of the slice: x: 4, y: 4 (y_hi: 2, y_lo: 2; y = y_hi * 2 + y_lo), z: 8, core: 2. Of those that a mesh axis runs over, the one named last changes fastest.
Arguments:
- orders: float32 [8, 2, 512, 512], P('src', None, 'tx', 'ty'), may hold values from -0.00390625 to 0.00390625
- offsets: int32 [8, 2], P('src'), may hold values from -8 to 7
- material: int32 [6, 2048, 2048], P(None, 'tx', 'ty'), may hold values from 0 to 3
- e_field: float32 [3, 6, 2048, 2048], P(None, None, 'tx', 'ty'), may hold values from -6 to 6
- h_field: float32 [3, 6, 2048, 2048], P(None, None, 'tx', 'ty'), may hold values from -6 to 6
Outputs:
- e_out: float32 [3, 6, 2048, 2048], P(None, None, 'tx', 'ty')
- h_out: float32 [3, 6, 2048, 2048], P(None, None, 'tx', 'ty')
All inputs are finite; a program needn't handle non-finite values.
Results may differ from a plain program's by a relative error of at most 0.0003.
Values sent between devices are 32-bit elements; how exact they have to be, the bound alone decides.
A program may use at most 128 MiB of HBM per device.

v0:
```python
import math

import jax
import jax.numpy as jnp
from jax import lax
from jax.sharding import PartitionSpec as P
from jax.experimental import pallas as pl
from jax.experimental.pallas import tpu as pltpu

STEPS = 4
ZINJ = 1


COURANT = 0.5
OMEGA = 0.7
PERMITTIVITY = (1.0, 2.6, 11.9, 2.1)
PREC = lax.Precision.HIGH


def passed_along(block, axis, distance):
    devices = range(lax.axis_size(axis))
    route = [((i - distance) % len(devices), i) for i in devices]
    return lax.ppermute(block, axis, route)


def phase_tables(freqs, positions, length):
    product = jnp.mod(freqs[:, None] * positions[None, :], length)
    angle = product.astype(jnp.float32) * (2.0 * math.pi / length)
    return (jnp.cos(angle), jnp.sin(angle))


def cell_coefficient(material):
    total = jnp.zeros(material.shape, jnp.float32)
    for number in range(len(PERMITTIVITY)):
        total = total + jnp.where(material == number, COURANT / PERMITTIVITY[number], 0.0)
    return total


def ahead(field, rim, axis):
    following = lax.slice_in_dim(field, 1, field.shape[axis], axis=axis)
    return jnp.concatenate([following, rim], axis) - field


def behind(field, rim, axis):
    earlier = lax.slice_in_dim(field, 0, field.shape[axis] - 1, axis=axis)
    return field - jnp.concatenate([rim, earlier], axis)


def neighbour_rims(row_x, col_y, offset):
    got_x = passed_along(row_x, "tx", offset)
    got_y = passed_along(col_y, "ty", offset)
    return (got_x, got_y)


def butterfly_gather(block, axis, order):
    me = lax.axis_index(axis)
    n = lax.axis_size(axis)
    held = block[None]
    for d in order:
        other = lax.ppermute(held, axis, [(i, i ^ d) for i in range(n)])
        low = (me // d) % 2 == 0
        held = jnp.where(low, jnp.concatenate([held, other], 0), jnp.concatenate([other, held], 0))
    return held


def gather_order(n):
    order = []
    d = n // 2
    while d >= 1:
        order.append(d)
        d //= 2
    return order


def chunk_starts(order, size):
    starts = []
    for q in range(2 ** len(order)):
        c = sum(order[t] for t in range(len(order)) if (q >> t) & 1)
        starts.append(c * size)
    return jnp.array(starts, dtype=jnp.int32)


def chunk_tables(order, size, total, positions, length):
    c1, s1 = phase_tables(chunk_starts(order, size), positions, length)
    c2, s2 = phase_tables(jnp.arange(size, dtype=jnp.int32) - total // 2, positions, length)
    cos_t = c1[:, None, :] * c2[None, :, :] - s1[:, None, :] * s2[None, :, :]
    sin_t = s1[:, None, :] * c2[None, :, :] + c1[:, None, :] * s2[None, :, :]
    return cos_t, sin_t


def injection_plane(orders, offsets, cells_x, cells_y):
    points, _, rows_kx, cols_ky = orders.shape
    n_tx = lax.axis_size("tx")
    n_ty = lax.axis_size("ty")
    full_x = cells_x * n_tx
    full_y = cells_y * n_ty
    order_y = gather_order(n_ty)
    amp = butterfly_gather(orders, "ty", order_y)
    a_re = amp[:, :, 0]
    a_im = amp[:, :, 1]
    y_pos = lax.axis_index("ty") * cells_y + jnp.arange(cells_y, dtype=jnp.int32)
    by_c, by_s = chunk_tables(order_y, cols_ky, cols_ky * n_ty, y_pos, full_y)
    sy_c, sy_s = phase_tables(offsets[:, 1], y_pos, full_y)
    m_re = jnp.einsum("cpkj,cjy->pky", a_re, by_c, precision=PREC) - jnp.einsum(
        "cpkj,cjy->pky", a_im, by_s, precision=PREC
    )
    m_im = jnp.einsum("cpkj,cjy->pky", a_re, by_s, precision=PREC) + jnp.einsum(
        "cpkj,cjy->pky", a_im, by_c, precision=PREC
    )
    sy_c = sy_c[:, None, :]
    sy_s = sy_s[:, None, :]
    inner = jnp.stack([m_re * sy_c - m_im * sy_s, m_re * sy_s + m_im * sy_c], 1)
    order_x = gather_order(n_tx)
    inner = butterfly_gather(inner, "tx", order_x)
    i_re = inner[:, :, 0]
    i_im = inner[:, :, 1]
    x_pos = lax.axis_index("tx") * cells_x + jnp.arange(cells_x, dtype=jnp.int32)
    bx_c, bx_s = chunk_tables(order_x, rows_kx, rows_kx * n_tx, x_pos, full_x)
    sx_c, sx_s = phase_tables(offsets[:, 0], x_pos, full_x)
    q_re = jnp.einsum("ckx,cpky->pxy", bx_c, i_re, precision=PREC) - jnp.einsum(
        "ckx,cpky->pxy", bx_s, i_im, precision=PREC
    )
    q_im = jnp.einsum("ckx,cpky->pxy", bx_c, i_im, precision=PREC) + jnp.einsum(
        "ckx,cpky->pxy", bx_s, i_re, precision=PREC
    )
    sx_c = sx_c[:, :, None]
    sx_s = sx_s[:, :, None]
    plane = jnp.stack(
        [jnp.sum(q_re * sx_c - q_im * sx_s, 0), jnp.sum(q_re * sx_s + q_im * sx_c, 0)]
    )
    n_src = lax.axis_size("src")
    other = lax.ppermute(plane, "src", [(i, (i + 1) % n_src) for i in range(n_src)])
    return plane + other


def yee_kernel(e_ref, h_ref, coef_ref, plane_ref, xa_ref, xb_ref, yh_ref, eo_ref, ho_ref, ext, cp, tmp):
    layers, cells_x, cells_y = coef_ref.shape
    depth = xa_ref.shape[1]
    rows = cells_x + 2 * depth
    lanes = ext.shape[2]
    slab = layers + 2
    n_field = 6 * layers
    zero = jnp.zeros((rows, lanes), jnp.float32)
    for comp in range(3):
        ext[comp * slab + slab - 1] = zero
        ext[(3 + comp) * slab] = zero
    tmp[...] = jnp.zeros_like(tmp)
    lane = lax.broadcasted_iota(jnp.int32, (rows, cells_y), 1)

    def place(h, slot, own):
        dst = ext if slot is not None else cp
        idx = slot if slot is not None else h - n_field
        dst[idx, 0:cells_x, 0:cells_y] = own
        dst[idx, cells_x:cells_x + depth, 0:cells_y] = xa_ref[h]
        dst[idx, cells_x + depth:rows, 0:cells_y] = xb_ref[h]
        tmp[:, 0:2 * depth] = yh_ref[h].T
        v = tmp[...]
        front = jnp.where(lane < depth, v, 0.0)
        back = jnp.where(lane >= depth, v, 0.0)
        dst[idx, :, cells_y:lanes] = front + pltpu.roll(back, cells_y - 2 * depth, 1)

    def fields(h, carry):
        comp = h // layers
        z = h % layers
        slot = comp * slab + z + 1
        own = jnp.where(comp < 3, e_ref[comp % 3, z], h_ref[comp % 3, z])
        place(h, slot, own)
        return carry

    lax.fori_loop(0, n_field, fields, 0)
    for z in range(layers):
        place(n_field + z, None, coef_ref[z])
    for k in range(2):
        place(n_field + layers + k, None, plane_ref[k])

    ahead_x = lambda f: pltpu.roll(f, rows - 1, 0)
    ahead_y = lambda f: pltpu.roll(f, lanes - 1, 1)
    behind_x = lambda f: pltpu.roll(f, 1, 0)
    behind_y = lambda f: pltpu.roll(f, 1, 1)
    ex_, ey_, ez_, hx_, hy_, hz_ = (c * slab for c in range(6))

    for step in range(STEPS):
        def h_update(z, carry):
            s = z + 1
            e_x = ext[ex_ + s]
            e_y = ext[ey_ + s]
            e_z = ext[ez_ + s]
            ext[hx_ + s] = ext[hx_ + s] - COURANT * ((ahead_y(e_z) - e_z) - (ext[ey_ + s + 1] - e_y))
            ext[hy_ + s] = ext[hy_ + s] - COURANT * ((ext[ex_ + s + 1] - e_x) - (ahead_x(e_z) - e_z))
            ext[hz_ + s] = ext[hz_ + s] - COURANT * ((ahead_x(e_y) - e_y) - (ahead_y(e_x) - e_x))
            return carry

        def e_update(z, carry):
            s = z + 1
            h_x = ext[hx_ + s]
            h_y = ext[hy_ + s]
            h_z = ext[hz_ + s]
            c = cp[z]
            ext[ex_ + s] = ext[ex_ + s] + c * ((h_z - behind_y(h_z)) - (h_y - ext[hy_ + s - 1]))
            ext[ey_ + s] = ext[ey_ + s] + c * ((h_x - ext[hx_ + s - 1]) - (h_z - behind_x(h_z)))
            ext[ez_ + s] = ext[ez_ + s] + c * ((h_y - behind_x(h_y)) - (h_x - behind_y(h_x)))
            return carry

        lax.fori_loop(0, layers, h_update, 0)
        lax.fori_loop(0, layers, e_update, 0)
        cosine = math.cos(OMEGA * (step + 1))
        sine = math.sin(OMEGA * (step + 1))
        p_re = cp[layers]
        p_im = cp[layers + 1]
        s = ZINJ + 1
        ext[ex_ + s] = ext[ex_ + s] + COURANT * (cosine * p_re - sine * p_im)
        ext[ey_ + s] = ext[ey_ + s] + COURANT * (sine * p_re + cosine * p_im)

    for comp in range(3):
        for z in range(layers):
            eo_ref[comp, z] = ext[comp * slab + z + 1, 0:cells_x, 0:cells_y]
            ho_ref[comp, z] = ext[(3 + comp) * slab + z + 1, 0:cells_x, 0:cells_y]


def exchange_halos(parts, depth):
    n_tx = lax.axis_size("tx")
    n_ty = lax.axis_size("ty")

    def from_offset(block, dx, dy):
        pairs = []
        for i in range(n_tx):
            for j in range(n_ty):
                src_dev = ((i + dx) % n_tx) * n_ty + (j + dy) % n_ty
                pairs.append((src_dev, i * n_ty + j))
        return lax.ppermute(block, ("tx", "ty"), pairs)

    head = slice(0, depth)
    tail = slice(-depth, None)
    xa = from_offset(parts[:, head, :], 1, 0)
    xb = from_offset(parts[:, tail, :], -1, 0)
    t = lambda b: jnp.swapaxes(b, 1, 2)
    ya = from_offset(t(parts[:, :, head]), 0, 1)
    yb = from_offset(t(parts[:, :, tail]), 0, -1)
    aa = from_offset(t(parts[:, head, head]), 1, 1)
    ab = from_offset(t(parts[:, head, tail]), 1, -1)
    ba = from_offset(t(parts[:, tail, head]), -1, 1)
    bb = from_offset(t(parts[:, tail, tail]), -1, -1)
    y_ahead = jnp.concatenate([ya, aa, ba], 2)
    y_behind = jnp.concatenate([yb, ab, bb], 2)
    return xa, xb, jnp.concatenate([y_ahead, y_behind], 1)


def per_device(orders, offsets, material, e_field, h_field):
    layers, cells_x, cells_y = material.shape
    plane = injection_plane(orders, offsets, cells_x, cells_y)
    coefficient = cell_coefficient(material)
    parts = jnp.concatenate(
        [
            e_field.reshape(3 * layers, cells_x, cells_y),
            h_field.reshape(3 * layers, cells_x, cells_y),
            coefficient,
            plane,
        ],
        0,
    )
    depth = STEPS
    xa, xb, yh = exchange_halos(parts, depth)
    rows = cells_x + 2 * depth
    lanes = 2 * cells_y
    vmem = pltpu.MemorySpace.VMEM
    spec = pl.BlockSpec(memory_space=vmem)
    out = jax.ShapeDtypeStruct(e_field.shape, jnp.float32)
    return pl.pallas_call(
        yee_kernel,
        out_shape=(out, out),
        in_specs=[spec] * 7,
        out_specs=(spec, spec),
        scratch_shapes=[
            pltpu.VMEM((6 * (layers + 2), rows, lanes), jnp.float32),
            pltpu.VMEM((layers + 2, rows, lanes), jnp.float32),
            pltpu.VMEM((rows, cells_y), jnp.float32),
        ],
        compiler_params=pltpu.CompilerParams(vmem_limit_bytes=64 * 1024 * 1024),
    )(e_field, h_field, coefficient, plane, xa, xb, yh)


def solution(mesh):
    in_specs = (
        P("src", None, "tx", "ty"),
        P("src", None),
        P(None, "tx", "ty"),
        P(None, None, "tx", "ty"),
        P(None, None, "tx", "ty"),
    )
    out_specs = (P(None, None, "tx", "ty"), P(None, None, "tx", "ty"))
    return jax.shard_map(
        per_device, mesh=mesh, in_specs=in_specs, out_specs=out_specs, check_vma=False
    )
```

profile of v0, /device:TPU:1, one launch (start us, length us, event | category | flops | bytes accessed | tf_op | source)
XLA Modules:
  0.0 175.9 jit_solution(11369281038103347695)
XLA Ops:
  0.6 0.0 copy-start.6
  0.6 0.9 copy.50
  1.6 7.8 %collective-permute-start = (f32[1,4,2,64,32]{3,4,0,1,2:T(8,128)S(1)}, f32[1,4,2,64,32]{3,4,0,1,2:T(8,128)S(1)}, u32[]{:S(2)}, u32[]{:S(2)}) collective-permute-start(f32[1,4,2,64,32]{3,4,0,1,2:T(8,128)S(1)} %bitcast.121), channel_id=1, source_target_pairs={{0,8},{1,9},{2,10},{3,11},{4,12},{5,13},{6,14},{7,15},{8,0},{9,1},... | collective-permute-start | bytes 196616 | tf_op jit(solution)/shard_map/ppermute | solution.py:60
  9.4 2.7 %collective-permute-done = f32[1,4,2,64,32]{3,4,0,1,2:T(8,128)S(1)} collective-permute-done((f32[1,4,2,64,32]{3,4,0,1,2:T(8,128)S(1)}, f32[1,4,2,64,32]{3,4,0,1,2:T(8,128)S(1)}, u32[]{:S(2)}, u32[]{:S(2)}) %collective-permute-start) | collective-permute-done | bytes 65568 | tf_op jit(solution)/shard_map/ppermute | solution.py:60
  12.1 5.0 %collective-permute-start.1 = (f32[2,4,2,64,32]{3,4,0,1,2:T(8,128)S(1)}, f32[2,4,2,64,32]{3,4,0,1,2:T(8,128)S(1)}, u32[]{:S(2)}, u32[]{:S(2)}) collective-permute-start(f32[2,4,2,64,32]{3,4,0,1,2:T(8,128)S(1)} %maximum_select_fusion.6), channel_id=1, source_target_pairs={{0,4},{1,5},{2,6},{3,7},{4,0},{5,1},{6,2},{7,3},{8,12},{9,13},{10,... | collective-permute-start | bytes 393224 | tf_op jit(solution)/shard_map/ppermute | solution.py:60
  17.1 0.8 slice_bitcast_fusion.12
  17.8 10.0 %collective-permute-done.1 = f32[2,4,2,64,32]{3,4,0,1,2:T(8,128)S(1)} collective-permute-done((f32[2,4,2,64,32]{3,4,0,1,2:T(8,128)S(1)}, f32[2,4,2,64,32]{3,4,0,1,2:T(8,128)S(1)}, u32[]{:S(2)}, u32[]{:S(2)}) %collective-permute-start.1) | collective-permute-done | bytes 131104 | tf_op jit(solution)/shard_map/ppermute | solution.py:60
  27.8 0.1 maximum_select_fusion.4
  27.9 0.1 collective-permute-start.2
  28.1 0.1 fusion.73
  28.2 12.7 %collective-permute-done.2 = f32[4,4,2,64,32]{3,4,0,1,2:T(8,128)S(1)} collective-permute-done((f32[4,4,2,64,32]{3,4,0,1,2:T(8,128)S(1)}, f32[4,4,2,64,32]{3,4,0,1,2:T(8,128)S(1)}, u32[]{:S(2)}, u32[]{:S(2)}) %collective-permute-start.2) | collective-permute-done | bytes 262176 | tf_op jit(solution)/shard_map/ppermute | solution.py:60
  40.9 0.1 maximum_select_fusion.2
  41.0 1.5 collective-permute-start.3
  42.6 0.1 fusion.66
  42.7 0.2 fusion.59
  42.9 2.0 %collective-permute-done.3 = f32[8,4,2,64,32]{3,4,0,1,2:T(8,128)S(1)} collective-permute-done((f32[8,4,2,64,32]{3,4,0,1,2:T(8,128)S(1)}, f32[8,4,2,64,32]{3,4,0,1,2:T(8,128)S(1)}, u32[]{:S(2)}, u32[]{:S(2)}) %collective-permute-start.3) | collective-permute-done | bytes 524320 | tf_op jit(solution)/shard_map/ppermute | solution.py:60
  44.9 0.4 maximum_select_fusion
  45.3 1.0 convolution_bitcast_fusion.6
  46.3 1.0 convolution_bitcast_fusion.4
  47.3 1.0 fusion.2
  48.3 1.0 subtract_bitcast_fusion
  49.3 0.0 copy-start.3
  49.3 3.0 %collective-permute-start.4 = (f32[1,4,2,64,128]{4,3,1,2,0:T(8,128)S(1)}, f32[1,4,2,64,128]{4,3,1,2,0:T(8,128)S(1)}, u32[]{:S(2)}, u32[]{:S(2)}) collective-permute-start(f32[1,4,2,64,128]{4,3,1,2,0:T(8,128)S(1)} %maximum_bitcast_fusion), channel_id=1, source_target_pairs={{0,64},{16,80},{32,96},{48,112},{64,0},{80,16},{96,32},{112,48},{1... | collective-permute-start | bytes 786440 | tf_op jit(solution)/shard_map/ppermute | solution.py:60
  52.3 6.1 %collective-permute-done.4 = f32[1,4,2,64,128]{4,3,1,2,0:T(8,128)S(1)} collective-permute-done((f32[1,4,2,64,128]{4,3,1,2,0:T(8,128)S(1)}, f32[1,4,2,64,128]{4,3,1,2,0:T(8,128)S(1)}, u32[]{:S(2)}, u32[]{:S(2)}) %collective-permute-start.4) | collective-permute-done | bytes 262176 | tf_op jit(solution)/shard_map/ppermute | solution.py:60
  58.5 2.8 %collective-permute-start.5 = (f32[2,4,2,64,128]{4,3,1,2,0:T(8,128)S(1)}, f32[2,4,2,64,128]{4,3,1,2,0:T(8,128)S(1)}, u32[]{:S(2)}, u32[]{:S(2)}) collective-permute-start(f32[2,4,2,64,128]{4,3,1,2,0:T(8,128)S(1)} %maximum_select_fusion.5), channel_id=1, source_target_pairs={{0,32},{16,48},{32,0},{48,16},{64,96},{80,112},{96,64},{112,80},{1... | collective-permute-start | bytes 1572872 | tf_op jit(solution)/shard_map/ppermute | solution.py:60
  61.3 11.0 %collective-permute-done.5 = f32[2,4,2,64,128]{4,3,1,2,0:T(8,128)S(1)} collective-permute-done((f32[2,4,2,64,128]{4,3,1,2,0:T(8,128)S(1)}, f32[2,4,2,64,128]{4,3,1,2,0:T(8,128)S(1)}, u32[]{:S(2)}, u32[]{:S(2)}) %collective-permute-start.5) | collective-permute-done | bytes 524320 | tf_op jit(solution)/shard_map/ppermute | solution.py:60
  72.3 0.1 maximum_select_fusion.3
  72.4 1.5 collective-permute-start.6
  73.9 1.1 copy.24
  75.0 2.0 %copy.33 = f32[3,6,256,128]{2,3,1,0:T(8,128)S(1)} copy(f32[3,6,256,128]{3,2,1,0:T(8,128)} %e_ref.1) | data formatting | bytes 4718592 | tf_op args[3]
  77.1 0.0 copy-start.5
  77.1 3.1 %copy.34 = f32[3,6,256,128]{2,3,1,0:T(8,128)} copy(f32[3,6,256,128]{3,2,1,0:T(8,128)} %h_ref.1) | data formatting | bytes 4718592 | tf_op args[4]
  80.1 0.1 fusion.71
  80.3 0.1 fusion.64
  80.4 0.3 fusion.48
  80.8 14.5 %collective-permute-done.6 = f32[4,4,2,64,128]{4,3,1,2,0:T(8,128)} collective-permute-done((f32[4,4,2,64,128]{4,3,1,2,0:T(8,128)S(1)}, f32[4,4,2,64,128]{4,3,1,2,0:T(8,128)}, u32[]{:S(2)}, u32[]{:S(2)}) %collective-permute-start.6) | collective-permute-done | bytes 1048608 | tf_op jit(solution)/shard_map/ppermute | solution.py:60
  95.3 1.8 %maximum_select_fusion.1 = f32[8,4,2,64,128]{4,3,1,2,0:T(8,128)S(1)} fusion(f32[4,4,2,64,128]{4,3,1,2,0:T(8,128)} %collective-permute-done.6, f32[4,4,2,64,128]{4,3,1,2,0:T(8,128)S(1)} %maximum_select_fusion.3, pred[]{:T(512)S(6)} %eq.73), kind=kLoop, calls=%fused_computation.2 | loop fusion | flops 1572864 | bytes 4194305 | tf_op jit(solution)/shard_map/jit(_where)/select_n | solution.py:62
  97.1 1.0 convolution_bitcast_fusion.2
  98.1 1.0 convolution_bitcast_fusion
  99.2 0.0 copy-start.1
  99.2 1.0 fusion
  100.2 1.0 subtract_reduce_fusion
  101.3 0.6 copy-done.2
  101.9 1.3 collective-permute-start.7
  103.1 0.3 select_add_fusion
  103.4 1.2 copy.37.coef_ref
  104.6 2.6 %collective-permute-done.7 = f32[2,256,128]{1,2,0:T(8,128)} collective-permute-done((f32[2,256,128]{1,2,0:T(8,128)S(1)}, f32[2,256,128]{1,2,0:T(8,128)}, u32[]{:S(2)}, u32[]{:S(2)}) %collective-permute-start.7) | collective-permute-done | bytes 262176 | tf_op jit(solution)/shard_map/ppermute | solution.py:132
  107.2 1.0 fusion.74
  108.2 2.0 %maximum_bitcast_fusion.6 = (f32[44,4,4]{2,1,0:T(4,128)S(1)}, f32[44,4,4]{2,1,0:T(4,128)}, f32[44,4,4]{2,1,0:T(4,128)}, f32[44,4,4]{2,1,0:T(4,128)}) fusion(f32[2,256,128]{1,2,0:T(8,128)S(1)} %fusion.74, f32[6,256,128]{1,2,0:T(8,128)S(1)} %select_add_fusion, f32[18,256,128]{1,2,0:T(8,128)} %bitcast.114, f32[18,256,128]{1,2,0:T(8,128)S(1)} %bitcast.111), kind=kLoop, calls=%fused_computation.87 | loop fusion | flops 8448 | bytes 5778432 | tf_op jit(solution)/shard_map/transpose | solution.py:236
  110.2 0.7 pad_maximum_fusion
  110.9 9.3 %collective-permute-start.11 = (f32[44,4,4]{2,1,0:T(4,128)S(1)}, f32[44,4,4]{2,1,0:T(4,128)S(1)}, u32[]{:S(2)}, u32[]{:S(2)}) collective-permute-start(f32[44,4,4]{2,1,0:T(4,128)S(1)} %get-tuple-element.6), channel_id=1, source_target_pairs={{17,0},{18,1},{19,2},{20,3},{21,4},{22,5},{23,6},{24,7},{25,8},{26... | collective-permute-start | bytes 8456 | tf_op jit(solution)/shard_map/ppermute | solution.py:230
  120.1 0.8 maximum_bitcast_fusion.2
  120.9 0.0 collective-permute-start.10
  121.0 1.7 collective-permute-start.13
  122.7 6.3 %collective-permute-start.14 = (f32[44,4,4]{2,1,0:T(4,128)}, f32[44,4,4]{2,1,0:T(4,128)}, u32[]{:S(2)}, u32[]{:S(2)}) collective-permute-start(f32[44,4,4]{2,1,0:T(4,128)} %get-tuple-element.8), channel_id=1, source_target_pairs={{31,0},{16,1},{17,2},{18,3},{19,4},{20,5},{21,6},{22,7},{23,8},{24... | collective-permute-start | bytes 8456 | tf_op jit(solution)/shard_map/ppermute | solution.py:230
  128.9 2.6 %fusion.75 = (f32[44,4,128]{1,2,0:T(8,128)S(1)}, f32[44,4,128]{1,2,0:T(8,128)}) fusion(f32[44,256,128]{1,2,0:T(8,128)S(1)} %pad_maximum_fusion), kind=kLoop, calls=%fused_computation.150 | loop fusion | bytes 360448 | tf_op jit(solution)/shard_map/slice | solution.py:235
  131.6 0.8 copy.38.plane_ref
  132.4 2.7 %copy.35 = f32[44,4,128]{2,1,0:T(4,128)S(1)} copy(f32[44,4,128]{1,2,0:T(8,128)} %get-tuple-element.11) | data formatting | bytes 180224 | tf_op jit(solution)/shard_map/slice | solution.py:234
  135.1 0.9 copy.36
  135.9 4.0 %collective-permute-start.8 = (f32[44,4,128]{2,1,0:T(4,128)S(1)}, f32[44,4,128]{2,1,0:T(4,128)S(1)}, u32[]{:S(2)}, u32[]{:S(2)}) collective-permute-start(f32[44,4,128]{2,1,0:T(4,128)S(1)} %copy.35), channel_id=1, source_target_pairs={{16,0},{17,1},{18,2},{19,3},{20,4},{21,5},{22,6},{23,7},{24,8},{25... | collective-permute-start | bytes 270344 | tf_op jit(solution)/shard_map/ppermute | solution.py:230
  139.9 2.1 %maximum_maximum_fusion.yh_ref = f32[44,8,264]{2,1,0:T(8,128)} fusion(f32[44,4,4]{2,1,0:T(4,128)} %collective-permute-done.15, f32[44,4,4]{2,1,0:T(4,128)} %collective-permute-done.14, f32[44,4,256]{2,1,0:T(4,128)} %collective-permute-done.13, f32[44,4,4]{2,1,0:T(4,128)} %collective-permute-done.12, f32[44,4,4]{2,1,0:T(4,128)S(1)} %collective-permute-done.11, ...), kind=kLoop, calls=%fused_computation.22 | loop fusion | flops 464640 | bytes 743424 | tf_op jit(solution)/shard_map/concatenate | solution.py:245
  142.0 0.6 copy-done.4
  142.6 4.4 %collective-permute-done.9.xb_ref = f32[44,4,128]{2,1,0:T(4,128)} collective-permute-done((f32[44,4,128]{2,1,0:T(4,128)S(1)}, f32[44,4,128]{2,1,0:T(4,128)}, u32[]{:S(2)}, u32[]{:S(2)}) %collective-permute-start.9) | collective-permute-done | bytes 90144 | tf_op jit(solution)/shard_map/ppermute | solution.py:230
  147.0 28.9 %shard_map.86 = (f32[3,6,256,128]{3,2,1,0:T(8,128)}, f32[3,6,256,128]{3,2,1,0:T(8,128)}) custom-call(f32[3,6,256,128]{3,2,1,0:T(8,128)} %e_ref.1, f32[3,6,256,128]{3,2,1,0:T(8,128)} %h_ref.1, f32[6,256,128]{2,1,0:T(8,128)} %copy.37.coef_ref, f32[2,256,128]{2,1,0:T(8,128)} %copy.38.plane_ref, f32[44,4,128]{2,1,0:T(4,128)} %copy-done.4, ...), custom_call_target="tpu_custom_call" | custom-call | tf_op jit(solution)/shard_map/pallas_call | solution.py:268
  (26 shorter events, 0.2 us)
Async XLA Ops:
  0.6 42.0 %copy-start.6 = (s32[16]{0:T(128)S(1)}, s32[16]{0:T(128)}, u32[]{:S(2)}) copy-start(s32[16]{0:T(128)} %constant.196.clone) | copy-start | bytes 196
  1.6 10.5 %collective-permute-start = (f32[1,4,2,64,32]{3,4,0,1,2:T(8,128)S(1)}, f32[1,4,2,64,32]{3,4,0,1,2:T(8,128)S(1)}, u32[]{:S(2)}, u32[]{:S(2)}) collective-permute-start(f32[1,4,2,64,32]{3,4,0,1,2:T(8,128)S(1)} %bitcast.121), channel_id=1, source_target_pairs={{0,8},{1,9},{2,10},{3,11},{4,12},{5,13},{6,14},{7,15},{8,0},{9,1},... | collective-permute-start | bytes 196616 | tf_op jit(solution)/shard_map/ppermute | solution.py:60
  12.1 15.7 %collective-permute-start.1 = (f32[2,4,2,64,32]{3,4,0,1,2:T(8,128)S(1)}, f32[2,4,2,64,32]{3,4,0,1,2:T(8,128)S(1)}, u32[]{:S(2)}, u32[]{:S(2)}) collective-permute-start(f32[2,4,2,64,32]{3,4,0,1,2:T(8,128)S(1)} %maximum_select_fusion.6), channel_id=1, source_target_pairs={{0,4},{1,5},{2,6},{3,7},{4,0},{5,1},{6,2},{7,3},{8,12},{9,13},{10,... | collective-permute-start | bytes 393224 | tf_op jit(solution)/shard_map/ppermute | solution.py:60
  27.9 13.0 %collective-permute-start.2 = (f32[4,4,2,64,32]{3,4,0,1,2:T(8,128)S(1)}, f32[4,4,2,64,32]{3,4,0,1,2:T(8,128)S(1)}, u32[]{:S(2)}, u32[]{:S(2)}) collective-permute-start(f32[4,4,2,64,32]{3,4,0,1,2:T(8,128)S(1)} %maximum_select_fusion.4), channel_id=1, source_target_pairs={{0,2},{1,3},{2,0},{3,1},{4,6},{5,7},{6,4},{7,5},{8,10},{9,11},{10,... | collective-permute-start | bytes 786440 | tf_op jit(solution)/shard_map/ppermute | solution.py:60
  41.0 3.8 %collective-permute-start.3 = (f32[8,4,2,64,32]{3,4,0,1,2:T(8,128)S(1)}, f32[8,4,2,64,32]{3,4,0,1,2:T(8,128)S(1)}, u32[]{:S(2)}, u32[]{:S(2)}) collective-permute-start(f32[8,4,2,64,32]{3,4,0,1,2:T(8,128)S(1)} %maximum_select_fusion.2), channel_id=1, source_target_pairs={{0,1},{1,0},{2,3},{3,2},{4,5},{5,4},{6,7},{7,6},{8,9},{9,8},{10,11... | collective-permute-start | bytes 1572872 | tf_op jit(solution)/shard_map/ppermute | solution.py:60
  49.3 24.6 %copy-start.3 = (s32[6,256,128]{2,1,0:T(8,128)S(1)}, s32[6,256,128]{2,1,0:T(8,128)}, u32[]{:S(2)}) copy-start(s32[6,256,128]{2,1,0:T(8,128)} %param.9) | copy-start | bytes 2359300
  49.3 9.1 %collective-permute-start.4 = (f32[1,4,2,64,128]{4,3,1,2,0:T(8,128)S(1)}, f32[1,4,2,64,128]{4,3,1,2,0:T(8,128)S(1)}, u32[]{:S(2)}, u32[]{:S(2)}) collective-permute-start(f32[1,4,2,64,128]{4,3,1,2,0:T(8,128)S(1)} %maximum_bitcast_fusion), channel_id=1, source_target_pairs={{0,64},{16,80},{32,96},{48,112},{64,0},{80,16},{96,32},{112,48},{1... | collective-permute-start | bytes 786440 | tf_op jit(solution)/shard_map/ppermute | solution.py:60
  58.5 13.8 %collective-permute-start.5 = (f32[2,4,2,64,128]{4,3,1,2,0:T(8,128)S(1)}, f32[2,4,2,64,128]{4,3,1,2,0:T(8,128)S(1)}, u32[]{:S(2)}, u32[]{:S(2)}) collective-permute-start(f32[2,4,2,64,128]{4,3,1,2,0:T(8,128)S(1)} %maximum_select_fusion.5), channel_id=1, source_target_pairs={{0,32},{16,48},{32,0},{48,16},{64,96},{80,112},{96,64},{112,80},{1... | collective-permute-start | bytes 1572872 | tf_op jit(solution)/shard_map/ppermute | solution.py:60
  72.4 22.9 %collective-permute-start.6 = (f32[4,4,2,64,128]{4,3,1,2,0:T(8,128)S(1)}, f32[4,4,2,64,128]{4,3,1,2,0:T(8,128)}, u32[]{:S(2)}, u32[]{:S(2)}) collective-permute-start(f32[4,4,2,64,128]{4,3,1,2,0:T(8,128)S(1)} %maximum_select_fusion.3), channel_id=1, source_target_pairs={{0,16},{16,0},{32,48},{48,32},{64,80},{80,64},{96,112},{112,96},{1... | collective-permute-start | bytes 3145736 | tf_op jit(solution)/shard_map/ppermute | solution.py:60
  77.1 3.2 %copy-start.5 = (s32[8]{0:T(128)S(1)}, s32[8]{0:T(128)}, u32[]{:S(2)}) copy-start(s32[8]{0:T(128)} %constant.197.clone) | copy-start | bytes 100
  99.2 4.0 %copy-start.1 = (s32[6,256,128]{1,2,0:T(8,128)S(1)}, s32[6,256,128]{1,2,0:T(8,128)}, u32[]{:S(2)}) copy-start(s32[6,256,128]{1,2,0:T(8,128)} %copy.24) | copy-start | bytes 2359300
  101.2 0.6 copy-start.2
  101.9 5.3 %collective-permute-start.7 = (f32[2,256,128]{1,2,0:T(8,128)S(1)}, f32[2,256,128]{1,2,0:T(8,128)}, u32[]{:S(2)}, u32[]{:S(2)}) collective-permute-start(f32[2,256,128]{1,2,0:T(8,128)S(1)} %pad_maximum_fusion.1), channel_id=1, source_target_pairs={{0,128},{128,0},{1,129},{129,1},{2,130},{130,2},{3,131},{131,3},{4... | collective-permute-start | bytes 786440 | tf_op jit(solution)/shard_map/ppermute | solution.py:132
  108.2 2.0 %copy-start = (f32[3,6,256,128]{2,3,1,0:T(8,128)S(1)}, f32[3,6,256,128]{2,3,1,0:T(8,128)}, u32[]{:S(2)}) copy-start(f32[3,6,256,128]{2,3,1,0:T(8,128)} %copy.34) | copy-start | bytes 7077892
  110.9 18.1 %collective-permute-start.11 = (f32[44,4,4]{2,1,0:T(4,128)S(1)}, f32[44,4,4]{2,1,0:T(4,128)S(1)}, u32[]{:S(2)}, u32[]{:S(2)}) collective-permute-start(f32[44,4,4]{2,1,0:T(4,128)S(1)} %get-tuple-element.6), channel_id=1, source_target_pairs={{17,0},{18,1},{19,2},{20,3},{21,4},{22,5},{23,6},{24,7},{25,8},{26... | collective-permute-start | bytes 8456 | tf_op jit(solution)/shard_map/ppermute | solution.py:230
  120.9 18.9 %collective-permute-start.10 = (f32[44,4,256]{2,1,0:T(4,128)}, f32[44,4,256]{2,1,0:T(4,128)S(1)}, u32[]{:S(2)}, u32[]{:S(2)}) collective-permute-start(f32[44,4,256]{2,1,0:T(4,128)} %get-tuple-element.4), channel_id=1, source_target_pairs={{1,0},{2,1},{3,2},{4,3},{5,4},{6,5},{7,6},{8,7},{9,8},{10,9},{11,1... | collective-permute-start | bytes 540680 | tf_op jit(solution)/shard_map/ppermute | solution.py:230
  121.0 18.9 %collective-permute-start.13 = (f32[44,4,256]{2,1,0:T(4,128)}, f32[44,4,256]{2,1,0:T(4,128)}, u32[]{:S(2)}, u32[]{:S(2)}) collective-permute-start(f32[44,4,256]{2,1,0:T(4,128)} %get-tuple-element.5), channel_id=1, source_target_pairs={{15,0},{0,1},{1,2},{2,3},{3,4},{4,5},{5,6},{6,7},{7,8},{8,9},{9,10... | collective-permute-start | bytes 540680 | tf_op jit(solution)/shard_map/ppermute | solution.py:230
  122.7 13.2 %collective-permute-start.12 = (f32[44,4,4]{2,1,0:T(4,128)}, f32[44,4,4]{2,1,0:T(4,128)}, u32[]{:S(2)}, u32[]{:S(2)}) collective-permute-start(f32[44,4,4]{2,1,0:T(4,128)} %get-tuple-element.9), channel_id=1, source_target_pairs={{113,0},{114,1},{115,2},{116,3},{117,4},{118,5},{119,6},{120,7},{1... | collective-permute-start | bytes 8456 | tf_op jit(solution)/shard_map/ppermute | solution.py:230
  122.7 17.2 %collective-permute-start.14 = (f32[44,4,4]{2,1,0:T(4,128)}, f32[44,4,4]{2,1,0:T(4,128)}, u32[]{:S(2)}, u32[]{:S(2)}) collective-permute-start(f32[44,4,4]{2,1,0:T(4,128)} %get-tuple-element.8), channel_id=1, source_target_pairs={{31,0},{16,1},{17,2},{18,3},{19,4},{20,5},{21,6},{22,7},{23,8},{24... | collective-permute-start | bytes 8456 | tf_op jit(solution)/shard_map/ppermute | solution.py:230
  128.9 10.9 %collective-permute-start.15 = (f32[44,4,4]{2,1,0:T(4,128)}, f32[44,4,4]{2,1,0:T(4,128)}, u32[]{:S(2)}, u32[]{:S(2)}) collective-permute-start(f32[44,4,4]{2,1,0:T(4,128)} %get-tuple-element.7), channel_id=1, source_target_pairs={{127,0},{112,1},{113,2},{114,3},{115,4},{116,5},{117,6},{118,7},{1... | collective-permute-start | bytes 8456 | tf_op jit(solution)/shard_map/ppermute | solution.py:230
  135.9 6.1 %collective-permute-start.8 = (f32[44,4,128]{2,1,0:T(4,128)S(1)}, f32[44,4,128]{2,1,0:T(4,128)S(1)}, u32[]{:S(2)}, u32[]{:S(2)}) collective-permute-start(f32[44,4,128]{2,1,0:T(4,128)S(1)} %copy.35), channel_id=1, source_target_pairs={{16,0},{17,1},{18,2},{19,3},{20,4},{21,5},{22,6},{23,7},{24,8},{25... | collective-permute-start | bytes 270344 | tf_op jit(solution)/shard_map/ppermute | solution.py:230
  139.9 7.1 %collective-permute-start.9 = (f32[44,4,128]{2,1,0:T(4,128)S(1)}, f32[44,4,128]{2,1,0:T(4,128)}, u32[]{:S(2)}, u32[]{:S(2)}) collective-permute-start(f32[44,4,128]{2,1,0:T(4,128)S(1)} %copy.36), channel_id=1, source_target_pairs={{112,0},{113,1},{114,2},{115,3},{116,4},{117,5},{118,6},{119,7},{1... | collective-permute-start | bytes 270344 | tf_op jit(solution)/shard_map/ppermute | solution.py:230
  142.0 0.6 copy-start.4
where the time goes:
time: 179 us; the launch traced here: 176 us
  waiting for transfers between devices  66 us (37%)
  starting transfers between devices  44.2 us (25%)
  Pallas kernels  28.9 us (16%)
  local copies, waits for them, and re-layouts  17.3 us (10%)
  other arithmetic  10.5 us (6%)
  matrix products  8.02 us (4%)
    ppermute x7, waiting for transfers between devices, butterfly_gather(): other = lax.ppermute(held, axis, [(i, i ^ d) for i in range(n)])  59 us
    pallas_call x1, Pallas kernels, per_device(): pl.pallas_call(yee_kernel, out_shape=(out, out), in_specs=[spec] * 7, out...  28.9 us
    ppermute x7, starting transfers between devices, butterfly_gather(): other = lax.ppermute(held, axis, [(i, i ^ d) for i in range(n)])  21.7 us
    ppermute x8, starting transfers between devices, from_offset(): return lax.ppermute(block, ('tx', 'ty'), pairs)  21.2 us
    unnamed x18, local copies, waits for them, and re-layouts  8.43 us
    ppermute x8, waiting for transfers between devices, from_offset(): return lax.ppermute(block, ('tx', 'ty'), pairs)  4.38 us
  transfers between devices with their start and end apart: 16, of which 9 were waited for; matrix products, arithmetic and copies ran while one was open for 11% of the time, Pallas kernels for 0%

commit v1 on v0

--- a/solution.py
+++ b/solution.py
@@ -17,12 +17,6 @@
 PREC = lax.Precision.HIGH
 
 
-def passed_along(block, axis, distance):
-    devices = range(lax.axis_size(axis))
-    route = [((i - distance) % len(devices), i) for i in devices]
-    return lax.ppermute(block, axis, route)
-
-
 def phase_tables(freqs, positions, length):
     product = jnp.mod(freqs[:, None] * positions[None, :], length)
     angle = product.astype(jnp.float32) * (2.0 * math.pi / length)
@@ -36,53 +30,82 @@
     return total
 
 
-def ahead(field, rim, axis):
-    following = lax.slice_in_dim(field, 1, field.shape[axis], axis=axis)
-    return jnp.concatenate([following, rim], axis) - field
-
-
-def behind(field, rim, axis):
-    earlier = lax.slice_in_dim(field, 0, field.shape[axis] - 1, axis=axis)
-    return field - jnp.concatenate([rim, earlier], axis)
-
-
-def neighbour_rims(row_x, col_y, offset):
-    got_x = passed_along(row_x, "tx", offset)
-    got_y = passed_along(col_y, "ty", offset)
-    return (got_x, got_y)
-
-
-def butterfly_gather(block, axis, order):
-    me = lax.axis_index(axis)
+MESH = pl.DeviceIdType.MESH
+VMEM_SPEC = pl.BlockSpec(memory_space=pltpu.MemorySpace.VMEM)
+
+
+def gather_along(block, axis, collective):
     n = lax.axis_size(axis)
-    held = block[None]
-    for d in order:
-        other = lax.ppermute(held, axis, [(i, i ^ d) for i in range(n)])
-        low = (me // d) % 2 == 0
-        held = jnp.where(low, jnp.concatenate([held, other], 0), jnp.concatenate([other, held], 0))
-    return held
-
-
-def gather_order(n):
-    order = []
-    d = n // 2
-    while d >= 1:
-        order.append(d)
-        d //= 2
-    return order
-
-
-def chunk_starts(order, size):
-    starts = []
-    for q in range(2 ** len(order)):
-        c = sum(order[t] for t in range(len(order)) if (q >> t) & 1)
-        starts.append(c * size)
-    return jnp.array(starts, dtype=jnp.int32)
-
-
-def chunk_tables(order, size, total, positions, length):
-    c1, s1 = phase_tables(chunk_starts(order, size), positions, length)
-    c2, s2 = phase_tables(jnp.arange(size, dtype=jnp.int32) - total // 2, positions, length)
+
+    def kernel(x_ref, o_ref, send, recv, local):
+        me = lax.axis_index(axis)
+        barrier = pltpu.get_barrier_semaphore()
+        for k in range(1, n):
+            pl.semaphore_signal(barrier, 1, device_id={axis: lax.rem(me + k, n)}, device_id_type=MESH)
+        pl.semaphore_wait(barrier, n - 1)
+        own = pltpu.make_async_copy(x_ref, o_ref.at[me], local.at[0])
+        own.start()
+        copies = []
+        for k in range(1, n):
+            copy = pltpu.make_async_remote_copy(
+                src_ref=x_ref,
+                dst_ref=o_ref.at[me],
+                send_sem=send.at[k - 1],
+                recv_sem=recv.at[k - 1],
+                device_id={axis: lax.rem(me + k, n)},
+                device_id_type=MESH,
+            )
+            copy.start()
+            copies.append(copy)
+        own.wait()
+        for copy in copies:
+            copy.wait()
+
+    return pl.pallas_call(
+        kernel,
+        out_shape=jax.ShapeDtypeStruct((n,) + block.shape, block.dtype),
+        in_specs=[VMEM_SPEC],
+        out_specs=VMEM_SPEC,
+        scratch_shapes=[
+            pltpu.SemaphoreType.DMA((n - 1,)),
+            pltpu.SemaphoreType.DMA((n - 1,)),
+            pltpu.SemaphoreType.DMA((1,)),
+        ],
+        compiler_params=pltpu.CompilerParams(collective_id=collective, has_side_effects=True),
+    )(block)
+
+
+def summed_over_pair(block, axis, collective):
+    def kernel(x_ref, o_ref, got, send, recv):
+        other = 1 - lax.axis_index(axis)
+        barrier = pltpu.get_barrier_semaphore()
+        pl.semaphore_signal(barrier, 1, device_id={axis: other}, device_id_type=MESH)
+        pl.semaphore_wait(barrier, 1)
+        copy = pltpu.make_async_remote_copy(
+            src_ref=x_ref, dst_ref=got, send_sem=send.at[0], recv_sem=recv.at[0],
+            device_id={axis: other}, device_id_type=MESH,
+        )
+        copy.start()
+        copy.wait()
+        o_ref[...] = x_ref[...] + got[...]
+
+    return pl.pallas_call(
+        kernel,
+        out_shape=jax.ShapeDtypeStruct(block.shape, block.dtype),
+        in_specs=[VMEM_SPEC],
+        out_specs=VMEM_SPEC,
+        scratch_shapes=[
+            pltpu.VMEM(block.shape, block.dtype),
+            pltpu.SemaphoreType.DMA((1,)),
+            pltpu.SemaphoreType.DMA((1,)),
+        ],
+        compiler_params=pltpu.CompilerParams(collective_id=collective, has_side_effects=True),
+    )(block)
+
+
+def chunk_tables(size, count, positions, length):
+    c1, s1 = phase_tables(jnp.arange(count, dtype=jnp.int32) * size, positions, length)
+    c2, s2 = phase_tables(jnp.arange(size, dtype=jnp.int32) - size * count // 2, positions, length)
     cos_t = c1[:, None, :] * c2[None, :, :] - s1[:, None, :] * s2[None, :, :]
     sin_t = s1[:, None, :] * c2[None, :, :] + c1[:, None, :] * s2[None, :, :]
     return cos_t, sin_t
@@ -94,12 +117,11 @@
     n_ty = lax.axis_size("ty")
     full_x = cells_x * n_tx
     full_y = cells_y * n_ty
-    order_y = gather_order(n_ty)
-    amp = butterfly_gather(orders, "ty", order_y)
+    amp = gather_along(orders, "ty", 0)
     a_re = amp[:, :, 0]
     a_im = amp[:, :, 1]
     y_pos = lax.axis_index("ty") * cells_y + jnp.arange(cells_y, dtype=jnp.int32)
-    by_c, by_s = chunk_tables(order_y, cols_ky, cols_ky * n_ty, y_pos, full_y)
+    by_c, by_s = chunk_tables(cols_ky, n_ty, y_pos, full_y)
     sy_c, sy_s = phase_tables(offsets[:, 1], y_pos, full_y)
     m_re = jnp.einsum("cpkj,cjy->pky", a_re, by_c, precision=PREC) - jnp.einsum(
         "cpkj,cjy->pky", a_im, by_s, precision=PREC
@@ -110,12 +132,11 @@
     sy_c = sy_c[:, None, :]
     sy_s = sy_s[:, None, :]
     inner = jnp.stack([m_re * sy_c - m_im * sy_s, m_re * sy_s + m_im * sy_c], 1)
-    order_x = gather_order(n_tx)
-    inner = butterfly_gather(inner, "tx", order_x)
+    inner = gather_along(inner, "tx", 1)
     i_re = inner[:, :, 0]
     i_im = inner[:, :, 1]
     x_pos = lax.axis_index("tx") * cells_x + jnp.arange(cells_x, dtype=jnp.int32)
-    bx_c, bx_s = chunk_tables(order_x, rows_kx, rows_kx * n_tx, x_pos, full_x)
+    bx_c, bx_s = chunk_tables(rows_kx, n_tx, x_pos, full_x)
     sx_c, sx_s = phase_tables(offsets[:, 0], x_pos, full_x)
     q_re = jnp.einsum("ckx,cpky->pxy", bx_c, i_re, precision=PREC) - jnp.einsum(
         "ckx,cpky->pxy", bx_s, i_im, precision=PREC
@@ -128,9 +149,7 @@
     plane = jnp.stack(
         [jnp.sum(q_re * sx_c - q_im * sx_s, 0), jnp.sum(q_re * sx_s + q_im * sx_c, 0)]
     )
-    n_src = lax.axis_size("src")
-    other = lax.ppermute(plane, "src", [(i, (i + 1) % n_src) for i in range(n_src)])
-    return plane + other
+    return summed_over_pair(plane, "src", 2)
 
 
 def yee_kernel(e_ref, h_ref, coef_ref, plane_ref, xa_ref, xb_ref, yh_ref, eo_ref, ho_ref, ext, cp, tmp):
@@ -217,29 +236,61 @@
             ho_ref[comp, z] = ext[(3 + comp) * slab + z + 1, 0:cells_x, 0:cells_y]
 
 
+OFFSETS = ((1, 0), (-1, 0), (0, 1), (0, -1), (1, 1), (1, -1), (-1, 1), (-1, -1))
+
+
 def exchange_halos(parts, depth):
-    n_tx = lax.axis_size("tx")
-    n_ty = lax.axis_size("ty")
-
-    def from_offset(block, dx, dy):
-        pairs = []
-        for i in range(n_tx):
-            for j in range(n_ty):
-                src_dev = ((i + dx) % n_tx) * n_ty + (j + dy) % n_ty
-                pairs.append((src_dev, i * n_ty + j))
-        return lax.ppermute(block, ("tx", "ty"), pairs)
-
     head = slice(0, depth)
     tail = slice(-depth, None)
-    xa = from_offset(parts[:, head, :], 1, 0)
-    xb = from_offset(parts[:, tail, :], -1, 0)
     t = lambda b: jnp.swapaxes(b, 1, 2)
-    ya = from_offset(t(parts[:, :, head]), 0, 1)
-    yb = from_offset(t(parts[:, :, tail]), 0, -1)
-    aa = from_offset(t(parts[:, head, head]), 1, 1)
-    ab = from_offset(t(parts[:, head, tail]), 1, -1)
-    ba = from_offset(t(parts[:, tail, head]), -1, 1)
-    bb = from_offset(t(parts[:, tail, tail]), -1, -1)
+    outgoing = [
+        parts[:, head, :],
+        parts[:, tail, :],
+        t(parts[:, :, head]),
+        t(parts[:, :, tail]),
+        t(parts[:, head, head]),
+        t(parts[:, head, tail]),
+        t(parts[:, tail, head]),
+        t(parts[:, tail, tail]),
+    ]
+    count = len(OFFSETS)
+
+    def kernel(*refs):
+        ins = refs[:count]
+        outs = refs[count:2 * count]
+        send, recv = refs[2 * count:]
+        n_tx = lax.axis_size("tx")
+        n_ty = lax.axis_size("ty")
+        me_x = lax.axis_index("tx")
+        me_y = lax.axis_index("ty")
+        targets = [
+            {"tx": lax.rem(me_x - dx + n_tx, n_tx), "ty": lax.rem(me_y - dy + n_ty, n_ty)}
+            for dx, dy in OFFSETS
+        ]
+        barrier = pltpu.get_barrier_semaphore()
+        for target in targets:
+            pl.semaphore_signal(barrier, 1, device_id=target, device_id_type=MESH)
+        pl.semaphore_wait(barrier, count)
+        copies = []
+        for k in range(count):
+            copy = pltpu.make_async_remote_copy(
+                src_ref=ins[k], dst_ref=outs[k], send_sem=send.at[k], recv_sem=recv.at[k],
+                device_id=targets[k], device_id_type=MESH,
+            )
+            copy.start()
+            copies.append(copy)
+        for copy in copies:
+            copy.wait()
+
+    got = pl.pallas_call(
+        kernel,
+        out_shape=tuple(jax.ShapeDtypeStruct(p.shape, p.dtype) for p in outgoing),
+        in_specs=[VMEM_SPEC] * count,
+        out_specs=tuple([VMEM_SPEC] * count),
+        scratch_shapes=[pltpu.SemaphoreType.DMA((count,)), pltpu.SemaphoreType.DMA((count,))],
+        compiler_params=pltpu.CompilerParams(collective_id=3, has_side_effects=True),
+    )(*outgoing)
+    xa, xb, ya, yb, aa, ab, ba, bb = got
     y_ahead = jnp.concatenate([ya, aa, ba], 2)
     y_behind = jnp.concatenate([yb, ab, bb], 2)
     return xa, xb, jnp.concatenate([y_ahead, y_behind], 1)

time: 179 us -> 242 us (1.35); the launches traced: 176 us -> 242 us
  Pallas kernels: 28.9 us -> 198 us
  waiting for transfers between devices: 66 us -> 0 us
  starting transfers between devices: 44.2 us -> 0 us
  matrix products: 8.02 us -> 15.7 us
    pallas_call x0 -> x4, Pallas kernels: none -> 169 us  [the longest x2 144 us: gather_along(): pl.pallas_call(kernel, out_shape=jax.ShapeDtypeStruct((n,) + block.shape,...]
    ppermute x16 -> x0, waiting for transfers between devices: 66 us -> none  [the longest x7 59 us: butterfly_gather(): other = lax.ppermute(held, axis, [(i, i ^ d) for i in range(n)])]
    ppermute x16 -> x0, starting transfers between devices: 44.2 us -> none  [the longest x7 21.7 us: butterfly_gather(): other = lax.ppermute(held, axis, [(i, i ^ d) for i in range(n)])]
    select_n x7 -> x0, other arithmetic: 2.62 us -> none  [butterfly_gather(): jnp.where(low, jnp.concatenate([held, other], 0), jnp.concatenate([other,...]
    unnamed x18 -> x15, local copies, waits for them, and re-layouts: 8.43 us -> 7.75 us
  transfers between devices with their start and end apart: 16 -> 0, of which waited for: 9 -> 0; matrix products, arithmetic and copies ran while one was open for 11% -> 0% of each run, Pallas kernels for 0% -> 0%
where the time goes in v1:
time: 242 us
  Pallas kernels  198 us (82%)
  local copies, waits for them, and re-layouts  17.5 us (7%)
  matrix products  15.7 us (6%)
  other arithmetic  10.3 us (4%)
    pallas_call x2, Pallas kernels, gather_along(): pl.pallas_call(kernel, out_shape=jax.ShapeDtypeStruct((n,) + block.shape,...  144 us
    pallas_call x1, Pallas kernels, per_device(): pl.pallas_call(yee_kernel, out_shape=(out, out), in_specs=[spec] * 7, out...  28.9 us
    pallas_call x1, Pallas kernels, exchange_halos(): pl.pallas_call(kernel, out_shape=tuple((jax.ShapeDtypeStruct(p.shape, p.d...  15.8 us
    pallas_call x1, Pallas kernels, summed_over_pair(): pl.pallas_call(kernel, out_shape=jax.ShapeDtypeStruct(block.shape, block....  9.2 us
    unnamed x15, local copies, waits for them, and re-layouts  7.75 us
    slice x2, local copies, waits for them, and re-layouts, exchange_halos(): parts[:, tail, :]  5.96 us

profile of v1, /device:TPU:1, one launch (start us, length us, event | category | flops | bytes accessed | tf_op | source)
XLA Modules:
  0.0 241.9 jit_solution(14551509078501133055)
XLA Ops:
  0.7 0.8 slice_bitcast_fusion
  1.5 0.1 fusion.115
  1.6 0.7 fusion.113
  2.3 0.1 fusion.106
  2.4 0.1 fusion.108
  2.6 0.2 fusion.101
  2.7 0.3 fusion.90
  3.1 1.7 copy.23.x_ref
  4.8 1.4 select_add_fusion.coef_ref
  6.2 0.0 copy-start.3
  6.2 0.9 copy-done.3
  7.1 0.3 copy.37
  7.4 2.1 copy.35
  9.4 3.1 %copy.36 = f32[3,6,256,128]{2,3,1,0:T(8,128)} copy(f32[3,6,256,128]{3,2,1,0:T(8,128)} %h_ref.1) | data formatting | bytes 4718592 | tf_op args[4]
  12.5 103.2 %shard_map.68 = f32[16,4,2,64,32]{4,3,2,1,0:T(8,128)} custom-call(f32[4,2,64,32]{3,2,1,0:T(8,128)} %copy.23.x_ref), custom_call_target="tpu_custom_call" | custom-call | tf_op jit(solution)/shard_map/pallas_call | solution.py:64
  115.7 0.0 copy-start
  115.7 3.2 %fusion.17 = f32[128,4,64]{0,2,1:T(8,128)S(1)} fusion(f32[16,4,2,64,32]{4,3,2,1,0:T(8,128)} %shard_map.68, f32[32,128]{1,0:T(8,128)S(1)} %get-tuple-element.43, f32[16,128]{1,0:T(8,128)S(1)} %get-tuple-element.41, f32[32,128]{1,0:T(8,128)S(1)} %get-tuple-element.42, f32[16,128]{1,0:T(8,128)S(1)} %get-tuple-element.40), kind=kOutput, calls=%fused_computation.20 | convolution fusion | flops 100859904 | bytes 2277376 | tf_op jit(solution)/shard_map/cpkj,cjy->pky/dot_general | solution.py:126
  118.9 3.0 %fusion.29 = f32[4,64,128]{2,1,0:T(8,128)S(1)} fusion(f32[128,4,64]{0,2,1:T(8,128)S(1)} %fusion.17, f32[16,4,2,64,32]{4,3,2,1,0:T(8,128)} %shard_map.68, f32[32,128]{1,0:T(8,128)S(1)} %get-tuple-element.43, f32[16,128]{1,0:T(8,128)S(1)} %get-tuple-element.41, f32[32,128]{1,0:T(8,128)S(1)} %get-tuple-element.42, f32[16,128]{1,0:T(8,128)S(1)} %get-tuple-element.40), kind=kOutput, calls=%fused_computation.24 | convolution fusion | flops 100892672 | bytes 2408448 | tf_op jit(solution)/shard_map/cpkj,cjy->pky/dot_general | solution.py:126
  121.9 0.0 copy-done
  121.9 1.4 fusion.14
  123.3 1.4 subtract_bitcast_fusion
  124.7 0.7 pad_maximum_fusion.1.x_ref
  125.4 40.5 %shard_map.69 = f32[8,4,2,64,128]{4,3,2,1,0:T(8,128)} custom-call(f32[4,2,64,128]{3,2,1,0:T(8,128)} %pad_maximum_fusion.1.x_ref), custom_call_target="tpu_custom_call" | custom-call | tf_op jit(solution)/shard_map/pallas_call | solution.py:64
  165.9 0.0 copy-start.2
  165.9 2.4 convolution_bitcast_fusion
  168.3 0.0 copy-start.4
  168.3 0.0 copy-start.5
  168.3 2.2 convolution_bitcast_fusion.2
  170.6 0.0 copy-done.2
  170.6 1.0 fusion.12
  171.6 0.0 copy-done.4
  171.6 0.0 copy-done.5
  171.6 1.0 subtract_reduce_fusion
  172.6 0.1 copy.33
  172.7 0.1 copy.34
  172.8 0.7 pad_maximum_fusion.2.x_ref
  173.6 9.2 %shard_map.70.plane_ref = f32[2,256,128]{2,1,0:T(8,128)} custom-call(f32[2,256,128]{2,1,0:T(8,128)} %pad_maximum_fusion.2.x_ref), custom_call_target="tpu_custom_call" | custom-call | tf_op jit(solution)/shard_map/pallas_call | solution.py:92
  182.8 1.1 copy.38
  183.9 0.0 copy-start.1
  183.9 2.0 maximum_bitcast_fusion.2
  185.9 0.0 copy-done.1
  185.9 0.8 maximum_bitcast_fusion
  186.7 0.9 pad_maximum_fusion
  187.6 2.7 %fusion.116 = (f32[44,4,128]{1,2,0:T(8,128)}, f32[44,4,128]{1,2,0:T(8,128)S(1)}) fusion(f32[44,256,128]{1,2,0:T(8,128)S(1)} %pad_maximum_fusion), kind=kLoop, calls=%fused_computation.161 | loop fusion | bytes 360448 | tf_op jit(solution)/shard_map/slice | solution.py:248
  190.2 3.3 %copy.40.refs_1_ = f32[44,4,128]{2,1,0:T(4,128)} copy(f32[44,4,128]{1,2,0:T(8,128)} %get-tuple-element.26) | data formatting | bytes 180224 | tf_op jit(solution)/shard_map/slice | solution.py:248
  193.5 1.5 copy.39.refs_0_
  195.0 15.8 %shard_map.71 = (f32[44,4,128]{2,1,0:T(4,128)}, f32[44,4,128]{2,1,0:T(4,128)}, f32[44,4,256]{2,1,0:T(4,128)}, f32[44,4,256]{2,1,0:T(4,128)}, f32[44,4,4]{2,1,0:T...) custom-call(f32[44,4,128]{2,1,0:T(4,128)} %copy.39.refs_0_, f32[44,4,128]{2,1,0:T(4,128)} %copy.40.refs_1_, ...), custom_call_target="tpu_custom_call" | custom-call | tf_op jit(solution)/shard_map/pallas_call | solution.py:285
  210.8 2.2 maximum_maximum_fusion.yh_ref
  213.0 28.9 %shard_map.72 = (f32[3,6,256,128]{3,2,1,0:T(8,128)}, f32[3,6,256,128]{3,2,1,0:T(8,128)}) custom-call(f32[3,6,256,128]{3,2,1,0:T(8,128)} %e_ref.1, f32[3,6,256,128]{3,2,1,0:T(8,128)} %h_ref.1, f32[6,256,128]{2,1,0:T(8,128)} %copy-done.3, f32[2,256,128]{2,1,0:T(8,128)} %shard_map.70.plane_ref, f32[44,4,128]{2,1,0:T(4,128)} %get-tuple-element.10.xa_ref, ...), custom_call_target="tpu_custom_call" | custom-call | tf_op jit(solution)/shard_map/pallas_call | solution.py:319
  (6 shorter events, 0.0 us)
Async XLA Ops:
  6.2 0.9 copy-start.3
  115.7 6.2 %copy-start = (f32[16,4,2,64,32]{4,3,2,1,0:T(8,128)S(1)}, f32[16,4,2,64,32]{4,3,2,1,0:T(8,128)}, u32[]{:S(2)}) copy-start(f32[16,4,2,64,32]{4,3,2,1,0:T(8,128)} %shard_map.68) | copy-start | bytes 3145732
  165.9 4.7 %copy-start.2 = (f32[8,4,2,64,128]{4,3,2,1,0:T(8,128)S(1)}, f32[8,4,2,64,128]{4,3,2,1,0:T(8,128)}, u32[]{:S(2)}) copy-start(f32[8,4,2,64,128]{4,3,2,1,0:T(8,128)} %shard_map.69) | copy-start | bytes 6291460
  168.3 3.3 %copy-start.4 = (f32[4,256]{1,0:T(4,128)S(1)}, f32[4,256]{1,0:T(4,128)}, u32[]{:S(2)}) copy-start(f32[4,256]{1,0:T(4,128)} %get-tuple-element.30) | copy-start | bytes 12292
  168.3 3.3 %copy-start.5 = (f32[4,256]{1,0:T(4,128)S(1)}, f32[4,256]{1,0:T(4,128)}, u32[]{:S(2)}) copy-start(f32[4,256]{1,0:T(4,128)} %get-tuple-element.31) | copy-start | bytes 12292
  183.9 2.0 copy-start.1

commit v2 on v1

--- a/solution.py
+++ b/solution.py
@@ -15,6 +15,7 @@
 OMEGA = 0.7
 PERMITTIVITY = (1.0, 2.6, 11.9, 2.1)
 PREC = lax.Precision.HIGH
+SHIFT = 8
 
 
 def phase_tables(freqs, positions, length):
@@ -34,14 +35,26 @@
 VMEM_SPEC = pl.BlockSpec(memory_space=pltpu.MemorySpace.VMEM)
 
 
-def gather_along(block, axis, collective):
-    n = lax.axis_size(axis)
+def gather_along(block, axes, collective):
+    sizes = [lax.axis_size(a) for a in axes]
+    n = 1
+    for s in sizes:
+        n *= s
+
+    def coords(linear):
+        out = {}
+        for a, s in reversed(list(zip(axes, sizes))):
+            out[a] = lax.rem(linear, s)
+            linear = linear // s
+        return out
 
     def kernel(x_ref, o_ref, send, recv, local):
-        me = lax.axis_index(axis)
+        me = 0
+        for a, s in zip(axes, sizes):
+            me = me * s + lax.axis_index(a)
         barrier = pltpu.get_barrier_semaphore()
         for k in range(1, n):
-            pl.semaphore_signal(barrier, 1, device_id={axis: lax.rem(me + k, n)}, device_id_type=MESH)
+            pl.semaphore_signal(barrier, 1, device_id=coords(lax.rem(me + k, n)), device_id_type=MESH)
         pl.semaphore_wait(barrier, n - 1)
         own = pltpu.make_async_copy(x_ref, o_ref.at[me], local.at[0])
         own.start()
@@ -52,7 +65,7 @@
                 dst_ref=o_ref.at[me],
                 send_sem=send.at[k - 1],
                 recv_sem=recv.at[k - 1],
-                device_id={axis: lax.rem(me + k, n)},
+                device_id=coords(lax.rem(me + k, n)),
                 device_id_type=MESH,
             )
             copy.start()
@@ -75,81 +88,65 @@
     )(block)
 
 
-def summed_over_pair(block, axis, collective):
-    def kernel(x_ref, o_ref, got, send, recv):
-        other = 1 - lax.axis_index(axis)
-        barrier = pltpu.get_barrier_semaphore()
-        pl.semaphore_signal(barrier, 1, device_id={axis: other}, device_id_type=MESH)
-        pl.semaphore_wait(barrier, 1)
-        copy = pltpu.make_async_remote_copy(
-            src_ref=x_ref, dst_ref=got, send_sem=send.at[0], recv_sem=recv.at[0],
-            device_id={axis: other}, device_id_type=MESH,
-        )
-        copy.start()
-        copy.wait()
-        o_ref[...] = x_ref[...] + got[...]
-
-    return pl.pallas_call(
-        kernel,
-        out_shape=jax.ShapeDtypeStruct(block.shape, block.dtype),
-        in_specs=[VMEM_SPEC],
-        out_specs=VMEM_SPEC,
-        scratch_shapes=[
-            pltpu.VMEM(block.shape, block.dtype),
-            pltpu.SemaphoreType.DMA((1,)),
-            pltpu.SemaphoreType.DMA((1,)),
-        ],
-        compiler_params=pltpu.CompilerParams(collective_id=collective, has_side_effects=True),
-    )(block)
-
-
-def chunk_tables(size, count, positions, length):
-    c1, s1 = phase_tables(jnp.arange(count, dtype=jnp.int32) * size, positions, length)
-    c2, s2 = phase_tables(jnp.arange(size, dtype=jnp.int32) - size * count // 2, positions, length)
+def chunk_tables(step, span, count, base, positions, length):
+    c1, s1 = phase_tables(jnp.arange(count, dtype=jnp.int32) * step, positions, length)
+    c2, s2 = phase_tables(jnp.arange(span, dtype=jnp.int32) - base, positions, length)
     cos_t = c1[:, None, :] * c2[None, :, :] - s1[:, None, :] * s2[None, :, :]
     sin_t = s1[:, None, :] * c2[None, :, :] + c1[:, None, :] * s2[None, :, :]
     return cos_t, sin_t
 
 
+def lane_dense(block):
+    flat = block.reshape(-1)
+    pad = (-flat.shape[0]) % 1024
+    return jnp.pad(flat, (0, pad)).reshape(-1, 128)
+
+
 def injection_plane(orders, offsets, cells_x, cells_y):
     points, _, rows_kx, cols_ky = orders.shape
+    n_src = lax.axis_size("src")
     n_tx = lax.axis_size("tx")
     n_ty = lax.axis_size("ty")
     full_x = cells_x * n_tx
     full_y = cells_y * n_ty
-    amp = gather_along(orders, "ty", 0)
-    a_re = amp[:, :, 0]
-    a_im = amp[:, :, 1]
+    mx = rows_kx * n_tx
+    my = cols_ky * n_ty
+    span_x = rows_kx + 2 * SHIFT
+    span_y = cols_ky + 2 * SHIFT
+    merged = jnp.zeros((2, span_x, span_y), jnp.float32)
+    for p in range(points):
+        placed = lax.dynamic_update_slice(
+            jnp.zeros((2, span_x, span_y), jnp.float32),
+            orders[p],
+            (0, offsets[p, 0] + SHIFT, offsets[p, 1] + SHIFT),
+        )
+        merged = merged + placed
+    size = merged.size
+    got = gather_along(lane_dense(merged), ("src", "ty"), 0)
+    got = got.reshape(n_src * n_ty, -1)[:, :size].reshape(n_src, n_ty, 2, span_x, span_y)
+    got = jnp.sum(got, 0)
+    g_re = got[:, 0]
+    g_im = got[:, 1]
     y_pos = lax.axis_index("ty") * cells_y + jnp.arange(cells_y, dtype=jnp.int32)
-    by_c, by_s = chunk_tables(cols_ky, n_ty, y_pos, full_y)
-    sy_c, sy_s = phase_tables(offsets[:, 1], y_pos, full_y)
-    m_re = jnp.einsum("cpkj,cjy->pky", a_re, by_c, precision=PREC) - jnp.einsum(
-        "cpkj,cjy->pky", a_im, by_s, precision=PREC
-    )
-    m_im = jnp.einsum("cpkj,cjy->pky", a_re, by_s, precision=PREC) + jnp.einsum(
-        "cpkj,cjy->pky", a_im, by_c, precision=PREC
-    )
-    sy_c = sy_c[:, None, :]
-    sy_s = sy_s[:, None, :]
-    inner = jnp.stack([m_re * sy_c - m_im * sy_s, m_re * sy_s + m_im * sy_c], 1)
-    inner = gather_along(inner, "tx", 1)
-    i_re = inner[:, :, 0]
-    i_im = inner[:, :, 1]
+    by_c, by_s = chunk_tables(cols_ky, span_y, n_ty, my // 2 + SHIFT, y_pos, full_y)
+    i_re = jnp.einsum("cuv,cvy->uy", g_re, by_c, precision=PREC) - jnp.einsum(
+        "cuv,cvy->uy", g_im, by_s, precision=PREC
+    )
+    i_im = jnp.einsum("cuv,cvy->uy", g_re, by_s, precision=PREC) + jnp.einsum(
+        "cuv,cvy->uy", g_im, by_c, precision=PREC
+    )
+    inner = gather_along(jnp.stack([i_re, i_im]), ("tx",), 1)
+    i_re = inner[:, 0]
+    i_im = inner[:, 1]
     x_pos = lax.axis_index("tx") * cells_x + jnp.arange(cells_x, dtype=jnp.int32)
-    bx_c, bx_s = chunk_tables(rows_kx, n_tx, x_pos, full_x)
-    sx_c, sx_s = phase_tables(offsets[:, 0], x_pos, full_x)
-    q_re = jnp.einsum("ckx,cpky->pxy", bx_c, i_re, precision=PREC) - jnp.einsum(
-        "ckx,cpky->pxy", bx_s, i_im, precision=PREC
-    )
-    q_im = jnp.einsum("ckx,cpky->pxy", bx_c, i_im, precision=PREC) + jnp.einsum(
-        "ckx,cpky->pxy", bx_s, i_re, precision=PREC
-    )
-    sx_c = sx_c[:, :, None]
-    sx_s = sx_s[:, :, None]
-    plane = jnp.stack(
-        [jnp.sum(q_re * sx_c - q_im * sx_s, 0), jnp.sum(q_re * sx_s + q_im * sx_c, 0)]
-    )
-    return summed_over_pair(plane, "src", 2)
+    bx_c, bx_s = chunk_tables(rows_kx, span_x, n_tx, mx // 2 + SHIFT, x_pos, full_x)
+    p_re = jnp.einsum("cux,cuy->xy", bx_c, i_re, precision=PREC) - jnp.einsum(
+        "cux,cuy->xy", bx_s, i_im, precision=PREC
+    )
+    p_im = jnp.einsum("cux,cuy->xy", bx_c, i_im, precision=PREC) + jnp.einsum(
+        "cux,cuy->xy", bx_s, i_re, precision=PREC
+    )
+    return jnp.stack([p_re, p_im])
 
 
 def yee_kernel(e_ref, h_ref, coef_ref, plane_ref, xa_ref, xb_ref, yh_ref, eo_ref, ho_ref, ext, cp, tmp):
@@ -282,6 +279,8 @@
         for copy in copies:
             copy.wait()
 
+    shapes = [p.shape for p in outgoing]
+    outgoing = [lane_dense(p) for p in outgoing]
     got = pl.pallas_call(
         kernel,
         out_shape=tuple(jax.ShapeDtypeStruct(p.shape, p.dtype) for p in outgoing),
@@ -290,6 +289,7 @@
         scratch_shapes=[pltpu.SemaphoreType.DMA((count,)), pltpu.SemaphoreType.DMA((count,))],
         compiler_params=pltpu.CompilerParams(collective_id=3, has_side_effects=True),
     )(*outgoing)
+    got = [g.reshape(-1)[:math.prod(s)].reshape(s) for g, s in zip(got, shapes)]
     xa, xb, ya, yb, aa, ab, ba, bb = got
     y_ahead = jnp.concatenate([ya, aa, ba], 2)
     y_behind = jnp.concatenate([yb, ab, bb], 2)

time: 242 us -> 172 us (0.71)
  Pallas kernels: 198 us -> 93.8 us
  local copies, waits for them, and re-layouts: 17.5 us -> 47.7 us
  between operations: 0.89 us -> 11 us
  matrix products: 15.7 us -> 8.58 us
    pallas_call x2, Pallas kernels: 144 us -> 53 us  [gather_along(): pl.pallas_call(kernel, out_shape=jax.ShapeDtypeStruct((n,) + block.shape,...]
    reshape x0 -> x13, local copies, waits for them, and re-layouts: none -> 11.6 us  [the longest x5 3.33 us: lane_dense(): return jnp.pad(flat, (0, pad)).reshape(-1, 128)]
    pallas_call x1 -> x0, Pallas kernels: 9.2 us -> none  [summed_over_pair(): pl.pallas_call(kernel, out_shape=jax.ShapeDtypeStruct(block.shape, block....]
    dot_general x8, matrix products: 15.7 us -> 8.58 us  [the longest x1 1.7 us: injection_plane(): jnp.einsum('cux,cuy->xy', bx_c, i_im, precision=PREC)]
    slice x1 -> x10, local copies, waits for them, and re-layouts: 0.76 us -> 5.14 us  [the longest x8 3.45 us: exchange_halos(): got = [g.reshape(-1)[:math.prod(s)].reshape(s) for g, s in zip(got, shapes)]]
    pallas_call x1, Pallas kernels: 15.8 us -> 11.9 us  [exchange_halos(): pl.pallas_call(kernel, out_shape=tuple((jax.ShapeDtypeStruct(p.shape, p.d...]
    add x0 -> x4, local copies, waits for them, and re-layouts: none -> 3.55 us  [injection_plane(): merged = merged + placed]
    transpose x2 -> x0, other arithmetic: 2.81 us -> none  [exchange_halos(): t = lambda b: jnp.swapaxes(b, 1, 2)]
where the time goes in v2:
time: 172 us; the launch traced here: 170 us
  Pallas kernels  93.8 us (55%)
  local copies, waits for them, and re-layouts  47.7 us (28%)
  between operations  11 us (6%)
  other arithmetic  9.29 us (5%)
  matrix products  8.58 us (5%)
    pallas_call x2, Pallas kernels, gather_along(): pl.pallas_call(kernel, out_shape=jax.ShapeDtypeStruct((n,) + block.shape,...  53 us
    pallas_call x1, Pallas kernels, per_device(): pl.pallas_call(yee_kernel, out_shape=(out, out), in_specs=[spec] * 7, out...  28.9 us
    pallas_call x1, Pallas kernels, exchange_halos(): pl.pallas_call(kernel, out_shape=tuple((jax.ShapeDtypeStruct(p.shape, p.d...  11.9 us
    unnamed x9, local copies, waits for them, and re-layouts  10.2 us
    slice x2, local copies, waits for them, and re-layouts, exchange_halos(): parts[:, tail, :]  6.91 us
    add x4, local copies, waits for them, and re-layouts, injection_plane(): merged = merged + placed  3.55 us
    slice x8, local copies, waits for them, and re-layouts, exchange_halos(): got = [g.reshape(-1)[:math.prod(s)].reshape(s) for g, s in zip(got, shapes)]  3.45 us

profile of v2, /device:TPU:1, one launch (start us, length us, event | category | flops | bytes accessed | tf_op | source)
XLA Modules:
  0.0 170.3 jit_solution(18310042556201648833)
XLA Ops:
  0.6 1.4 select_add_fusion.coef_ref
  2.1 0.4 fusion.52
  2.5 0.1 fusion.67
  2.6 0.8 slice_bitcast_fusion.12
  3.4 1.6 fusion.69
  7.5 0.6 dynamic_update_slice.14
  10.6 0.8 bitcast_add_fusion.2
  11.4 1.2 add.264
  15.1 0.8 bitcast_add_fusion.1
  16.0 1.2 add.274
  19.7 0.8 bitcast_add_fusion
  20.5 1.2 add.284
  21.7 0.1 copy.22
  21.8 0.1 reshape.394
  21.9 0.6 pad_bitcast_fusion.x_ref
  22.5 37.5 %shard_map.68 = f32[32,64,128]{2,1,0:T(8,128)} custom-call(f32[64,128]{1,0:T(8,128)} %pad_bitcast_fusion.x_ref), custom_call_target="tpu_custom_call" | custom-call | tf_op jit(solution)/shard_map/pallas_call | solution.py:77
  60.0 1.8 %copy.36 = f32[4,8,64,128]{3,1,2,0:T(8,128)S(1)} copy(f32[4,8,64,128]{3,2,1,0:T(8,128)} %bitcast.120) | data formatting | bytes 2097152
  61.9 2.6 %reshape.397 = f32[2,16,2,80,48]{4,3,2,1,0:T(8,128)} reshape(f32[32,7680]{1,0:T(8,128)S(1)} %slice.132) | data formatting | bytes 1966080 | tf_op jit(solution)/shard_map/reshape | solution.py:126
  64.5 2.2 %reduce_sum.9 = f32[16,2,80,48]{3,2,1,0:T(8,128)S(1)} reduce(f32[2,16,2,80,48]{4,3,2,1,0:T(8,128)} %reshape.397, f32[]{:T(128)} %constant.95.clone.1), dimensions={0}, to_apply=%region_0.1 | reduce | flops 122880 | bytes 1474564 | tf_op jit(solution)/shard_map/reduce_sum | solution.py:127
  66.7 0.2 fusion.57
  66.9 0.1 fusion.65
  67.0 0.4 convolution_bitcast_fusion.4
  67.5 0.4 fusion.7
  67.9 0.4 convolution_bitcast_fusion.6
  68.4 0.4 fusion.5
  68.8 0.6 pad_maximum_fusion.1.x_ref
  69.5 15.6 %shard_map.69 = f32[8,2,80,128]{3,2,1,0:T(8,128)} custom-call(f32[2,80,128]{2,1,0:T(8,128)} %pad_maximum_fusion.1.x_ref), custom_call_target="tpu_custom_call" | custom-call | tf_op jit(solution)/shard_map/pallas_call | solution.py:77
  85.1 1.7 convolution_bitcast_fusion
  86.8 1.7 fusion.3
  88.5 1.7 convolution_bitcast_fusion.2
  90.2 1.7 fusion.1
  91.9 0.7 pad_maximum_fusion.plane_ref
  92.6 3.0 %copy.25 = f32[18,256,128]{1,2,0:T(8,128)} copy(f32[18,256,128]{2,1,0:T(8,128)} %bitcast.118) | data formatting | bytes 4718592 | tf_op jit(solution)/shard_map/reshape | solution.py:305
  95.7 3.4 %constant_dynamic-update-slice_fusion.4 = f32[44,256,128]{1,2,0:T(8,128)} fusion(f32[18,256,128]{1,2,0:T(8,128)} %copy.25), kind=kLoop, calls=%fused_computation.112 | loop fusion | bytes 4718592
  99.1 1.9 %copy.26 = f32[18,256,128]{1,2,0:T(8,128)} copy(f32[18,256,128]{2,1,0:T(8,128)S(1)} %bitcast.119) | data formatting | bytes 4718592 | tf_op jit(solution)/shard_map/reshape | solution.py:306
  101.0 3.3 %constant_dynamic-update-slice_fusion.3 = f32[44,256,128]{1,2,0:T(8,128)} fusion(f32[44,256,128]{1,2,0:T(8,128)} %constant_dynamic-update-slice_fusion.4, f32[18,256,128]{1,2,0:T(8,128)} %copy.26), kind=kLoop, calls=%fused_computation.111 | loop fusion | bytes 4718592
  104.3 0.3 copy.27
  104.6 1.0 constant_dynamic-update-slice_fusion.2
  105.5 0.1 copy.28
  105.6 0.7 constant_dynamic-update-slice_fusion.1
  106.3 0.1 copy.29
  106.4 0.7 constant_dynamic-update-slice_fusion
  107.1 5.4 %fusion.68 = (f32[44,4,128]{1,2,0:T(8,128)S(1)}, f32[44,4,128]{1,2,0:T(8,128)}) fusion(f32[44,256,128]{1,2,0:T(8,128)} %constant_dynamic-update-slice_fusion), kind=kLoop, calls=%fused_computation.133 | loop fusion | bytes 360448 | tf_op jit(solution)/shard_map/slice | solution.py:245
  112.5 3.3 %copy.30 = f32[44,4,128]{2,1,0:T(4,128)} copy(f32[44,4,128]{1,2,0:T(8,128)} %get-tuple-element.25) | data formatting | bytes 180224 | tf_op jit(solution)/shard_map/slice | solution.py:244
  115.8 1.5 copy.31
  117.3 1.2 slice_bitcast_fusion.6
  118.5 0.7 reshape.402.refs_2_
  119.2 0.7 reshape.403.refs_3_
  120.0 1.4 slice_bitcast_fusion.8
  121.3 0.1 reshape.406
  121.4 0.1 reshape.404
  121.6 0.6 pad_bitcast_fusion.3
  122.2 0.1 reshape.410
  122.3 0.1 reshape.408
  122.4 0.6 pad_bitcast_fusion.1
  123.1 11.9 %shard_map.70 = (f32[176,128]{1,0:T(8,128)}, f32[176,128]{1,0:T(8,128)}, f32[352,128]{1,0:T(8,128)}, f32[352,128]{1,0:T(8,128)}, f32[8,128]{1,0:T(8,128)}, /*ind...) custom-call(f32[176,128]{1,0:T(8,128)} %bitcast.122, f32[176,128]{1,0:T(8,128)} %bitcast.123, ...), custom_call_target="tpu_custom_call" | custom-call | tf_op jit(solution)/shard_map/pallas_call | solution.py:284
  134.9 0.8 slice.130
  135.8 0.9 slice.128
  136.7 1.0 reshape_reshape.15
  137.7 0.9 slice.126
  138.6 0.9 slice.124
  139.4 1.0 reshape_reshape.14
  140.5 1.0 maximum_maximum_fusion.yh_ref
  141.4 28.9 %shard_map.71 = (f32[3,6,256,128]{3,2,1,0:T(8,128)}, f32[3,6,256,128]{3,2,1,0:T(8,128)}) custom-call(f32[3,6,256,128]{3,2,1,0:T(8,128)} %e_ref.1, f32[3,6,256,128]{3,2,1,0:T(8,128)} %h_ref.1, f32[6,256,128]{2,1,0:T(8,128)} %copy-done.1, f32[2,256,128]{2,1,0:T(8,128)} %pad_maximum_fusion.plane_ref, f32[44,4,128]{2,1,0:T(4,128)} %bitcast.124, ...), custom_call_target="tpu_custom_call" | custom-call | tf_op jit(solution)/shard_map/pallas_call | solution.py:319
  (16 shorter events, 0.1 us)
Async XLA Ops:
  2.0 102.3 %copy-start.1 = (f32[6,256,128]{2,1,0:T(8,128)}, f32[6,256,128]{2,1,0:T(8,128)S(1)}, u32[]{:S(2)}) copy-start(f32[6,256,128]{2,1,0:T(8,128)S(1)} %select_add_fusion.coef_ref) | copy-start | bytes 2359300
  95.7 3.4 %copy-start = (f32[3,6,256,128]{3,2,1,0:T(8,128)S(1)}, f32[3,6,256,128]{3,2,1,0:T(8,128)}, u32[]{:S(2)}) copy-start(f32[3,6,256,128]{3,2,1,0:T(8,128)} %h_ref.1) | copy-start | bytes 7077892

commit v3 on v2

--- a/solution.py
+++ b/solution.py
@@ -16,6 +16,7 @@
 PERMITTIVITY = (1.0, 2.6, 11.9, 2.1)
 PREC = lax.Precision.HIGH
 SHIFT = 8
+HALO = 8
 
 
 def phase_tables(freqs, positions, length):
@@ -113,14 +114,17 @@
     my = cols_ky * n_ty
     span_x = rows_kx + 2 * SHIFT
     span_y = cols_ky + 2 * SHIFT
-    merged = jnp.zeros((2, span_x, span_y), jnp.float32)
-    for p in range(points):
-        placed = lax.dynamic_update_slice(
-            jnp.zeros((2, span_x, span_y), jnp.float32),
-            orders[p],
-            (0, offsets[p, 0] + SHIFT, offsets[p, 1] + SHIFT),
-        )
-        merged = merged + placed
+    lift_x = (
+        lax.broadcasted_iota(jnp.int32, (points, span_x, rows_kx), 1)
+        == lax.broadcasted_iota(jnp.int32, (points, span_x, rows_kx), 2) + offsets[:, 0:1, None] + SHIFT
+    ).astype(jnp.float32)
+    lift_y = (
+        lax.broadcasted_iota(jnp.int32, (points, span_y, cols_ky), 1)
+        == lax.broadcasted_iota(jnp.int32, (points, span_y, cols_ky), 2) + offsets[:, 1:2, None] + SHIFT
+    ).astype(jnp.float32)
+    exact = lax.Precision.HIGHEST
+    placed = jnp.einsum("puk,prkj->pruj", lift_x, orders, precision=exact)
+    merged = jnp.einsum("pruj,pvj->ruv", placed, lift_y, precision=exact)
     size = merged.size
     got = gather_along(lane_dense(merged), ("src", "ty"), 0)
     got = got.reshape(n_src * n_ty, -1)[:, :size].reshape(n_src, n_ty, 2, span_x, span_y)
@@ -149,45 +153,115 @@
     return jnp.stack([p_re, p_im])
 
 
-def yee_kernel(e_ref, h_ref, coef_ref, plane_ref, xa_ref, xb_ref, yh_ref, eo_ref, ho_ref, ext, cp, tmp):
+def yee_kernel(e_ref, h_ref, coef_ref, plane_ref, eo_ref, ho_ref,
+               ext, cp, tmp, srow, rrow, scol, rcol, send, recv):
     layers, cells_x, cells_y = coef_ref.shape
-    depth = xa_ref.shape[1]
+    depth = srow.shape[2]
     rows = cells_x + 2 * depth
     lanes = ext.shape[2]
     slab = layers + 2
     n_field = 6 * layers
+    n_parts = n_field + layers + 2
+    n_tx = lax.axis_size("tx")
+    n_ty = lax.axis_size("ty")
+    me_x = lax.axis_index("tx")
+    me_y = lax.axis_index("ty")
+    x_lo = {"tx": lax.rem(me_x + n_tx - 1, n_tx)}
+    x_hi = {"tx": lax.rem(me_x + 1, n_tx)}
+    y_lo = {"ty": lax.rem(me_y + n_ty - 1, n_ty)}
+    y_hi = {"ty": lax.rem(me_y + 1, n_ty)}
+
+    barrier = pltpu.get_barrier_semaphore()
+    for peer in (x_lo, x_hi, y_lo, y_hi):
+        pl.semaphore_signal(barrier, 1, device_id=peer, device_id_type=MESH)
+    pl.semaphore_wait(barrier, 4)
+
+    def own_part(h):
+        comp = h // layers
+        z = h % layers
+        return jnp.where(comp < 3, e_ref[comp % 3, z], h_ref[comp % 3, z])
+
+    def field_slot(h):
+        return (h // layers) * slab + h % layers + 1
+
+    def fill_rows(h, carry):
+        part = own_part(h)
+        srow[0, h] = part[0:depth]
+        srow[1, h] = part[cells_x - depth:cells_x]
+        ext[field_slot(h), 0:cells_x, 0:cells_y] = part
+        return carry
+
+    lax.fori_loop(0, n_field, fill_rows, 0)
+    for k in range(layers + 2):
+        part = coef_ref[k] if k < layers else plane_ref[k - layers]
+        srow[0, n_field + k] = part[0:depth]
+        srow[1, n_field + k] = part[cells_x - depth:cells_x]
+        cp[k, 0:cells_x, 0:cells_y] = part
+    row_copies = [
+        pltpu.make_async_remote_copy(
+            src_ref=srow.at[0], dst_ref=rrow.at[0], send_sem=send.at[0], recv_sem=recv.at[0],
+            device_id=x_lo, device_id_type=MESH,
+        ),
+        pltpu.make_async_remote_copy(
+            src_ref=srow.at[1], dst_ref=rrow.at[1], send_sem=send.at[1], recv_sem=recv.at[1],
+            device_id=x_hi, device_id_type=MESH,
+        ),
+    ]
+    for copy in row_copies:
+        copy.start()
     zero = jnp.zeros((rows, lanes), jnp.float32)
     for comp in range(3):
         ext[comp * slab + slab - 1] = zero
         ext[(3 + comp) * slab] = zero
     tmp[...] = jnp.zeros_like(tmp)
+    for copy in row_copies:
+        copy.wait()
+
+    def fill_cols(dst, idx, h):
+        dst[idx, cells_x:cells_x + depth, 0:cells_y] = rrow[0, h]
+        dst[idx, cells_x + depth:rows, 0:cells_y] = rrow[1, h]
+        t = dst[idx, :, 0:cells_y].T
+        scol[0, h] = t[0:depth]
+        scol[1, h] = t[cells_y - depth:cells_y]
+
+    def cols_fields(h, carry):
+        fill_cols(ext, field_slot(h), h)
+        return carry
+
+    lax.fori_loop(0, n_field, cols_fields, 0)
+    for k in range(layers + 2):
+        fill_cols(cp, k, n_field + k)
+    col_copies = [
+        pltpu.make_async_remote_copy(
+            src_ref=scol.at[0], dst_ref=rcol.at[0], send_sem=send.at[2], recv_sem=recv.at[2],
+            device_id=y_lo, device_id_type=MESH,
+        ),
+        pltpu.make_async_remote_copy(
+            src_ref=scol.at[1], dst_ref=rcol.at[1], send_sem=send.at[3], recv_sem=recv.at[3],
+            device_id=y_hi, device_id_type=MESH,
+        ),
+    ]
+    for copy in col_copies:
+        copy.start()
+    for copy in col_copies:
+        copy.wait()
     lane = lax.broadcasted_iota(jnp.int32, (rows, cells_y), 1)
 
-    def place(h, slot, own):
-        dst = ext if slot is not None else cp
-        idx = slot if slot is not None else h - n_field
-        dst[idx, 0:cells_x, 0:cells_y] = own
-        dst[idx, cells_x:cells_x + depth, 0:cells_y] = xa_ref[h]
-        dst[idx, cells_x + depth:rows, 0:cells_y] = xb_ref[h]
-        tmp[:, 0:2 * depth] = yh_ref[h].T
-        v = tmp[...]
-        front = jnp.where(lane < depth, v, 0.0)
-        back = jnp.where(lane >= depth, v, 0.0)
+    def place_cols(dst, idx, h):
+        v = jnp.concatenate([rcol[0, h], rcol[1, h]], 0)
+        tmp[:, 0:2 * depth] = v.T
+        w = tmp[...]
+        front = jnp.where(lane < depth, w, 0.0)
+        back = jnp.where(lane >= depth, w, 0.0)
         dst[idx, :, cells_y:lanes] = front + pltpu.roll(back, cells_y - 2 * depth, 1)
 
-    def fields(h, carry):
-        comp = h // layers
-        z = h % layers
-        slot = comp * slab + z + 1
-        own = jnp.where(comp < 3, e_ref[comp % 3, z], h_ref[comp % 3, z])
-        place(h, slot, own)
+    def place_fields(h, carry):
+        place_cols(ext, field_slot(h), h)
         return carry
 
-    lax.fori_loop(0, n_field, fields, 0)
-    for z in range(layers):
-        place(n_field + z, None, coef_ref[z])
-    for k in range(2):
-        place(n_field + layers + k, None, plane_ref[k])
+    lax.fori_loop(0, n_field, place_fields, 0)
+    for k in range(layers + 2):
+        place_cols(cp, k, n_field + k)
 
     ahead_x = lambda f: pltpu.roll(f, rows - 1, 0)
     ahead_y = lambda f: pltpu.roll(f, lanes - 1, 1)
@@ -233,101 +307,35 @@
             ho_ref[comp, z] = ext[(3 + comp) * slab + z + 1, 0:cells_x, 0:cells_y]
 
 
-OFFSETS = ((1, 0), (-1, 0), (0, 1), (0, -1), (1, 1), (1, -1), (-1, 1), (-1, -1))
-
-
-def exchange_halos(parts, depth):
-    head = slice(0, depth)
-    tail = slice(-depth, None)
-    t = lambda b: jnp.swapaxes(b, 1, 2)
-    outgoing = [
-        parts[:, head, :],
-        parts[:, tail, :],
-        t(parts[:, :, head]),
-        t(parts[:, :, tail]),
-        t(parts[:, head, head]),
-        t(parts[:, head, tail]),
-        t(parts[:, tail, head]),
-        t(parts[:, tail, tail]),
-    ]
-    count = len(OFFSETS)
-
-    def kernel(*refs):
-        ins = refs[:count]
-        outs = refs[count:2 * count]
-        send, recv = refs[2 * count:]
-        n_tx = lax.axis_size("tx")
-        n_ty = lax.axis_size("ty")
-        me_x = lax.axis_index("tx")
-        me_y = lax.axis_index("ty")
-        targets = [
-            {"tx": lax.rem(me_x - dx + n_tx, n_tx), "ty": lax.rem(me_y - dy + n_ty, n_ty)}
-            for dx, dy in OFFSETS
-        ]
-        barrier = pltpu.get_barrier_semaphore()
-        for target in targets:
-            pl.semaphore_signal(barrier, 1, device_id=target, device_id_type=MESH)
-        pl.semaphore_wait(barrier, count)
-        copies = []
-        for k in range(count):
-            copy = pltpu.make_async_remote_copy(
-                src_ref=ins[k], dst_ref=outs[k], send_sem=send.at[k], recv_sem=recv.at[k],
-                device_id=targets[k], device_id_type=MESH,
-            )
-            copy.start()
-            copies.append(copy)
-        for copy in copies:
-            copy.wait()
-
-    shapes = [p.shape for p in outgoing]
-    outgoing = [lane_dense(p) for p in outgoing]
-    got = pl.pallas_call(
-        kernel,
-        out_shape=tuple(jax.ShapeDtypeStruct(p.shape, p.dtype) for p in outgoing),
-        in_specs=[VMEM_SPEC] * count,
-        out_specs=tuple([VMEM_SPEC] * count),
-        scratch_shapes=[pltpu.SemaphoreType.DMA((count,)), pltpu.SemaphoreType.DMA((count,))],
-        compiler_params=pltpu.CompilerParams(collective_id=3, has_side_effects=True),
-    )(*outgoing)
-    got = [g.reshape(-1)[:math.prod(s)].reshape(s) for g, s in zip(got, shapes)]
-    xa, xb, ya, yb, aa, ab, ba, bb = got
-    y_ahead = jnp.concatenate([ya, aa, ba], 2)
-    y_behind = jnp.concatenate([yb, ab, bb], 2)
-    return xa, xb, jnp.concatenate([y_ahead, y_behind], 1)
-
-
 def per_device(orders, offsets, material, e_field, h_field):
     layers, cells_x, cells_y = material.shape
     plane = injection_plane(orders, offsets, cells_x, cells_y)
     coefficient = cell_coefficient(material)
-    parts = jnp.concatenate(
-        [
-            e_field.reshape(3 * layers, cells_x, cells_y),
-            h_field.reshape(3 * layers, cells_x, cells_y),
-            coefficient,
-            plane,
-        ],
-        0,
-    )
-    depth = STEPS
-    xa, xb, yh = exchange_halos(parts, depth)
+    depth = HALO
     rows = cells_x + 2 * depth
     lanes = 2 * cells_y
-    vmem = pltpu.MemorySpace.VMEM
-    spec = pl.BlockSpec(memory_space=vmem)
+    n_parts = 6 * layers + layers + 2
     out = jax.ShapeDtypeStruct(e_field.shape, jnp.float32)
     return pl.pallas_call(
         yee_kernel,
         out_shape=(out, out),
-        in_specs=[spec] * 7,
-        out_specs=(spec, spec),
+        in_specs=[VMEM_SPEC] * 4,
+        out_specs=(VMEM_SPEC, VMEM_SPEC),
         scratch_shapes=[
             pltpu.VMEM((6 * (layers + 2), rows, lanes), jnp.float32),
             pltpu.VMEM((layers + 2, rows, lanes), jnp.float32),
             pltpu.VMEM((rows, cells_y), jnp.float32),
+            pltpu.VMEM((2, n_parts, depth, cells_y), jnp.float32),
+            pltpu.VMEM((2, n_parts, depth, cells_y), jnp.float32),
+            pltpu.VMEM((2, n_parts, depth, rows), jnp.float32),
+            pltpu.VMEM((2, n_parts, depth, rows), jnp.float32),
+            pltpu.SemaphoreType.DMA((4,)),
+            pltpu.SemaphoreType.DMA((4,)),
         ],
-        compiler_params=pltpu.CompilerParams(vmem_limit_bytes=64 * 1024 * 1024),
-    )(e_field, h_field, coefficient, plane, xa, xb, yh)
+        compiler_params=pltpu.CompilerParams(
+            collective_id=3, has_side_effects=True, vmem_limit_bytes=64 * 1024 * 1024
+        ),
+    )(e_field, h_field, coefficient, plane)
 
 
 def solution(mesh):

time: 172 us -> 130 us (0.76)
  local copies, waits for them, and re-layouts: 47.7 us -> 10.9 us
  Pallas kernels: 93.8 us -> 104 us
  between operations: 11 us -> 0.84 us
  other arithmetic: 9.29 us -> 5.53 us
    slice x12 -> x0, local copies, waits for them, and re-layouts: 15.3 us -> none  [the longest x2 6.91 us: exchange_halos(): parts[:, tail, :]]
    pallas_call x2 -> x1, Pallas kernels: 40.8 us -> 51.7 us  [per_device(): pl.pallas_call(yee_kernel, out_shape=(out, out), in_specs=[VMEM_SPEC] * 4...]
    reshape x2 -> x0, local copies, waits for them, and re-layouts: 4.99 us -> none  [the longest x1 3.04 us: per_device(): e_field.reshape(3 * layers, cells_x, cells_y)]
    unnamed x9, local copies, waits for them, and re-layouts: 10.2 us -> 6.68 us
    add x5 -> x1, local copies, waits for them, and re-layouts: 3.81 us -> 0.76 us  [injection_plane(): lax.broadcasted_iota(jnp.int32, (points, span_y, cols_ky), 2)]
    reshape x5 -> x1, local copies, waits for them, and re-layouts: 3.33 us -> 0.62 us  [lane_dense(): return jnp.pad(flat, (0, pad)).reshape(-1, 128)]
    dynamic_update_slice x3 -> x0, other arithmetic: 2.52 us -> none  [injection_plane(): lax.dynamic_update_slice(jnp.zeros((2, span_x, span_y), jnp.float32), ord...]
    transpose x2 -> x0, local copies, waits for them, and re-layouts: 2.51 us -> none  [exchange_halos(): t = lambda b: jnp.swapaxes(b, 1, 2)]
where the time goes in v3:
time: 130 us
  Pallas kernels  104 us (80%)
  local copies, waits for them, and re-layouts  10.9 us (8%)
  matrix products  8.17 us (6%)
  other arithmetic  5.53 us (4%)
    pallas_call x2, Pallas kernels, gather_along(): pl.pallas_call(kernel, out_shape=jax.ShapeDtypeStruct((n,) + block.shape,...  52.5 us
    pallas_call x1, Pallas kernels, per_device(): pl.pallas_call(yee_kernel, out_shape=(out, out), in_specs=[VMEM_SPEC] * 4...  51.7 us
    unnamed x9, local copies, waits for them, and re-layouts  6.68 us
    reshape x1, local copies, waits for them, and re-layouts, injection_plane(): got.reshape(n_src * n_ty, -1)[:, :size]  2.64 us

profile of v3, /device:TPU:1, one launch (start us, length us, event | category | flops | bytes accessed | tf_op | source)
XLA Modules:
  0.0 129.6 jit_solution(11254215151474628386)
XLA Ops:
  0.6 0.0 copy-start.1
  0.7 0.8 slice_bitcast_fusion.6
  1.5 0.1 fusion.74
  1.6 0.1 fusion.76
  1.7 0.2 fusion.66
  1.9 1.2 convolution_bitcast_fusion.4
  3.1 0.3 convolution_bitcast_fusion.5
  3.4 0.1 reshape.298
  3.5 0.6 pad_bitcast_fusion.x_ref
  4.1 0.4 fusion.59
  4.5 0.0 copy-done.1
  4.5 1.2 select_add_fusion.coef_ref
  5.7 36.9 %shard_map.68 = f32[32,64,128]{2,1,0:T(8,128)} custom-call(f32[64,128]{1,0:T(8,128)} %pad_bitcast_fusion.x_ref), custom_call_target="tpu_custom_call" | custom-call | tf_op jit(solution)/shard_map/pallas_call | solution.py:78
  42.6 1.8 %copy.20 = f32[4,8,64,128]{3,1,2,0:T(8,128)S(1)} copy(f32[4,8,64,128]{3,2,1,0:T(8,128)} %bitcast.83) | data formatting | bytes 2097152
  44.5 0.1 slice.28
  44.5 2.6 %reshape.301 = f32[2,16,2,80,48]{4,3,2,1,0:T(8,128)} reshape(f32[32,7680]{1,0:T(8,128)S(1)} %slice.28) | data formatting | bytes 1966080 | tf_op jit(solution)/shard_map/reshape | solution.py:130
  47.2 2.2 %reduce_sum.9 = f32[16,2,80,48]{3,2,1,0:T(8,128)S(1)} reduce(f32[2,16,2,80,48]{4,3,2,1,0:T(8,128)} %reshape.301, f32[]{:T(128)} %constant.34.clone.1), dimensions={0}, to_apply=%region_0.1 | reduce | flops 122880 | bytes 1474564 | tf_op jit(solution)/shard_map/reduce_sum | solution.py:131
  49.3 0.4 convolution_bitcast_fusion.6
  49.8 0.4 fusion.7
  50.2 0.4 convolution_bitcast_fusion.8
  50.7 0.4 fusion.5
  51.1 0.6 pad_maximum_fusion.1.x_ref
  51.8 15.6 %shard_map.69 = f32[8,2,80,128]{3,2,1,0:T(8,128)} custom-call(f32[2,80,128]{2,1,0:T(8,128)} %pad_maximum_fusion.1.x_ref), custom_call_target="tpu_custom_call" | custom-call | tf_op jit(solution)/shard_map/pallas_call | solution.py:78
  67.3 0.0 copy-start.2
  67.4 1.8 %convolution_bitcast_fusion = f32[256,128]{1,0:T(8,128)S(1)} fusion(f32[80,256]{1,0:T(8,128)S(1)} %get-tuple-element.5, f32[8,256]{1,0:T(8,128)S(1)} %get-tuple-element.3, f32[80,256]{1,0:T(8,128)S(1)} %get-tuple-element.4, f32[8,256]{1,0:T(8,128)S(1)} %get-tuple-element.2, f32[8,2,80,128]{3,2,1,0:T(8,128)} %shard_map.69), kind=kOutput, calls=%fused_computation | convolution fusion | flops 126320640 | bytes 638976 | tf_op jit(solution)/shard_map/cux,cuy->xy/dot_general | solution.py:150
  69.1 1.7 %fusion.3 = f32[1,256,128]{2,1,0:T(8,128)S(1)} fusion(f32[256,128]{1,0:T(8,128)S(1)} %convolution_bitcast_fusion, f32[80,256]{1,0:T(8,128)S(1)} %get-tuple-element.5, f32[8,256]{1,0:T(8,128)S(1)} %get-tuple-element.3, f32[80,256]{1,0:T(8,128)S(1)} %get-tuple-element.4, f32[8,256]{1,0:T(8,128)S(1)} %get-tuple-element.2, f32[8,2,80,128]{3,2,1,0:T(8,128)} %shard_map.69), kind=kOutput, calls=%fused_computation.8 | convolution fusion | flops 126353408 | bytes 770048 | tf_op jit(solution)/shard_map/cux,cuy->xy/dot_general | solution.py:150
  70.8 0.0 copy-done.2
  70.8 0.7 convolution_bitcast_fusion.2
  71.6 0.7 fusion.1
  72.3 0.7 pad_maximum_fusion.plane_ref
  73.0 51.7 %shard_map.70 = (f32[3,6,256,128]{3,2,1,0:T(8,128)}, f32[3,6,256,128]{3,2,1,0:T(8,128)}) custom-call(f32[3,6,256,128]{3,2,1,0:T(8,128)} %e_ref.1, f32[3,6,256,128]{3,2,1,0:T(8,128)} %h_ref.1, f32[6,256,128]{2,1,0:T(8,128)} %select_add_fusion.coef_ref, f32[2,256,128]{2,1,0:T(8,128)} %pad_maximum_fusion.plane_ref), custom_call_target="tpu_custom_call" | custom-call | tf_op jit(solution)/shard_map/pallas_call | solution.py:319
  124.7 0.0 copy-start
  124.7 3.4 %copy.23 = f32[3,6,256,128]{3,2,1,0:T(8,128)} copy(f32[3,6,256,128]{3,2,1,0:T(8,128)} %get-tuple-element.14) | data formatting | bytes 4718592
  128.2 0.0 copy-done
  128.2 1.4 %copy.24 = f32[3,6,256,128]{3,2,1,0:T(8,128)} copy(f32[3,6,256,128]{3,2,1,0:T(8,128)S(1)} %copy-done) | data formatting | bytes 4718592
  (6 shorter events, 0.0 us)
Async XLA Ops:
  0.6 3.9 %copy-start.1 = (s32[6,256,128]{2,1,0:T(8,128)S(1)}, s32[6,256,128]{2,1,0:T(8,128)}, u32[]{:S(2)}) copy-start(s32[6,256,128]{2,1,0:T(8,128)} %param.7) | copy-start | bytes 2359300
  67.3 3.5 %copy-start.2 = (f32[8,2,80,128]{3,2,1,0:T(8,128)S(1)}, f32[8,2,80,128]{3,2,1,0:T(8,128)}, u32[]{:S(2)}) copy-start(f32[8,2,80,128]{3,2,1,0:T(8,128)} %shard_map.69) | copy-start | bytes 1966084
  124.7 3.4 %copy-start = (f32[3,6,256,128]{3,2,1,0:T(8,128)S(1)}, f32[3,6,256,128]{3,2,1,0:T(8,128)}, u32[]{:S(2)}) copy-start(f32[3,6,256,128]{3,2,1,0:T(8,128)} %get-tuple-element.15) | copy-start | bytes 7077892

commit v4 on v3

--- a/solution.py
+++ b/solution.py
@@ -89,6 +89,34 @@
     )(block)
 
 
+def summed_over_pair(block, axis, collective):
+    def kernel(x_ref, o_ref, got, send, recv):
+        other = {axis: 1 - lax.axis_index(axis)}
+        barrier = pltpu.get_barrier_semaphore()
+        pl.semaphore_signal(barrier, 1, device_id=other, device_id_type=MESH)
+        pl.semaphore_wait(barrier, 1)
+        copy = pltpu.make_async_remote_copy(
+            src_ref=x_ref, dst_ref=got, send_sem=send.at[0], recv_sem=recv.at[0],
+            device_id=other, device_id_type=MESH,
+        )
+        copy.start()
+        copy.wait()
+        o_ref[...] = x_ref[...] + got[...]
+
+    return pl.pallas_call(
+        kernel,
+        out_shape=jax.ShapeDtypeStruct(block.shape, block.dtype),
+        in_specs=[VMEM_SPEC],
+        out_specs=VMEM_SPEC,
+        scratch_shapes=[
+            pltpu.VMEM(block.shape, block.dtype),
+            pltpu.SemaphoreType.DMA((1,)),
+            pltpu.SemaphoreType.DMA((1,)),
+        ],
+        compiler_params=pltpu.CompilerParams(collective_id=collective, has_side_effects=True),
+    )(block)
+
+
 def chunk_tables(step, span, count, base, positions, length):
     c1, s1 = phase_tables(jnp.arange(count, dtype=jnp.int32) * step, positions, length)
     c2, s2 = phase_tables(jnp.arange(span, dtype=jnp.int32) - base, positions, length)
@@ -126,9 +154,9 @@
     placed = jnp.einsum("puk,prkj->pruj", lift_x, orders, precision=exact)
     merged = jnp.einsum("pruj,pvj->ruv", placed, lift_y, precision=exact)
     size = merged.size
-    got = gather_along(lane_dense(merged), ("src", "ty"), 0)
-    got = got.reshape(n_src * n_ty, -1)[:, :size].reshape(n_src, n_ty, 2, span_x, span_y)
-    got = jnp.sum(got, 0)
+    merged = summed_over_pair(lane_dense(merged), "src", 2)
+    got = gather_along(merged, ("ty",), 0)
+    got = got.reshape(n_ty, -1)[:, :size].reshape(n_ty, 2, span_x, span_y)
     g_re = got[:, 0]
     g_im = got[:, 1]
     y_pos = lax.axis_index("ty") * cells_y + jnp.arange(cells_y, dtype=jnp.int32)

time: 130 us -> 118 us (0.908)
  Pallas kernels: 104 us -> 97.3 us
  local copies, waits for them, and re-layouts: 10.9 us -> 8.25 us
  other arithmetic: 5.53 us -> 3.38 us
    pallas_call x2, Pallas kernels: 52.5 us -> 39.6 us  [gather_along(): pl.pallas_call(kernel, out_shape=jax.ShapeDtypeStruct((n,) + block.shape,...]
    pallas_call x0 -> x1, Pallas kernels: none -> 4.81 us  [summed_over_pair(): pl.pallas_call(kernel, out_shape=jax.ShapeDtypeStruct(block.shape, block....]
    reduce_sum x1 -> x0, other arithmetic: 2.15 us -> none  [injection_plane(): got = jnp.sum(got, 0)]
    reshape x1, local copies, waits for them, and re-layouts: 2.64 us -> 0.55 us  [injection_plane(): got = got.reshape(n_ty, -1)[:, :size].reshape(n_ty, 2, span_x, span_y)]
where the time goes in v4:
time: 118 us
  Pallas kernels  97.3 us (82%)
  local copies, waits for them, and re-layouts  8.25 us (7%)
  matrix products  8.23 us (7%)
  other arithmetic  3.38 us (3%)
    pallas_call x1, Pallas kernels, per_device(): pl.pallas_call(yee_kernel, out_shape=(out, out), in_specs=[VMEM_SPEC] * 4...  53 us
    pallas_call x2, Pallas kernels, gather_along(): pl.pallas_call(kernel, out_shape=jax.ShapeDtypeStruct((n,) + block.shape,...  39.6 us
    unnamed x9, local copies, waits for them, and re-layouts  6.19 us
    pallas_call x1, Pallas kernels, summed_over_pair(): pl.pallas_call(kernel, out_shape=jax.ShapeDtypeStruct(block.shape, block....  4.81 us

profile of v4, /device:TPU:1, one launch (start us, length us, event | category | flops | bytes accessed | tf_op | source)
XLA Modules:
  0.0 118.1 jit_solution(9757097444606878840)
XLA Ops:
  0.7 0.8 slice_bitcast_fusion.6
  1.5 0.1 fusion.74
  1.6 0.1 fusion.76
  1.7 0.2 fusion.66
  1.9 1.2 %convolution_bitcast_fusion.4 = f32[4,2,80,32]{2,3,0,1:T(8,128)S(1)} fusion(f32[4,2,64,32]{2,3,1,0:T(8,128)} %param.5, s32[4]{0:T(128)S(1)} %get-tuple-element.11), kind=kOutput, calls=%fused_computation.4 | convolution fusion | flops 15790080 | bytes 147472 | tf_op jit(solution)/shard_map/puk,prkj->pruj/dot_general | solution.py:154
  3.2 0.3 convolution_bitcast_fusion.5
  3.4 0.1 reshape.298
  3.6 0.6 pad_bitcast_fusion.x_ref
  4.2 4.8 %shard_map.68.x_ref = f32[64,128]{1,0:T(8,128)} custom-call(f32[64,128]{1,0:T(8,128)} %pad_bitcast_fusion.x_ref), custom_call_target="tpu_custom_call" | custom-call | tf_op jit(solution)/shard_map/pallas_call | solution.py:106
  9.0 0.4 fusion.59
  9.4 0.0 copy-start.1
  9.4 23.9 %shard_map.69 = f32[16,64,128]{2,1,0:T(8,128)} custom-call(f32[64,128]{1,0:T(8,128)} %shard_map.68.x_ref), custom_call_target="tpu_custom_call" | custom-call | tf_op jit(solution)/shard_map/pallas_call | solution.py:78
  33.3 1.4 %copy.19 = f32[2,8,64,128]{3,1,2,0:T(8,128)S(1)} copy(f32[2,8,64,128]{3,2,1,0:T(8,128)} %bitcast.83) | data formatting | bytes 1048576
  34.7 0.0 copy-done.1
  34.7 1.2 select_add_fusion.coef_ref
  35.9 0.5 reshape.301
  36.4 0.4 convolution_bitcast_fusion.6
  36.9 0.4 fusion.7
  37.3 0.4 convolution_bitcast_fusion.8
  37.8 0.4 fusion.5
  38.2 0.6 pad_maximum_fusion.1.x_ref
  38.9 15.7 %shard_map.70 = f32[8,2,80,128]{3,2,1,0:T(8,128)} custom-call(f32[2,80,128]{2,1,0:T(8,128)} %pad_maximum_fusion.1.x_ref), custom_call_target="tpu_custom_call" | custom-call | tf_op jit(solution)/shard_map/pallas_call | solution.py:78
  54.6 0.0 copy-start.2
  54.6 1.8 %convolution_bitcast_fusion = f32[256,128]{1,0:T(8,128)S(1)} fusion(f32[80,256]{1,0:T(8,128)S(1)} %get-tuple-element.5, f32[8,256]{1,0:T(8,128)S(1)} %get-tuple-element.3, f32[80,256]{1,0:T(8,128)S(1)} %get-tuple-element.4, f32[8,256]{1,0:T(8,128)S(1)} %get-tuple-element.2, f32[8,2,80,128]{3,2,1,0:T(8,128)} %shard_map.70), kind=kOutput, calls=%fused_computation | convolution fusion | flops 126320640 | bytes 638976 | tf_op jit(solution)/shard_map/cux,cuy->xy/dot_general | solution.py:178
  56.3 1.7 %fusion.3 = f32[1,256,128]{2,1,0:T(8,128)S(1)} fusion(f32[256,128]{1,0:T(8,128)S(1)} %convolution_bitcast_fusion, f32[80,256]{1,0:T(8,128)S(1)} %get-tuple-element.5, f32[8,256]{1,0:T(8,128)S(1)} %get-tuple-element.3, f32[80,256]{1,0:T(8,128)S(1)} %get-tuple-element.4, f32[8,256]{1,0:T(8,128)S(1)} %get-tuple-element.2, f32[8,2,80,128]{3,2,1,0:T(8,128)} %shard_map.70), kind=kOutput, calls=%fused_computation.8 | convolution fusion | flops 126353408 | bytes 770048 | tf_op jit(solution)/shard_map/cux,cuy->xy/dot_general | solution.py:178
  58.0 0.0 copy-done.2
  58.1 0.7 convolution_bitcast_fusion.2
  58.8 0.7 fusion.1
  59.5 0.7 pad_maximum_fusion.plane_ref
  60.2 53.0 %shard_map.71 = (f32[3,6,256,128]{3,2,1,0:T(8,128)}, f32[3,6,256,128]{3,2,1,0:T(8,128)}) custom-call(f32[3,6,256,128]{3,2,1,0:T(8,128)} %e_ref.1, f32[3,6,256,128]{3,2,1,0:T(8,128)} %h_ref.1, f32[6,256,128]{2,1,0:T(8,128)} %select_add_fusion.coef_ref, f32[2,256,128]{2,1,0:T(8,128)} %pad_maximum_fusion.plane_ref), custom_call_target="tpu_custom_call" | custom-call | tf_op jit(solution)/shard_map/pallas_call | solution.py:347
  113.2 0.0 copy-start
  113.2 3.4 %copy.22 = f32[3,6,256,128]{3,2,1,0:T(8,128)} copy(f32[3,6,256,128]{3,2,1,0:T(8,128)} %get-tuple-element.14) | data formatting | bytes 4718592
  116.6 0.0 copy-done
  116.6 1.4 %copy.23 = f32[3,6,256,128]{3,2,1,0:T(8,128)} copy(f32[3,6,256,128]{3,2,1,0:T(8,128)S(1)} %copy-done) | data formatting | bytes 4718592
  (7 shorter events, 0.1 us)
Async XLA Ops:
  9.4 25.3 %copy-start.1 = (s32[6,256,128]{2,1,0:T(8,128)S(1)}, s32[6,256,128]{2,1,0:T(8,128)}, u32[]{:S(2)}) copy-start(s32[6,256,128]{2,1,0:T(8,128)} %param.7) | copy-start | bytes 2359300
  54.6 3.5 %copy-start.2 = (f32[8,2,80,128]{3,2,1,0:T(8,128)S(1)}, f32[8,2,80,128]{3,2,1,0:T(8,128)}, u32[]{:S(2)}) copy-start(f32[8,2,80,128]{3,2,1,0:T(8,128)} %shard_map.70) | copy-start | bytes 1966084
  113.2 3.4 %copy-start = (f32[3,6,256,128]{3,2,1,0:T(8,128)S(1)}, f32[3,6,256,128]{3,2,1,0:T(8,128)}, u32[]{:S(2)}) copy-start(f32[3,6,256,128]{3,2,1,0:T(8,128)} %get-tuple-element.15) | copy-start | bytes 7077892

commit v5 on v4

--- a/solution.py
+++ b/solution.py
@@ -89,6 +89,119 @@
     )(block)
 
 
+def gather_with_halo(block, e_field, h_field, coefficient, depth, collective):
+    n = lax.axis_size("ty")
+    layers, cells_x, cells_y = coefficient.shape
+    rows = cells_x + 2 * depth
+    n_parts = 7 * layers
+
+    def kernel(x_ref, e_ref, h_ref, coef_ref, o_ref, rrow, rcol,
+               gsend, grecv, local, srow, scol, tmp, hsend, hrecv):
+        me = lax.axis_index("ty")
+        n_tx = lax.axis_size("tx")
+        me_x = lax.axis_index("tx")
+        x_lo = {"tx": lax.rem(me_x + n_tx - 1, n_tx)}
+        x_hi = {"tx": lax.rem(me_x + 1, n_tx)}
+        y_lo = {"ty": lax.rem(me + n - 1, n)}
+        y_hi = {"ty": lax.rem(me + 1, n)}
+        barrier = pltpu.get_barrier_semaphore()
+        for k in range(1, n):
+            pl.semaphore_signal(barrier, 1, device_id={"ty": lax.rem(me + k, n)}, device_id_type=MESH)
+        for peer in (x_lo, x_hi):
+            pl.semaphore_signal(barrier, 1, device_id=peer, device_id_type=MESH)
+        pl.semaphore_wait(barrier, n + 1)
+        own = pltpu.make_async_copy(x_ref, o_ref.at[me], local.at[0])
+        own.start()
+        gathers = []
+        for k in range(1, n):
+            copy = pltpu.make_async_remote_copy(
+                src_ref=x_ref, dst_ref=o_ref.at[me], send_sem=gsend.at[k - 1], recv_sem=grecv.at[k - 1],
+                device_id={"ty": lax.rem(me + k, n)}, device_id_type=MESH,
+            )
+            copy.start()
+            gathers.append(copy)
+
+        def part_of(h):
+            comp = h // layers
+            z = h % layers
+            field = jnp.where(comp < 3, e_ref[comp % 3, z], h_ref[comp % 3, z])
+            return jnp.where(comp < 6, field, coef_ref[z])
+
+        def fill_rows(h, carry):
+            part = part_of(h)
+            srow[0, h] = part[0:depth]
+            srow[1, h] = part[cells_x - depth:cells_x]
+            return carry
+
+        lax.fori_loop(0, n_parts, fill_rows, 0)
+        row_copies = [
+            pltpu.make_async_remote_copy(
+                src_ref=srow.at[0], dst_ref=rrow.at[0], send_sem=hsend.at[0], recv_sem=hrecv.at[0],
+                device_id=x_lo, device_id_type=MESH,
+            ),
+            pltpu.make_async_remote_copy(
+                src_ref=srow.at[1], dst_ref=rrow.at[1], send_sem=hsend.at[1], recv_sem=hrecv.at[1],
+                device_id=x_hi, device_id_type=MESH,
+            ),
+        ]
+        for copy in row_copies:
+            copy.start()
+        for copy in row_copies:
+            copy.wait()
+
+        def fill_cols(h, carry):
+            tmp[0:cells_x] = part_of(h)
+            tmp[cells_x:cells_x + depth] = rrow[0, h]
+            tmp[cells_x + depth:rows] = rrow[1, h]
+            t = tmp[...].T
+            scol[0, h] = t[0:depth]
+            scol[1, h] = t[cells_y - depth:cells_y]
+            return carry
+
+        lax.fori_loop(0, n_parts, fill_cols, 0)
+        col_copies = [
+            pltpu.make_async_remote_copy(
+                src_ref=scol.at[0], dst_ref=rcol.at[0], send_sem=hsend.at[2], recv_sem=hrecv.at[2],
+                device_id=y_lo, device_id_type=MESH,
+            ),
+            pltpu.make_async_remote_copy(
+                src_ref=scol.at[1], dst_ref=rcol.at[1], send_sem=hsend.at[3], recv_sem=hrecv.at[3],
+                device_id=y_hi, device_id_type=MESH,
+            ),
+        ]
+        for copy in col_copies:
+            copy.start()
+        for copy in col_copies:
+            copy.wait()
+        own.wait()
+        for copy in gathers:
+            copy.wait()
+
+    return pl.pallas_call(
+        kernel,
+        out_shape=(
+            jax.ShapeDtypeStruct((n,) + block.shape, block.dtype),
+            jax.ShapeDtypeStruct((2, n_parts, depth, cells_y), jnp.float32),
+            jax.ShapeDtypeStruct((2, n_parts, depth, rows), jnp.float32),
+        ),
+        in_specs=[VMEM_SPEC] * 4,
+        out_specs=(VMEM_SPEC, VMEM_SPEC, VMEM_SPEC),
+        scratch_shapes=[
+            pltpu.SemaphoreType.DMA((n - 1,)),
+            pltpu.SemaphoreType.DMA((n - 1,)),
+            pltpu.SemaphoreType.DMA((1,)),
+            pltpu.VMEM((2, n_parts, depth, cells_y), jnp.float32),
+            pltpu.VMEM((2, n_parts, depth, rows), jnp.float32),
+            pltpu.VMEM((rows, cells_y), jnp.float32),
+            pltpu.SemaphoreType.DMA((4,)),
+            pltpu.SemaphoreType.DMA((4,)),
+        ],
+        compiler_params=pltpu.CompilerParams(
+            collective_id=collective, has_side_effects=True, vmem_limit_bytes=64 * 1024 * 1024
+        ),
+    )(block, e_field, h_field, coefficient)
+
+
 def summed_over_pair(block, axis, collective):
     def kernel(x_ref, o_ref, got, send, recv):
         other = {axis: 1 - lax.axis_index(axis)}
@@ -131,7 +244,8 @@
     return jnp.pad(flat, (0, pad)).reshape(-1, 128)
 
 
-def injection_plane(orders, offsets, cells_x, cells_y):
+def injection_plane(orders, offsets, e_field, h_field, coefficient):
+    layers, cells_x, cells_y = coefficient.shape
     points, _, rows_kx, cols_ky = orders.shape
     n_src = lax.axis_size("src")
     n_tx = lax.axis_size("tx")
@@ -155,7 +269,7 @@
     merged = jnp.einsum("pruj,pvj->ruv", placed, lift_y, precision=exact)
     size = merged.size
     merged = summed_over_pair(lane_dense(merged), "src", 2)
-    got = gather_along(merged, ("ty",), 0)
+    got, frow, fcol = gather_with_halo(merged, e_field, h_field, coefficient, HALO, 0)
     got = got.reshape(n_ty, -1)[:, :size].reshape(n_ty, 2, span_x, span_y)
     g_re = got[:, 0]
     g_im = got[:, 1]
@@ -178,10 +292,10 @@
     p_im = jnp.einsum("cux,cuy->xy", bx_c, i_im, precision=PREC) + jnp.einsum(
         "cux,cuy->xy", bx_s, i_re, precision=PREC
     )
-    return jnp.stack([p_re, p_im])
-
-
-def yee_kernel(e_ref, h_ref, coef_ref, plane_ref, eo_ref, ho_ref,
+    return jnp.stack([p_re, p_im]), frow, fcol
+
+
+def yee_kernel(e_ref, h_ref, coef_ref, plane_ref, frow, fcol, eo_ref, ho_ref,
                ext, cp, tmp, srow, rrow, scol, rcol, send, recv):
     layers, cells_x, cells_y = coef_ref.shape
     depth = srow.shape[2]
@@ -189,7 +303,6 @@
     lanes = ext.shape[2]
     slab = layers + 2
     n_field = 6 * layers
-    n_parts = n_field + layers + 2
     n_tx = lax.axis_size("tx")
     n_ty = lax.axis_size("ty")
     me_x = lax.axis_index("tx")
@@ -204,27 +317,9 @@
         pl.semaphore_signal(barrier, 1, device_id=peer, device_id_type=MESH)
     pl.semaphore_wait(barrier, 4)
 
-    def own_part(h):
-        comp = h // layers
-        z = h % layers
-        return jnp.where(comp < 3, e_ref[comp % 3, z], h_ref[comp % 3, z])
-
-    def field_slot(h):
-        return (h // layers) * slab + h % layers + 1
-
-    def fill_rows(h, carry):
-        part = own_part(h)
-        srow[0, h] = part[0:depth]
-        srow[1, h] = part[cells_x - depth:cells_x]
-        ext[field_slot(h), 0:cells_x, 0:cells_y] = part
-        return carry
-
-    lax.fori_loop(0, n_field, fill_rows, 0)
-    for k in range(layers + 2):
-        part = coef_ref[k] if k < layers else plane_ref[k - layers]
-        srow[0, n_field + k] = part[0:depth]
-        srow[1, n_field + k] = part[cells_x - depth:cells_x]
-        cp[k, 0:cells_x, 0:cells_y] = part
+    for k in range(2):
+        srow[0, k] = plane_ref[k, 0:depth]
+        srow[1, k] = plane_ref[k, cells_x - depth:cells_x]
     row_copies = [
         pltpu.make_async_remote_copy(
             src_ref=srow.at[0], dst_ref=rrow.at[0], send_sem=send.at[0], recv_sem=recv.at[0],
@@ -237,28 +332,49 @@
     ]
     for copy in row_copies:
         copy.start()
+
+    tmp[...] = jnp.zeros_like(tmp)
+    lane = lax.broadcasted_iota(jnp.int32, (rows, cells_y), 1)
+
+    def place_cols(dst, idx, col_a, col_b):
+        v = jnp.concatenate([col_a, col_b], 0)
+        tmp[:, 0:2 * depth] = v.T
+        w = tmp[...]
+        front = jnp.where(lane < depth, w, 0.0)
+        back = jnp.where(lane >= depth, w, 0.0)
+        dst[idx, :, cells_y:lanes] = front + pltpu.roll(back, cells_y - 2 * depth, 1)
+
+    def place_part(dst, idx, own, h):
+        dst[idx, 0:cells_x, 0:cells_y] = own
+        dst[idx, cells_x:cells_x + depth, 0:cells_y] = frow[0, h]
+        dst[idx, cells_x + depth:rows, 0:cells_y] = frow[1, h]
+        place_cols(dst, idx, fcol[0, h], fcol[1, h])
+
+    def place_fields(h, carry):
+        comp = h // layers
+        z = h % layers
+        own = jnp.where(comp < 3, e_ref[comp % 3, z], h_ref[comp % 3, z])
+        place_part(ext, comp * slab + z + 1, own, h)
+        return carry
+
+    lax.fori_loop(0, n_field, place_fields, 0)
+    for z in range(layers):
+        place_part(cp, z, coef_ref[z], n_field + z)
     zero = jnp.zeros((rows, lanes), jnp.float32)
     for comp in range(3):
         ext[comp * slab + slab - 1] = zero
         ext[(3 + comp) * slab] = zero
-    tmp[...] = jnp.zeros_like(tmp)
     for copy in row_copies:
         copy.wait()
 
-    def fill_cols(dst, idx, h):
-        dst[idx, cells_x:cells_x + depth, 0:cells_y] = rrow[0, h]
-        dst[idx, cells_x + depth:rows, 0:cells_y] = rrow[1, h]
-        t = dst[idx, :, 0:cells_y].T
-        scol[0, h] = t[0:depth]
-        scol[1, h] = t[cells_y - depth:cells_y]
-
-    def cols_fields(h, carry):
-        fill_cols(ext, field_slot(h), h)
-        return carry
-
-    lax.fori_loop(0, n_field, cols_fields, 0)
-    for k in range(layers + 2):
-        fill_cols(cp, k, n_field + k)
+    for k in range(2):
+        idx = layers + k
+        cp[idx, 0:cells_x, 0:cells_y] = plane_ref[k]
+        cp[idx, cells_x:cells_x + depth, 0:cells_y] = rrow[0, k]
+        cp[idx, cells_x + depth:rows, 0:cells_y] = rrow[1, k]
+        t = cp[idx, :, 0:cells_y].T
+        scol[0, k] = t[0:depth]
+        scol[1, k] = t[cells_y - depth:cells_y]
     col_copies = [
         pltpu.make_async_remote_copy(
             src_ref=scol.at[0], dst_ref=rcol.at[0], send_sem=send.at[2], recv_sem=recv.at[2],
@@ -273,23 +389,8 @@
         copy.start()
     for copy in col_copies:
         copy.wait()
-    lane = lax.broadcasted_iota(jnp.int32, (rows, cells_y), 1)
-
-    def place_cols(dst, idx, h):
-        v = jnp.concatenate([rcol[0, h], rcol[1, h]], 0)
-        tmp[:, 0:2 * depth] = v.T
-        w = tmp[...]
-        front = jnp.where(lane < depth, w, 0.0)
-        back = jnp.where(lane >= depth, w, 0.0)
-        dst[idx, :, cells_y:lanes] = front + pltpu.roll(back, cells_y - 2 * depth, 1)
-
-    def place_fields(h, carry):
-        place_cols(ext, field_slot(h), h)
-        return carry
-
-    lax.fori_loop(0, n_field, place_fields, 0)
-    for k in range(layers + 2):
-        place_cols(cp, k, n_field + k)
+    for k in range(2):
+        place_cols(cp, layers + k, rcol[0, k], rcol[1, k])
 
     ahead_x = lambda f: pltpu.roll(f, rows - 1, 0)
     ahead_y = lambda f: pltpu.roll(f, lanes - 1, 1)
@@ -337,33 +438,32 @@
 
 def per_device(orders, offsets, material, e_field, h_field):
     layers, cells_x, cells_y = material.shape
-    plane = injection_plane(orders, offsets, cells_x, cells_y)
     coefficient = cell_coefficient(material)
+    plane, frow, fcol = injection_plane(orders, offsets, e_field, h_field, coefficient)
     depth = HALO
     rows = cells_x + 2 * depth
     lanes = 2 * cells_y
-    n_parts = 6 * layers + layers + 2
     out = jax.ShapeDtypeStruct(e_field.shape, jnp.float32)
     return pl.pallas_call(
         yee_kernel,
         out_shape=(out, out),
-        in_specs=[VMEM_SPEC] * 4,
+        in_specs=[VMEM_SPEC] * 6,
         out_specs=(VMEM_SPEC, VMEM_SPEC),
         scratch_shapes=[
             pltpu.VMEM((6 * (layers + 2), rows, lanes), jnp.float32),
             pltpu.VMEM((layers + 2, rows, lanes), jnp.float32),
             pltpu.VMEM((rows, cells_y), jnp.float32),
-            pltpu.VMEM((2, n_parts, depth, cells_y), jnp.float32),
-            pltpu.VMEM((2, n_parts, depth, cells_y), jnp.float32),
-            pltpu.VMEM((2, n_parts, depth, rows), jnp.float32),
-            pltpu.VMEM((2, n_parts, depth, rows), jnp.float32),
+            pltpu.VMEM((2, 2, depth, cells_y), jnp.float32),
+            pltpu.VMEM((2, 2, depth, cells_y), jnp.float32),
+            pltpu.VMEM((2, 2, depth, rows), jnp.float32),
+            pltpu.VMEM((2, 2, depth, rows), jnp.float32),
             pltpu.SemaphoreType.DMA((4,)),
             pltpu.SemaphoreType.DMA((4,)),
         ],
         compiler_params=pltpu.CompilerParams(
             collective_id=3, has_side_effects=True, vmem_limit_bytes=64 * 1024 * 1024
         ),
-    )(e_field, h_field, coefficient, plane)
+    )(e_field, h_field, coefficient, plane, frow, fcol)
 
 
 def solution(mesh):

time: 118 us -> 114 us (0.966)
  Pallas kernels: 97.3 us -> 90.5 us
  other arithmetic: 3.38 us -> 5.86 us
    pallas_call x2 -> x1, Pallas kernels: 39.6 us -> 12.9 us  [gather_along(): pl.pallas_call(kernel, out_shape=jax.ShapeDtypeStruct((n,) + block.shape,...]
    pallas_call x1 -> x2, Pallas kernels: 53 us -> 72.8 us  [the longest x1 37.9 us: gather_with_halo(): pl.pallas_call(kernel, out_shape=(jax.ShapeDtypeStruct((n,) + block.shape...]
    cos x4, other arithmetic: 0.83 us -> 3.33 us  [phase_tables(): return (jnp.cos(angle), jnp.sin(angle))]
    unnamed x9 -> x25, local copies, waits for them, and re-layouts: 6.19 us -> 6.34 us
where the time goes in v5:
time: 114 us
  Pallas kernels  90.5 us (79%)
  local copies, waits for them, and re-layouts  8.4 us (7%)
  matrix products  8.23 us (7%)
  other arithmetic  5.86 us (5%)
    pallas_call x1, Pallas kernels, gather_with_halo(): pl.pallas_call(kernel, out_shape=(jax.ShapeDtypeStruct((n,) + block.shape...  37.9 us
    pallas_call x1, Pallas kernels, per_device(): pl.pallas_call(yee_kernel, out_shape=(out, out), in_specs=[VMEM_SPEC] * 6...  34.9 us
    pallas_call x1, Pallas kernels, gather_along(): pl.pallas_call(kernel, out_shape=jax.ShapeDtypeStruct((n,) + block.shape,...  12.9 us
    unnamed x25, local copies, waits for them, and re-layouts  6.34 us
    pallas_call x1, Pallas kernels, summed_over_pair(): pl.pallas_call(kernel, out_shape=jax.ShapeDtypeStruct(block.shape, block....  4.8 us
    cos x4, other arithmetic, phase_tables(): return (jnp.cos(angle), jnp.sin(angle))  3.33 us

profile of v5, /device:TPU:1, one launch (start us, length us, event | category | flops | bytes accessed | tf_op | source)
XLA Modules:
  0.0 113.9 jit_solution(8028423729081548615)
XLA Ops:
  0.6 0.0 copy-start.1
  0.7 0.8 slice_bitcast_fusion.6
  1.5 0.7 fusion.74
  2.2 0.7 fusion.76
  2.9 0.8 fusion.66
  3.7 1.2 %convolution_bitcast_fusion.4 = f32[4,2,80,32]{2,3,0,1:T(8,128)S(1)} fusion(f32[4,2,64,32]{2,3,1,0:T(8,128)} %param.5, s32[4]{0:T(128)S(1)} %get-tuple-element.17), kind=kOutput, calls=%fused_computation.4 | convolution fusion | flops 15790080 | bytes 147472 | tf_op jit(solution)/shard_map/puk,prkj->pruj/dot_general | solution.py:268
  5.0 0.3 convolution_bitcast_fusion.5
  5.3 0.1 reshape.298
  5.4 0.6 pad_bitcast_fusion.x_ref
  6.0 4.8 %shard_map.68.x_ref = f32[64,128]{1,0:T(8,128)} custom-call(f32[64,128]{1,0:T(8,128)} %pad_bitcast_fusion.x_ref), custom_call_target="tpu_custom_call" | custom-call | tf_op jit(solution)/shard_map/pallas_call | solution.py:219
  10.8 1.1 fusion.59
  11.9 0.0 copy-done.1
  11.9 1.2 %select_add_fusion.coef_ref = f32[6,256,128]{2,1,0:T(8,128)} fusion(s32[6,256,128]{2,1,0:T(8,128)S(1)} %copy-done.1), kind=kLoop, calls=%fused_computation.18 | loop fusion | flops 2162688 | bytes 1572864 | tf_op jit(solution)/shard_map/add | solution.py:31
  13.0 37.9 %shard_map.69 = (f32[16,64,128]{2,1,0:T(8,128)}, f32[2,42,8,128]{3,2,1,0:T(8,128)}, f32[2,42,8,272]{3,2,1,0:T(8,128)}) custom-call(f32[64,128]{1,0:T(8,128)} %shard_map.68.x_ref, f32[3,6,256,128]{3,2,1,0:T(8,128)} %e_ref.3, f32[3,6,256,128]{3,2,1,0:T(8,128)} %h_ref.3, f32[6,256,128]{2,1,0:T(8,128)} %select_add_fusion.coef_ref), custom_call_target="tpu_custom_call" | custom-call | tf_op jit(solution)/shard_map/pallas_call | solution.py:180
  50.9 1.4 %copy.19 = f32[2,8,64,128]{3,1,2,0:T(8,128)S(1)} copy(f32[2,8,64,128]{3,2,1,0:T(8,128)} %bitcast.84) | data formatting | bytes 1048576
  52.3 0.0 copy-start.3
  52.3 0.0 copy-start.4
  52.3 0.0 copy-start.5
  52.3 0.0 copy-start.6
  52.4 0.5 reshape.301
  52.9 0.1 copy-done.3
  53.0 0.0 copy-done.4
  53.1 0.0 copy-done.5
  53.1 0.0 copy-done.6
  53.1 0.4 convolution_bitcast_fusion.6
  53.5 0.4 fusion.7
  54.0 0.0 copy-start.7
  54.0 0.0 copy-start.8
  54.0 0.0 copy-start.9
  54.0 0.0 copy-start.10
  54.0 0.4 convolution_bitcast_fusion.8
  54.5 0.4 fusion.5
  54.9 0.6 pad_maximum_fusion.1.x_ref
  55.5 12.9 %shard_map.70 = f32[8,2,80,128]{3,2,1,0:T(8,128)} custom-call(f32[2,80,128]{2,1,0:T(8,128)} %pad_maximum_fusion.1.x_ref), custom_call_target="tpu_custom_call" | custom-call | tf_op jit(solution)/shard_map/pallas_call | solution.py:78
  68.5 0.0 copy-done.7
  68.5 0.0 copy-done.8
  68.5 0.0 copy-done.9
  68.5 0.0 copy-done.10
  68.5 0.0 copy-start.2
  68.5 1.8 %convolution_bitcast_fusion = f32[256,128]{1,0:T(8,128)S(1)} fusion(f32[80,256]{1,0:T(8,128)S(1)} %copy-done.8, f32[8,256]{1,0:T(8,128)S(1)} %copy-done.10, f32[80,256]{1,0:T(8,128)S(1)} %copy-done.7, f32[8,256]{1,0:T(8,128)S(1)} %copy-done.9, f32[8,2,80,128]{3,2,1,0:T(8,128)} %shard_map.70), kind=kOutput, calls=%fused_computation | convolution fusion | flops 126320640 | bytes 638976 | tf_op jit(solution)/shard_map/cux,cuy->xy/dot_general | solution.py:292
  70.3 1.7 %fusion.3 = f32[1,256,128]{2,1,0:T(8,128)S(1)} fusion(f32[256,128]{1,0:T(8,128)S(1)} %convolution_bitcast_fusion, f32[80,256]{1,0:T(8,128)S(1)} %copy-done.8, f32[8,256]{1,0:T(8,128)S(1)} %copy-done.10, f32[80,256]{1,0:T(8,128)S(1)} %copy-done.7, f32[8,256]{1,0:T(8,128)S(1)} %copy-done.9, f32[8,2,80,128]{3,2,1,0:T(8,128)} %shard_map.70), kind=kOutput, calls=%fused_computation.8 | convolution fusion | flops 126353408 | bytes 770048 | tf_op jit(solution)/shard_map/cux,cuy->xy/dot_general | solution.py:292
  72.0 0.0 copy-done.2
  72.0 0.7 convolution_bitcast_fusion.2
  72.7 0.7 fusion.1
  73.5 0.7 pad_maximum_fusion.plane_ref
  74.2 34.9 %shard_map.71 = (f32[3,6,256,128]{3,2,1,0:T(8,128)}, f32[3,6,256,128]{3,2,1,0:T(8,128)}) custom-call(f32[3,6,256,128]{3,2,1,0:T(8,128)} %e_ref.3, f32[3,6,256,128]{3,2,1,0:T(8,128)} %h_ref.3, f32[6,256,128]{2,1,0:T(8,128)} %select_add_fusion.coef_ref, f32[2,256,128]{2,1,0:T(8,128)} %pad_maximum_fusion.plane_ref, f32[2,42,8,128]{3,2,1,0:T(8,128)} %get-tuple-element.6.frow, ...), custom_call_target="tpu_custom_call" | custom-call | tf_op jit(solution)/shard_map/pallas_call | solution.py:447
  109.1 0.0 copy-start
  109.1 3.4 %copy.22 = f32[3,6,256,128]{3,2,1,0:T(8,128)} copy(f32[3,6,256,128]{3,2,1,0:T(8,128)} %get-tuple-element.20) | data formatting | bytes 4718592
  112.5 0.0 copy-done
  112.5 1.4 %copy.23 = f32[3,6,256,128]{3,2,1,0:T(8,128)} copy(f32[3,6,256,128]{3,2,1,0:T(8,128)S(1)} %copy-done) | data formatting | bytes 4718592
  (7 shorter events, 0.1 us)
Async XLA Ops:
  0.6 11.2 %copy-start.1 = (s32[6,256,128]{2,1,0:T(8,128)S(1)}, s32[6,256,128]{2,1,0:T(8,128)}, u32[]{:S(2)}) copy-start(s32[6,256,128]{2,1,0:T(8,128)} %param.7) | copy-start | bytes 2359300
  52.3 0.7 copy-start.3
  52.3 0.7 copy-start.4
  52.3 0.7 copy-start.5
  52.3 0.7 copy-start.6
  54.0 14.5 %copy-start.7 = (f32[80,256]{1,0:T(8,128)S(1)}, f32[80,256]{1,0:T(8,128)}, u32[]{:S(2)}) copy-start(f32[80,256]{1,0:T(8,128)} %get-tuple-element.10) | copy-start | bytes 245764
  54.0 14.5 %copy-start.8 = (f32[80,256]{1,0:T(8,128)S(1)}, f32[80,256]{1,0:T(8,128)}, u32[]{:S(2)}) copy-start(f32[80,256]{1,0:T(8,128)} %get-tuple-element.11) | copy-start | bytes 245764
  54.0 14.5 %copy-start.9 = (f32[8,256]{1,0:T(8,128)S(1)}, f32[8,256]{1,0:T(8,128)}, u32[]{:S(2)}) copy-start(f32[8,256]{1,0:T(8,128)} %get-tuple-element.8) | copy-start | bytes 24580
  54.0 14.5 %copy-start.10 = (f32[8,256]{1,0:T(8,128)S(1)}, f32[8,256]{1,0:T(8,128)}, u32[]{:S(2)}) copy-start(f32[8,256]{1,0:T(8,128)} %get-tuple-element.9) | copy-start | bytes 24580
  68.5 3.5 %copy-start.2 = (f32[8,2,80,128]{3,2,1,0:T(8,128)S(1)}, f32[8,2,80,128]{3,2,1,0:T(8,128)}, u32[]{:S(2)}) copy-start(f32[8,2,80,128]{3,2,1,0:T(8,128)} %shard_map.70) | copy-start | bytes 1966084
  109.1 3.4 %copy-start = (f32[3,6,256,128]{3,2,1,0:T(8,128)S(1)}, f32[3,6,256,128]{3,2,1,0:T(8,128)}, u32[]{:S(2)}) copy-start(f32[3,6,256,128]{3,2,1,0:T(8,128)} %get-tuple-element.21) | copy-start | bytes 7077892

commit v6 on v5

--- a/solution.py
+++ b/solution.py
@@ -236,6 +236,11 @@
     cos_t = c1[:, None, :] * c2[None, :, :] - s1[:, None, :] * s2[None, :, :]
     sin_t = s1[:, None, :] * c2[None, :, :] + c1[:, None, :] * s2[None, :, :]
     return cos_t, sin_t
+
+
+def ring_positions(cells, depth):
+    own = jnp.arange(cells + depth, dtype=jnp.int32)
+    return jnp.concatenate([own, jnp.arange(-depth, 0, dtype=jnp.int32)])
 
 
 def lane_dense(block):
@@ -273,7 +278,7 @@
     got = got.reshape(n_ty, -1)[:, :size].reshape(n_ty, 2, span_x, span_y)
     g_re = got[:, 0]
     g_im = got[:, 1]
-    y_pos = lax.axis_index("ty") * cells_y + jnp.arange(cells_y, dtype=jnp.int32)
+    y_pos = lax.axis_index("ty") * cells_y + ring_positions(cells_y, HALO)
     by_c, by_s = chunk_tables(cols_ky, span_y, n_ty, my // 2 + SHIFT, y_pos, full_y)
     i_re = jnp.einsum("cuv,cvy->uy", g_re, by_c, precision=PREC) - jnp.einsum(
         "cuv,cvy->uy", g_im, by_s, precision=PREC
@@ -281,10 +286,13 @@
     i_im = jnp.einsum("cuv,cvy->uy", g_re, by_s, precision=PREC) + jnp.einsum(
         "cuv,cvy->uy", g_im, by_c, precision=PREC
     )
-    inner = gather_along(jnp.stack([i_re, i_im]), ("tx",), 1)
+    inner = jnp.stack([i_re, i_im])
+    size = inner.size
+    inner = gather_along(lane_dense(inner), ("tx",), 1)
+    inner = inner.reshape(n_tx, -1)[:, :size].reshape((n_tx,) + (2, span_x, cells_y + 2 * HALO))
     i_re = inner[:, 0]
     i_im = inner[:, 1]
-    x_pos = lax.axis_index("tx") * cells_x + jnp.arange(cells_x, dtype=jnp.int32)
+    x_pos = lax.axis_index("tx") * cells_x + ring_positions(cells_x, HALO)
     bx_c, bx_s = chunk_tables(rows_kx, span_x, n_tx, mx // 2 + SHIFT, x_pos, full_x)
     p_re = jnp.einsum("cux,cuy->xy", bx_c, i_re, precision=PREC) - jnp.einsum(
         "cux,cuy->xy", bx_s, i_im, precision=PREC
@@ -295,44 +303,13 @@
     return jnp.stack([p_re, p_im]), frow, fcol
 
 
-def yee_kernel(e_ref, h_ref, coef_ref, plane_ref, frow, fcol, eo_ref, ho_ref,
-               ext, cp, tmp, srow, rrow, scol, rcol, send, recv):
+def yee_kernel(e_ref, h_ref, coef_ref, plane_ref, frow, fcol, eo_ref, ho_ref, ext, cp, tmp):
     layers, cells_x, cells_y = coef_ref.shape
-    depth = srow.shape[2]
+    depth = frow.shape[2]
     rows = cells_x + 2 * depth
     lanes = ext.shape[2]
     slab = layers + 2
     n_field = 6 * layers
-    n_tx = lax.axis_size("tx")
-    n_ty = lax.axis_size("ty")
-    me_x = lax.axis_index("tx")
-    me_y = lax.axis_index("ty")
-    x_lo = {"tx": lax.rem(me_x + n_tx - 1, n_tx)}
-    x_hi = {"tx": lax.rem(me_x + 1, n_tx)}
-    y_lo = {"ty": lax.rem(me_y + n_ty - 1, n_ty)}
-    y_hi = {"ty": lax.rem(me_y + 1, n_ty)}
-
-    barrier = pltpu.get_barrier_semaphore()
-    for peer in (x_lo, x_hi, y_lo, y_hi):
-        pl.semaphore_signal(barrier, 1, device_id=peer, device_id_type=MESH)
-    pl.semaphore_wait(barrier, 4)
-
-    for k in range(2):
-        srow[0, k] = plane_ref[k, 0:depth]
-        srow[1, k] = plane_ref[k, cells_x - depth:cells_x]
-    row_copies = [
-        pltpu.make_async_remote_copy(
-            src_ref=srow.at[0], dst_ref=rrow.at[0], send_sem=send.at[0], recv_sem=recv.at[0],
-            device_id=x_lo, device_id_type=MESH,
-        ),
-        pltpu.make_async_remote_copy(
-            src_ref=srow.at[1], dst_ref=rrow.at[1], send_sem=send.at[1], recv_sem=recv.at[1],
-            device_id=x_hi, device_id_type=MESH,
-        ),
-    ]
-    for copy in row_copies:
-        copy.start()
-
     tmp[...] = jnp.zeros_like(tmp)
     lane = lax.broadcasted_iota(jnp.int32, (rows, cells_y), 1)
 
@@ -364,33 +341,14 @@
     for comp in range(3):
         ext[comp * slab + slab - 1] = zero
         ext[(3 + comp) * slab] = zero
-    for copy in row_copies:
-        copy.wait()
-
     for k in range(2):
         idx = layers + k
-        cp[idx, 0:cells_x, 0:cells_y] = plane_ref[k]
-        cp[idx, cells_x:cells_x + depth, 0:cells_y] = rrow[0, k]
-        cp[idx, cells_x + depth:rows, 0:cells_y] = rrow[1, k]
-        t = cp[idx, :, 0:cells_y].T
-        scol[0, k] = t[0:depth]
-        scol[1, k] = t[cells_y - depth:cells_y]
-    col_copies = [
-        pltpu.make_async_remote_copy(
-            src_ref=scol.at[0], dst_ref=rcol.at[0], send_sem=send.at[2], recv_sem=recv.at[2],
-            device_id=y_lo, device_id_type=MESH,
-        ),
-        pltpu.make_async_remote_copy(
-            src_ref=scol.at[1], dst_ref=rcol.at[1], send_sem=send.at[3], recv_sem=recv.at[3],
-            device_id=y_hi, device_id_type=MESH,
-        ),
-    ]
-    for copy in col_copies:
-        copy.start()
-    for copy in col_copies:
-        copy.wait()
-    for k in range(2):
-        place_cols(cp, layers + k, rcol[0, k], rcol[1, k])
+        cp[idx, :, 0:cells_y] = plane_ref[k, :, 0:cells_y]
+        tmp[:, 0:2 * depth] = plane_ref[k, :, cells_y:cells_y + 2 * depth]
+        w = tmp[...]
+        front = jnp.where(lane < depth, w, 0.0)
+        back = jnp.where(lane >= depth, w, 0.0)
+        cp[idx, :, cells_y:lanes] = front + pltpu.roll(back, cells_y - 2 * depth, 1)
 
     ahead_x = lambda f: pltpu.roll(f, rows - 1, 0)
     ahead_y = lambda f: pltpu.roll(f, lanes - 1, 1)
@@ -453,16 +411,8 @@
             pltpu.VMEM((6 * (layers + 2), rows, lanes), jnp.float32),
             pltpu.VMEM((layers + 2, rows, lanes), jnp.float32),
             pltpu.VMEM((rows, cells_y), jnp.float32),
-            pltpu.VMEM((2, 2, depth, cells_y), jnp.float32),
-            pltpu.VMEM((2, 2, depth, cells_y), jnp.float32),
-            pltpu.VMEM((2, 2, depth, rows), jnp.float32),
-            pltpu.VMEM((2, 2, depth, rows), jnp.float32),
-            pltpu.SemaphoreType.DMA((4,)),
-            pltpu.SemaphoreType.DMA((4,)),
         ],
-        compiler_params=pltpu.CompilerParams(
-            collective_id=3, has_side_effects=True, vmem_limit_bytes=64 * 1024 * 1024
-        ),
+        compiler_params=pltpu.CompilerParams(vmem_limit_bytes=64 * 1024 * 1024),
     )(e_field, h_field, coefficient, plane, frow, fcol)
 
 

time: 114 us -> 109 us (0.956); the launches traced: 114 us -> 107 us
  Pallas kernels: 90.5 us -> 83.8 us
  matrix products: 8.23 us -> 9.72 us
  local copies, waits for them, and re-layouts: 8.4 us -> 7.08 us
    pallas_call x1, Pallas kernels: 34.9 us -> 27.3 us  [per_device(): pl.pallas_call(yee_kernel, out_shape=(out, out), in_specs=[VMEM_SPEC] * 6...]
    unnamed x25 -> x20, local copies, waits for them, and re-layouts: 6.34 us -> 2.85 us
where the time goes in v6:
time: 109 us; the launch traced here: 107 us
  Pallas kernels  83.8 us (77%)
  matrix products  9.72 us (9%)
  local copies, waits for them, and re-layouts  7.08 us (6%)
  other arithmetic  5.93 us (5%)
    pallas_call x1, Pallas kernels, gather_with_halo(): pl.pallas_call(kernel, out_shape=(jax.ShapeDtypeStruct((n,) + block.shape...  37.9 us
    pallas_call x1, Pallas kernels, per_device(): pl.pallas_call(yee_kernel, out_shape=(out, out), in_specs=[VMEM_SPEC] * 6...  27.3 us
    pallas_call x1, Pallas kernels, gather_along(): pl.pallas_call(kernel, out_shape=jax.ShapeDtypeStruct((n,) + block.shape,...  13.8 us
    pallas_call x1, Pallas kernels, summed_over_pair(): pl.pallas_call(kernel, out_shape=jax.ShapeDtypeStruct(block.shape, block....  4.81 us
    cos x4, other arithmetic, phase_tables(): return (jnp.cos(angle), jnp.sin(angle))  3.66 us
    unnamed x20, local copies, waits for them, and re-layouts  2.85 us

profile of v6, /device:TPU:1, one launch (start us, length us, event | category | flops | bytes accessed | tf_op | source)
XLA Modules:
  0.0 107.5 jit_solution(12979846211784539893)
XLA Ops:
  0.6 0.0 copy-start.2
  0.7 0.1 add_add_fusion.1
  0.8 0.8 slice_bitcast_fusion.12
  1.6 0.1 add_add_fusion
  1.6 0.7 fusion.66
  2.4 0.8 fusion.64
  3.2 0.9 fusion.56
  4.1 1.2 %convolution_bitcast_fusion.4 = f32[4,2,80,32]{2,3,0,1:T(8,128)S(1)} fusion(f32[4,2,64,32]{2,3,1,0:T(8,128)} %param.5, s32[4]{0:T(128)S(1)} %get-tuple-element.17), kind=kOutput, calls=%fused_computation.6 | convolution fusion | flops 15790080 | bytes 147472 | tf_op jit(solution)/shard_map/puk,prkj->pruj/dot_general | solution.py:273
  5.2 0.3 convolution_bitcast_fusion.5
  5.5 0.1 reshape.323
  5.6 0.6 pad_bitcast_fusion.1.x_ref
  6.3 4.8 %shard_map.68.x_ref = f32[64,128]{1,0:T(8,128)} custom-call(f32[64,128]{1,0:T(8,128)} %pad_bitcast_fusion.1.x_ref), custom_call_target="tpu_custom_call" | custom-call | tf_op jit(solution)/shard_map/pallas_call | solution.py:219
  11.1 1.3 %fusion.49 = (f32[80,272]{1,0:T(8,128)}, f32[80,272]{1,0:T(8,128)}) fusion(s32[272]{0:T(512)S(1)} %add_add_fusion, s32[80]{0:T(128)S(1)} %iota_add_fusion.1), kind=kLoop, calls=%fused_computation.83 | loop fusion | flops 304640 | bytes 175488 | tf_op jit(solution)/shard_map/cos | solution.py:25
  12.3 0.0 copy-done.2
  12.3 1.2 %select_add_fusion.coef_ref = f32[6,256,128]{2,1,0:T(8,128)} fusion(s32[6,256,128]{2,1,0:T(8,128)S(1)} %copy-done.2), kind=kLoop, calls=%fused_computation.20 | loop fusion | flops 2162688 | bytes 1572864 | tf_op jit(solution)/shard_map/add | solution.py:31
  13.6 37.9 %shard_map.69 = (f32[16,64,128]{2,1,0:T(8,128)}, f32[2,42,8,128]{3,2,1,0:T(8,128)}, f32[2,42,8,272]{3,2,1,0:T(8,128)}) custom-call(f32[64,128]{1,0:T(8,128)} %shard_map.68.x_ref, f32[3,6,256,128]{3,2,1,0:T(8,128)} %e_ref.3, f32[3,6,256,128]{3,2,1,0:T(8,128)} %h_ref.3, f32[6,256,128]{2,1,0:T(8,128)} %select_add_fusion.coef_ref), custom_call_target="tpu_custom_call" | custom-call | tf_op jit(solution)/shard_map/pallas_call | solution.py:180
  51.4 1.4 %copy.43 = f32[2,8,64,128]{3,1,2,0:T(8,128)S(1)} copy(f32[2,8,64,128]{3,2,1,0:T(8,128)} %bitcast.90) | data formatting | bytes 1048576
  52.8 0.0 copy-start.5
  52.8 0.0 copy-start.6
  52.8 0.0 copy-start.7
  52.8 0.0 copy-start.8
  52.9 0.5 reshape.326
  53.4 0.2 copy-done.5
  53.6 0.0 copy-done.6
  53.6 0.0 copy-done.7
  53.6 0.0 copy-done.8
  53.6 1.3 %convolution_bitcast_fusion.6 = f32[80,144]{0,1:T(8,128)S(1)} fusion(f32[16,2,80,48]{3,2,1,0:T(8,128)S(1)} %reshape.326, f32[48,144]{1,0:T(8,128)S(1)} %copy-done.6, f32[16,144]{1,0:T(8,128)S(1)} %copy-done.8, f32[48,144]{1,0:T(8,128)S(1)} %copy-done.5, f32[16,144]{1,0:T(8,128)S(1)} %copy-done.7), kind=kOutput, calls=%fused_computation.8 | convolution fusion | flops 53415936 | bytes 832512 | tf_op jit(solution)/shard_map/cuv,cvy->uy/dot_general | solution.py:286
  54.9 1.3 %fusion.5 = f32[1,80,144]{1,2,0:T(8,128)S(1)} fusion(f32[80,144]{0,1:T(8,128)S(1)} %convolution_bitcast_fusion.6, f32[16,2,80,48]{3,2,1,0:T(8,128)S(1)} %reshape.326, f32[48,144]{1,0:T(8,128)S(1)} %copy-done.6, f32[16,144]{1,0:T(8,128)S(1)} %copy-done.8, f32[48,144]{1,0:T(8,128)S(1)} %copy-done.5, f32[16,144]{1,0:T(8,128)S(1)} %copy-done.7), kind=kOutput, calls=%fused_computation.15 | convolution fusion | flops 53427456 | bytes 906240 | tf_op jit(solution)/shard_map/cuv,cvy->uy/dot_general | solution.py:286
  56.2 1.3 %convolution_bitcast_fusion.8 = f32[80,144]{0,1:T(8,128)S(1)} fusion(f32[16,2,80,48]{3,2,1,0:T(8,128)S(1)} %reshape.326, f32[48,144]{1,0:T(8,128)S(1)} %copy-done.6, f32[16,144]{1,0:T(8,128)S(1)} %copy-done.8, f32[48,144]{1,0:T(8,128)S(1)} %copy-done.5, f32[16,144]{1,0:T(8,128)S(1)} %copy-done.7), kind=kOutput, calls=%fused_computation.10 | convolution fusion | flops 53415936 | bytes 832512 | tf_op jit(solution)/shard_map/cuv,cvy->uy/dot_general | solution.py:283
  57.5 1.3 %fusion.3 = f32[1,80,144]{1,2,0:T(8,128)S(1)} fusion(f32[80,144]{0,1:T(8,128)S(1)} %convolution_bitcast_fusion.8, f32[16,2,80,48]{3,2,1,0:T(8,128)S(1)} %reshape.326, f32[48,144]{1,0:T(8,128)S(1)} %copy-done.6, f32[16,144]{1,0:T(8,128)S(1)} %copy-done.8, f32[48,144]{1,0:T(8,128)S(1)} %copy-done.5, f32[16,144]{1,0:T(8,128)S(1)} %copy-done.7), kind=kOutput, calls=%fused_computation.13 | convolution fusion | flops 53427456 | bytes 906240 | tf_op jit(solution)/shard_map/cuv,cvy->uy/dot_general | solution.py:283
  58.9 0.1 copy.25
  59.0 0.1 reshape.327
  59.1 0.6 pad_bitcast_fusion.x_ref
  59.8 13.8 %shard_map.70 = f32[8,184,128]{2,1,0:T(8,128)} custom-call(f32[184,128]{1,0:T(8,128)} %pad_bitcast_fusion.x_ref), custom_call_target="tpu_custom_call" | custom-call | tf_op jit(solution)/shard_map/pallas_call | solution.py:78
  73.6 1.3 %copy.42 = f32[1,8,184,128]{3,1,2,0:T(8,128)S(1)} copy(f32[1,8,184,128]{3,2,1,0:T(8,128)} %bitcast.85) | data formatting | bytes 1507328
  75.0 0.0 copy-start
  75.0 0.0 copy-start.1
  75.0 0.0 copy-start.3
  75.0 0.0 copy-start.4
  75.0 0.9 reshape.330
  76.0 0.0 copy-done
  76.0 0.0 copy-done.1
  76.0 0.0 copy-done.3
  76.0 0.0 copy-done.4
  76.0 0.8 convolution_bitcast_fusion
  76.8 0.8 fusion.1
  77.5 0.1 copy.29
  77.7 0.8 convolution_bitcast_fusion.2
  78.4 0.8 fusion
  79.2 0.1 copy.28
  79.3 0.9 pad_maximum_fusion.plane_ref
  80.2 27.3 %shard_map.71 = (f32[3,6,256,128]{3,2,1,0:T(8,128)}, f32[3,6,256,128]{3,2,1,0:T(8,128)}) custom-call(f32[3,6,256,128]{3,2,1,0:T(8,128)} %e_ref.3, f32[3,6,256,128]{3,2,1,0:T(8,128)} %h_ref.3, f32[6,256,128]{2,1,0:T(8,128)} %select_add_fusion.coef_ref, f32[2,272,144]{2,1,0:T(8,128)} %pad_maximum_fusion.plane_ref, f32[2,42,8,128]{3,2,1,0:T(8,128)} %get-tuple-element.6.frow, ...), custom_call_target="tpu_custom_call" | custom-call | tf_op jit(solution)/shard_map/pallas_call | solution.py:405
  (10 shorter events, 0.1 us)
Async XLA Ops:
  0.6 11.7 %copy-start.2 = (s32[6,256,128]{2,1,0:T(8,128)S(1)}, s32[6,256,128]{2,1,0:T(8,128)}, u32[]{:S(2)}) copy-start(s32[6,256,128]{2,1,0:T(8,128)} %param.7) | copy-start | bytes 2359300
  52.8 0.8 copy-start.5
  52.8 0.8 copy-start.6
  52.8 0.8 copy-start.7
  52.8 0.8 copy-start.8
  75.0 1.0 copy-start
  75.0 1.0 copy-start.1
  75.0 1.0 copy-start.3
  75.0 1.0 copy-start.4

commit v7 on v6

--- a/solution.py
+++ b/solution.py
@@ -153,11 +153,18 @@
             tmp[0:cells_x] = part_of(h)
             tmp[cells_x:cells_x + depth] = rrow[0, h]
             tmp[cells_x + depth:rows] = rrow[1, h]
-            t = tmp[...].T
+            t = lax.dot_general(
+                pick, tmp[...], (((1,), (1,)), ((), ())),
+                precision=lax.Precision.HIGHEST, preferred_element_type=jnp.float32,
+            )
             scol[0, h] = t[0:depth]
-            scol[1, h] = t[cells_y - depth:cells_y]
+            scol[1, h] = t[depth:2 * depth]
             return carry
 
+        row_id = lax.broadcasted_iota(jnp.int32, (2 * depth, cells_y), 0)
+        col_id = lax.broadcasted_iota(jnp.int32, (2 * depth, cells_y), 1)
+        wanted = jnp.where(row_id < depth, row_id, row_id - 2 * depth + cells_y)
+        pick = (col_id == wanted).astype(jnp.float32)
         lax.fori_loop(0, n_parts, fill_cols, 0)
         col_copies = [
             pltpu.make_async_remote_copy(

time: 109 us -> 113 us (1.037)
  Pallas kernels: 83.8 us -> 88 us
    pallas_call x1, Pallas kernels: 37.9 us -> 42.1 us  [gather_with_halo(): pl.pallas_call(kernel, out_shape=(jax.ShapeDtypeStruct((n,) + block.shape...]
where the time goes in v7:
time: 113 us; the launch traced here: 112 us
  Pallas kernels  88 us (78%)
  matrix products  9.72 us (9%)
  local copies, waits for them, and re-layouts  7.08 us (6%)
  other arithmetic  5.93 us (5%)
    pallas_call x1, Pallas kernels, gather_with_halo(): pl.pallas_call(kernel, out_shape=(jax.ShapeDtypeStruct((n,) + block.shape...  42.1 us
    pallas_call x1, Pallas kernels, per_device(): pl.pallas_call(yee_kernel, out_shape=(out, out), in_specs=[VMEM_SPEC] * 6...  27.3 us
    pallas_call x1, Pallas kernels, gather_along(): pl.pallas_call(kernel, out_shape=jax.ShapeDtypeStruct((n,) + block.shape,...  13.8 us
    pallas_call x1, Pallas kernels, summed_over_pair(): pl.pallas_call(kernel, out_shape=jax.ShapeDtypeStruct(block.shape, block....  4.81 us
    cos x4, other arithmetic, phase_tables(): return (jnp.cos(angle), jnp.sin(angle))  3.66 us
    unnamed x20, local copies, waits for them, and re-layouts  2.85 us

profile of v7, /device:TPU:1, one launch (start us, length us, event | category | flops | bytes accessed | tf_op | source)
XLA Modules:
  0.0 111.7 jit_solution(7945161473198458543)
XLA Ops:
  0.6 0.0 copy-start.2
  0.7 0.1 add_add_fusion.1
  0.8 0.8 slice_bitcast_fusion.12
  1.6 0.1 add_add_fusion
  1.6 0.7 fusion.66
  2.4 0.8 fusion.64
  3.2 0.9 fusion.56
  4.1 1.2 %convolution_bitcast_fusion.4 = f32[4,2,80,32]{2,3,0,1:T(8,128)S(1)} fusion(f32[4,2,64,32]{2,3,1,0:T(8,128)} %param.5, s32[4]{0:T(128)S(1)} %get-tuple-element.17), kind=kOutput, calls=%fused_computation.6 | convolution fusion | flops 15790080 | bytes 147472 | tf_op jit(solution)/shard_map/puk,prkj->pruj/dot_general | solution.py:280
  5.2 0.3 convolution_bitcast_fusion.5
  5.5 0.1 reshape.323
  5.6 0.6 pad_bitcast_fusion.1.x_ref
  6.3 4.8 %shard_map.68.x_ref = f32[64,128]{1,0:T(8,128)} custom-call(f32[64,128]{1,0:T(8,128)} %pad_bitcast_fusion.1.x_ref), custom_call_target="tpu_custom_call" | custom-call | tf_op jit(solution)/shard_map/pallas_call | solution.py:226
  11.1 1.3 %fusion.49 = (f32[80,272]{1,0:T(8,128)}, f32[80,272]{1,0:T(8,128)}) fusion(s32[272]{0:T(512)S(1)} %add_add_fusion, s32[80]{0:T(128)S(1)} %iota_add_fusion.1), kind=kLoop, calls=%fused_computation.83 | loop fusion | flops 304640 | bytes 175488 | tf_op jit(solution)/shard_map/cos | solution.py:25
  12.3 0.0 copy-done.2
  12.3 1.2 %select_add_fusion.coef_ref = f32[6,256,128]{2,1,0:T(8,128)} fusion(s32[6,256,128]{2,1,0:T(8,128)S(1)} %copy-done.2), kind=kLoop, calls=%fused_computation.20 | loop fusion | flops 2162688 | bytes 1572864 | tf_op jit(solution)/shard_map/add | solution.py:31
  13.6 42.1 %shard_map.69 = (f32[16,64,128]{2,1,0:T(8,128)}, f32[2,42,8,128]{3,2,1,0:T(8,128)}, f32[2,42,8,272]{3,2,1,0:T(8,128)}) custom-call(f32[64,128]{1,0:T(8,128)} %shard_map.68.x_ref, f32[3,6,256,128]{3,2,1,0:T(8,128)} %e_ref.3, f32[3,6,256,128]{3,2,1,0:T(8,128)} %h_ref.3, f32[6,256,128]{2,1,0:T(8,128)} %select_add_fusion.coef_ref), custom_call_target="tpu_custom_call" | custom-call | tf_op jit(solution)/shard_map/pallas_call | solution.py:187
  55.7 1.4 %copy.43 = f32[2,8,64,128]{3,1,2,0:T(8,128)S(1)} copy(f32[2,8,64,128]{3,2,1,0:T(8,128)} %bitcast.90) | data formatting | bytes 1048576
  57.1 0.0 copy-start.5
  57.1 0.0 copy-start.6
  57.1 0.0 copy-start.7
  57.1 0.0 copy-start.8
  57.1 0.5 reshape.326
  57.7 0.2 copy-done.5
  57.9 0.0 copy-done.6
  57.9 0.0 copy-done.7
  57.9 0.0 copy-done.8
  57.9 1.3 %convolution_bitcast_fusion.6 = f32[80,144]{0,1:T(8,128)S(1)} fusion(f32[16,2,80,48]{3,2,1,0:T(8,128)S(1)} %reshape.326, f32[48,144]{1,0:T(8,128)S(1)} %copy-done.6, f32[16,144]{1,0:T(8,128)S(1)} %copy-done.8, f32[48,144]{1,0:T(8,128)S(1)} %copy-done.5, f32[16,144]{1,0:T(8,128)S(1)} %copy-done.7), kind=kOutput, calls=%fused_computation.8 | convolution fusion | flops 53415936 | bytes 832512 | tf_op jit(solution)/shard_map/cuv,cvy->uy/dot_general | solution.py:293
  59.2 1.3 %fusion.5 = f32[1,80,144]{1,2,0:T(8,128)S(1)} fusion(f32[80,144]{0,1:T(8,128)S(1)} %convolution_bitcast_fusion.6, f32[16,2,80,48]{3,2,1,0:T(8,128)S(1)} %reshape.326, f32[48,144]{1,0:T(8,128)S(1)} %copy-done.6, f32[16,144]{1,0:T(8,128)S(1)} %copy-done.8, f32[48,144]{1,0:T(8,128)S(1)} %copy-done.5, f32[16,144]{1,0:T(8,128)S(1)} %copy-done.7), kind=kOutput, calls=%fused_computation.15 | convolution fusion | flops 53427456 | bytes 906240 | tf_op jit(solution)/shard_map/cuv,cvy->uy/dot_general | solution.py:293
  60.5 1.3 %convolution_bitcast_fusion.8 = f32[80,144]{0,1:T(8,128)S(1)} fusion(f32[16,2,80,48]{3,2,1,0:T(8,128)S(1)} %reshape.326, f32[48,144]{1,0:T(8,128)S(1)} %copy-done.6, f32[16,144]{1,0:T(8,128)S(1)} %copy-done.8, f32[48,144]{1,0:T(8,128)S(1)} %copy-done.5, f32[16,144]{1,0:T(8,128)S(1)} %copy-done.7), kind=kOutput, calls=%fused_computation.10 | convolution fusion | flops 53415936 | bytes 832512 | tf_op jit(solution)/shard_map/cuv,cvy->uy/dot_general | solution.py:290
  61.8 1.3 %fusion.3 = f32[1,80,144]{1,2,0:T(8,128)S(1)} fusion(f32[80,144]{0,1:T(8,128)S(1)} %convolution_bitcast_fusion.8, f32[16,2,80,48]{3,2,1,0:T(8,128)S(1)} %reshape.326, f32[48,144]{1,0:T(8,128)S(1)} %copy-done.6, f32[16,144]{1,0:T(8,128)S(1)} %copy-done.8, f32[48,144]{1,0:T(8,128)S(1)} %copy-done.5, f32[16,144]{1,0:T(8,128)S(1)} %copy-done.7), kind=kOutput, calls=%fused_computation.13 | convolution fusion | flops 53427456 | bytes 906240 | tf_op jit(solution)/shard_map/cuv,cvy->uy/dot_general | solution.py:290
  63.2 0.1 copy.25
  63.3 0.1 reshape.327
  63.4 0.6 pad_bitcast_fusion.x_ref
  64.1 13.8 %shard_map.70 = f32[8,184,128]{2,1,0:T(8,128)} custom-call(f32[184,128]{1,0:T(8,128)} %pad_bitcast_fusion.x_ref), custom_call_target="tpu_custom_call" | custom-call | tf_op jit(solution)/shard_map/pallas_call | solution.py:78
  77.9 1.3 %copy.42 = f32[1,8,184,128]{3,1,2,0:T(8,128)S(1)} copy(f32[1,8,184,128]{3,2,1,0:T(8,128)} %bitcast.85) | data formatting | bytes 1507328
  79.2 0.0 copy-start
  79.2 0.0 copy-start.1
  79.3 0.0 copy-start.3
  79.3 0.0 copy-start.4
  79.3 0.9 reshape.330
  80.2 0.0 copy-done
  80.2 0.0 copy-done.1
  80.3 0.0 copy-done.3
  80.3 0.0 copy-done.4
  80.3 0.8 convolution_bitcast_fusion
  81.0 0.8 fusion.1
  81.8 0.1 copy.29
  81.9 0.8 convolution_bitcast_fusion.2
  82.7 0.8 fusion
  83.5 0.1 copy.28
  83.6 0.9 pad_maximum_fusion.plane_ref
  84.5 27.3 %shard_map.71 = (f32[3,6,256,128]{3,2,1,0:T(8,128)}, f32[3,6,256,128]{3,2,1,0:T(8,128)}) custom-call(f32[3,6,256,128]{3,2,1,0:T(8,128)} %e_ref.3, f32[3,6,256,128]{3,2,1,0:T(8,128)} %h_ref.3, f32[6,256,128]{2,1,0:T(8,128)} %select_add_fusion.coef_ref, f32[2,272,144]{2,1,0:T(8,128)} %pad_maximum_fusion.plane_ref, f32[2,42,8,128]{3,2,1,0:T(8,128)} %get-tuple-element.6.frow, ...), custom_call_target="tpu_custom_call" | custom-call | tf_op jit(solution)/shard_map/pallas_call | solution.py:412
  (10 shorter events, 0.1 us)
Async XLA Ops:
  0.6 11.7 %copy-start.2 = (s32[6,256,128]{2,1,0:T(8,128)S(1)}, s32[6,256,128]{2,1,0:T(8,128)}, u32[]{:S(2)}) copy-start(s32[6,256,128]{2,1,0:T(8,128)} %param.7) | copy-start | bytes 2359300
  57.1 0.8 copy-start.5
  57.1 0.8 copy-start.6
  57.1 0.8 copy-start.7
  57.1 0.8 copy-start.8
  79.2 1.0 copy-start
  79.2 1.0 copy-start.1
  79.3 1.0 copy-start.3
  79.3 1.0 copy-start.4

commit v8 on v6

--- a/solution.py
+++ b/solution.py
@@ -110,16 +110,6 @@
         for peer in (x_lo, x_hi):
             pl.semaphore_signal(barrier, 1, device_id=peer, device_id_type=MESH)
         pl.semaphore_wait(barrier, n + 1)
-        own = pltpu.make_async_copy(x_ref, o_ref.at[me], local.at[0])
-        own.start()
-        gathers = []
-        for k in range(1, n):
-            copy = pltpu.make_async_remote_copy(
-                src_ref=x_ref, dst_ref=o_ref.at[me], send_sem=gsend.at[k - 1], recv_sem=grecv.at[k - 1],
-                device_id={"ty": lax.rem(me + k, n)}, device_id_type=MESH,
-            )
-            copy.start()
-            gathers.append(copy)
 
         def part_of(h):
             comp = h // layers
@@ -146,6 +136,16 @@
         ]
         for copy in row_copies:
             copy.start()
+        own = pltpu.make_async_copy(x_ref, o_ref.at[me], local.at[0])
+        own.start()
+        gathers = []
+        for k in range(1, n):
+            copy = pltpu.make_async_remote_copy(
+                src_ref=x_ref, dst_ref=o_ref.at[me], send_sem=gsend.at[k - 1], recv_sem=grecv.at[k - 1],
+                device_id={"ty": lax.rem(me + k, n)}, device_id_type=MESH,
+            )
+            copy.start()
+            gathers.append(copy)
         for copy in row_copies:
             copy.wait()
 

time: 109 us -> 108 us (level)
  no operation moved by 1% of the time
where the time goes in v8:
time: 108 us; the launch traced here: 107 us
  Pallas kernels  83.6 us (77%)
  matrix products  9.72 us (9%)
  local copies, waits for them, and re-layouts  7.08 us (7%)
  other arithmetic  5.93 us (5%)
    pallas_call x1, Pallas kernels, gather_with_halo(): pl.pallas_call(kernel, out_shape=(jax.ShapeDtypeStruct((n,) + block.shape...  37.7 us
    pallas_call x1, Pallas kernels, per_device(): pl.pallas_call(yee_kernel, out_shape=(out, out), in_specs=[VMEM_SPEC] * 6...  27.3 us
    pallas_call x1, Pallas kernels, gather_along(): pl.pallas_call(kernel, out_shape=jax.ShapeDtypeStruct((n,) + block.shape,...  13.8 us
    pallas_call x1, Pallas kernels, summed_over_pair(): pl.pallas_call(kernel, out_shape=jax.ShapeDtypeStruct(block.shape, block....  4.81 us
    cos x4, other arithmetic, phase_tables(): return (jnp.cos(angle), jnp.sin(angle))  3.66 us
    unnamed x20, local copies, waits for them, and re-layouts  2.85 us

profile of v8, /device:TPU:1, one launch (start us, length us, event | category | flops | bytes accessed | tf_op | source)
XLA Modules:
  0.0 107.3 jit_solution(11702587143255363149)
XLA Ops:
  0.6 0.0 copy-start.2
  0.7 0.1 add_add_fusion.1
  0.8 0.8 slice_bitcast_fusion.12
  1.6 0.1 add_add_fusion
  1.6 0.7 fusion.66
  2.4 0.8 fusion.64
  3.2 0.9 fusion.56
  4.1 1.2 %convolution_bitcast_fusion.4 = f32[4,2,80,32]{2,3,0,1:T(8,128)S(1)} fusion(f32[4,2,64,32]{2,3,1,0:T(8,128)} %param.5, s32[4]{0:T(128)S(1)} %get-tuple-element.17), kind=kOutput, calls=%fused_computation.6 | convolution fusion | flops 15790080 | bytes 147472 | tf_op jit(solution)/shard_map/puk,prkj->pruj/dot_general | solution.py:273
  5.2 0.3 convolution_bitcast_fusion.5
  5.5 0.1 reshape.323
  5.6 0.6 pad_bitcast_fusion.1.x_ref
  6.3 4.8 %shard_map.68.x_ref = f32[64,128]{1,0:T(8,128)} custom-call(f32[64,128]{1,0:T(8,128)} %pad_bitcast_fusion.1.x_ref), custom_call_target="tpu_custom_call" | custom-call | tf_op jit(solution)/shard_map/pallas_call | solution.py:219
  11.1 1.3 %fusion.49 = (f32[80,272]{1,0:T(8,128)}, f32[80,272]{1,0:T(8,128)}) fusion(s32[272]{0:T(512)S(1)} %add_add_fusion, s32[80]{0:T(128)S(1)} %iota_add_fusion.1), kind=kLoop, calls=%fused_computation.83 | loop fusion | flops 304640 | bytes 175488 | tf_op jit(solution)/shard_map/cos | solution.py:25
  12.3 0.0 copy-done.2
  12.3 1.2 %select_add_fusion.coef_ref = f32[6,256,128]{2,1,0:T(8,128)} fusion(s32[6,256,128]{2,1,0:T(8,128)S(1)} %copy-done.2), kind=kLoop, calls=%fused_computation.20 | loop fusion | flops 2162688 | bytes 1572864 | tf_op jit(solution)/shard_map/add | solution.py:31
  13.6 37.7 %shard_map.69 = (f32[16,64,128]{2,1,0:T(8,128)}, f32[2,42,8,128]{3,2,1,0:T(8,128)}, f32[2,42,8,272]{3,2,1,0:T(8,128)}) custom-call(f32[64,128]{1,0:T(8,128)} %shard_map.68.x_ref, f32[3,6,256,128]{3,2,1,0:T(8,128)} %e_ref.3, f32[3,6,256,128]{3,2,1,0:T(8,128)} %h_ref.3, f32[6,256,128]{2,1,0:T(8,128)} %select_add_fusion.coef_ref), custom_call_target="tpu_custom_call" | custom-call | tf_op jit(solution)/shard_map/pallas_call | solution.py:180
  51.3 1.4 %copy.43 = f32[2,8,64,128]{3,1,2,0:T(8,128)S(1)} copy(f32[2,8,64,128]{3,2,1,0:T(8,128)} %bitcast.90) | data formatting | bytes 1048576
  52.6 0.0 copy-start.5
  52.6 0.0 copy-start.6
  52.6 0.0 copy-start.7
  52.7 0.0 copy-start.8
  52.7 0.5 reshape.326
  53.3 0.2 copy-done.5
  53.4 0.0 copy-done.6
  53.5 0.0 copy-done.7
  53.5 0.0 copy-done.8
  53.5 1.3 %convolution_bitcast_fusion.6 = f32[80,144]{0,1:T(8,128)S(1)} fusion(f32[16,2,80,48]{3,2,1,0:T(8,128)S(1)} %reshape.326, f32[48,144]{1,0:T(8,128)S(1)} %copy-done.6, f32[16,144]{1,0:T(8,128)S(1)} %copy-done.8, f32[48,144]{1,0:T(8,128)S(1)} %copy-done.5, f32[16,144]{1,0:T(8,128)S(1)} %copy-done.7), kind=kOutput, calls=%fused_computation.8 | convolution fusion | flops 53415936 | bytes 832512 | tf_op jit(solution)/shard_map/cuv,cvy->uy/dot_general | solution.py:286
  54.8 1.3 %fusion.5 = f32[1,80,144]{1,2,0:T(8,128)S(1)} fusion(f32[80,144]{0,1:T(8,128)S(1)} %convolution_bitcast_fusion.6, f32[16,2,80,48]{3,2,1,0:T(8,128)S(1)} %reshape.326, f32[48,144]{1,0:T(8,128)S(1)} %copy-done.6, f32[16,144]{1,0:T(8,128)S(1)} %copy-done.8, f32[48,144]{1,0:T(8,128)S(1)} %copy-done.5, f32[16,144]{1,0:T(8,128)S(1)} %copy-done.7), kind=kOutput, calls=%fused_computation.15 | convolution fusion | flops 53427456 | bytes 906240 | tf_op jit(solution)/shard_map/cuv,cvy->uy/dot_general | solution.py:286
  56.1 1.3 %convolution_bitcast_fusion.8 = f32[80,144]{0,1:T(8,128)S(1)} fusion(f32[16,2,80,48]{3,2,1,0:T(8,128)S(1)} %reshape.326, f32[48,144]{1,0:T(8,128)S(1)} %copy-done.6, f32[16,144]{1,0:T(8,128)S(1)} %copy-done.8, f32[48,144]{1,0:T(8,128)S(1)} %copy-done.5, f32[16,144]{1,0:T(8,128)S(1)} %copy-done.7), kind=kOutput, calls=%fused_computation.10 | convolution fusion | flops 53415936 | bytes 832512 | tf_op jit(solution)/shard_map/cuv,cvy->uy/dot_general | solution.py:283
  57.4 1.3 %fusion.3 = f32[1,80,144]{1,2,0:T(8,128)S(1)} fusion(f32[80,144]{0,1:T(8,128)S(1)} %convolution_bitcast_fusion.8, f32[16,2,80,48]{3,2,1,0:T(8,128)S(1)} %reshape.326, f32[48,144]{1,0:T(8,128)S(1)} %copy-done.6, f32[16,144]{1,0:T(8,128)S(1)} %copy-done.8, f32[48,144]{1,0:T(8,128)S(1)} %copy-done.5, f32[16,144]{1,0:T(8,128)S(1)} %copy-done.7), kind=kOutput, calls=%fused_computation.13 | convolution fusion | flops 53427456 | bytes 906240 | tf_op jit(solution)/shard_map/cuv,cvy->uy/dot_general | solution.py:283
  58.7 0.1 copy.25
  58.8 0.1 reshape.327
  59.0 0.6 pad_bitcast_fusion.x_ref
  59.6 13.8 %shard_map.70 = f32[8,184,128]{2,1,0:T(8,128)} custom-call(f32[184,128]{1,0:T(8,128)} %pad_bitcast_fusion.x_ref), custom_call_target="tpu_custom_call" | custom-call | tf_op jit(solution)/shard_map/pallas_call | solution.py:78
  73.5 1.3 %copy.42 = f32[1,8,184,128]{3,1,2,0:T(8,128)S(1)} copy(f32[1,8,184,128]{3,2,1,0:T(8,128)} %bitcast.85) | data formatting | bytes 1507328
  74.8 0.0 copy-start
  74.8 0.0 copy-start.1
  74.8 0.0 copy-start.3
  74.8 0.0 copy-start.4
  74.8 0.9 reshape.330
  75.8 0.0 copy-done
  75.8 0.0 copy-done.1
  75.8 0.0 copy-done.3
  75.8 0.0 copy-done.4
  75.8 0.8 convolution_bitcast_fusion
  76.6 0.8 fusion.1
  77.4 0.1 copy.29
  77.5 0.8 convolution_bitcast_fusion.2
  78.3 0.8 fusion
  79.0 0.1 copy.28
  79.2 0.9 pad_maximum_fusion.plane_ref
  80.0 27.3 %shard_map.71 = (f32[3,6,256,128]{3,2,1,0:T(8,128)}, f32[3,6,256,128]{3,2,1,0:T(8,128)}) custom-call(f32[3,6,256,128]{3,2,1,0:T(8,128)} %e_ref.3, f32[3,6,256,128]{3,2,1,0:T(8,128)} %h_ref.3, f32[6,256,128]{2,1,0:T(8,128)} %select_add_fusion.coef_ref, f32[2,272,144]{2,1,0:T(8,128)} %pad_maximum_fusion.plane_ref, f32[2,42,8,128]{3,2,1,0:T(8,128)} %get-tuple-element.6.frow, ...), custom_call_target="tpu_custom_call" | custom-call | tf_op jit(solution)/shard_map/pallas_call | solution.py:405
  (10 shorter events, 0.1 us)
Async XLA Ops:
  0.6 11.7 %copy-start.2 = (s32[6,256,128]{2,1,0:T(8,128)S(1)}, s32[6,256,128]{2,1,0:T(8,128)}, u32[]{:S(2)}) copy-start(s32[6,256,128]{2,1,0:T(8,128)} %param.7) | copy-start | bytes 2359300
  52.6 0.8 copy-start.5
  52.6 0.8 copy-start.6
  52.6 0.8 copy-start.7
  52.7 0.8 copy-start.8
  74.8 1.0 copy-start
  74.8 1.0 copy-start.1
  74.8 1.0 copy-start.3
  74.8 1.0 copy-start.4

commit v9 on v8

--- a/solution.py
+++ b/solution.py
@@ -276,31 +276,18 @@
     merged = summed_over_pair(lane_dense(merged), "src", 2)
     got, frow, fcol = gather_with_halo(merged, e_field, h_field, coefficient, HALO, 0)
     got = got.reshape(n_ty, -1)[:, :size].reshape(n_ty, 2, span_x, span_y)
-    g_re = got[:, 0]
-    g_im = got[:, 1]
     y_pos = lax.axis_index("ty") * cells_y + ring_positions(cells_y, HALO)
     by_c, by_s = chunk_tables(cols_ky, span_y, n_ty, my // 2 + SHIFT, y_pos, full_y)
-    i_re = jnp.einsum("cuv,cvy->uy", g_re, by_c, precision=PREC) - jnp.einsum(
-        "cuv,cvy->uy", g_im, by_s, precision=PREC
-    )
-    i_im = jnp.einsum("cuv,cvy->uy", g_re, by_s, precision=PREC) + jnp.einsum(
-        "cuv,cvy->uy", g_im, by_c, precision=PREC
-    )
-    inner = jnp.stack([i_re, i_im])
+    turn_y = jnp.stack([jnp.stack([by_c, by_s], 2), jnp.stack([-by_s, by_c], 2)], 1)
+    inner = jnp.einsum("cauv,cavoy->ouy", got, turn_y, precision=PREC)
     size = inner.size
     inner = gather_along(lane_dense(inner), ("tx",), 1)
     inner = inner.reshape(n_tx, -1)[:, :size].reshape((n_tx,) + (2, span_x, cells_y + 2 * HALO))
-    i_re = inner[:, 0]
-    i_im = inner[:, 1]
     x_pos = lax.axis_index("tx") * cells_x + ring_positions(cells_x, HALO)
     bx_c, bx_s = chunk_tables(rows_kx, span_x, n_tx, mx // 2 + SHIFT, x_pos, full_x)
-    p_re = jnp.einsum("cux,cuy->xy", bx_c, i_re, precision=PREC) - jnp.einsum(
-        "cux,cuy->xy", bx_s, i_im, precision=PREC
-    )
-    p_im = jnp.einsum("cux,cuy->xy", bx_c, i_im, precision=PREC) + jnp.einsum(
-        "cux,cuy->xy", bx_s, i_re, precision=PREC
-    )
-    return jnp.stack([p_re, p_im]), frow, fcol
+    turn_x = jnp.stack([jnp.stack([bx_c, bx_s], 2), jnp.stack([-bx_s, bx_c], 2)], 1)
+    plane = jnp.einsum("cauox,cauy->oxy", turn_x, inner, precision=PREC)
+    return plane, frow, fcol
 
 
 def yee_kernel(e_ref, h_ref, coef_ref, plane_ref, frow, fcol, eo_ref, ho_ref, ext, cp, tmp):

time: 108 us -> 109 us (level)
    dot_general x8 -> x2, matrix products: 8.25 us -> 8.81 us  [the longest x1 4.72 us: injection_plane(): inner = jnp.einsum('cauv,cavoy->ouy', got, turn_y, precision=PREC)]
where the time goes in v9:
time: 109 us; the launch traced here: 108 us
  Pallas kernels  83.7 us (77%)
  matrix products  10.3 us (9%)
  local copies, waits for them, and re-layouts  6.81 us (6%)
  other arithmetic  6.32 us (6%)
    pallas_call x1, Pallas kernels, gather_with_halo(): pl.pallas_call(kernel, out_shape=(jax.ShapeDtypeStruct((n,) + block.shape...  37.7 us
    pallas_call x1, Pallas kernels, per_device(): pl.pallas_call(yee_kernel, out_shape=(out, out), in_specs=[VMEM_SPEC] * 6...  27.3 us
    pallas_call x1, Pallas kernels, gather_along(): pl.pallas_call(kernel, out_shape=jax.ShapeDtypeStruct((n,) + block.shape,...  13.8 us
    pallas_call x1, Pallas kernels, summed_over_pair(): pl.pallas_call(kernel, out_shape=jax.ShapeDtypeStruct(block.shape, block....  4.81 us
    dot_general x1, matrix products, injection_plane(): inner = jnp.einsum('cauv,cavoy->ouy', got, turn_y, precision=PREC)  4.72 us
    dot_general x1, matrix products, injection_plane(): plane = jnp.einsum('cauox,cauy->oxy', turn_x, inner, precision=PREC)  4.09 us
    cos x4, other arithmetic, phase_tables(): return (jnp.cos(angle), jnp.sin(angle))  3.68 us
    unnamed x20, local copies, waits for them, and re-layouts  2.85 us

profile of v9, /device:TPU:1, one launch (start us, length us, event | category | flops | bytes accessed | tf_op | source)
XLA Modules:
  0.0 108.1 jit_solution(4932594002169064541)
XLA Ops:
  0.6 0.0 copy-start
  0.7 0.1 add_add_fusion.1
  0.8 0.8 slice_bitcast_fusion
  1.6 0.1 add_add_fusion
  1.6 0.8 fusion.52
  2.4 0.8 fusion.50
  3.2 0.9 fusion.42
  4.1 1.2 %convolution_bitcast_fusion = f32[4,2,80,32]{2,3,0,1:T(8,128)S(1)} fusion(f32[4,2,64,32]{2,3,1,0:T(8,128)} %param.5, s32[4]{0:T(128)S(1)} %get-tuple-element.27), kind=kOutput, calls=%fused_computation.18 | convolution fusion | flops 15790080 | bytes 147472 | tf_op jit(solution)/shard_map/puk,prkj->pruj/dot_general | solution.py:273
  5.3 0.3 convolution_bitcast_fusion.1
  5.6 0.1 reshape.365
  5.7 0.6 pad_bitcast_fusion.1.x_ref
  6.3 4.8 %shard_map.68.x_ref = f32[64,128]{1,0:T(8,128)} custom-call(f32[64,128]{1,0:T(8,128)} %pad_bitcast_fusion.1.x_ref), custom_call_target="tpu_custom_call" | custom-call | tf_op jit(solution)/shard_map/pallas_call | solution.py:219
  11.1 1.3 %fusion.35 = (f32[80,272]{1,0:T(8,128)}, f32[80,272]{1,0:T(8,128)}) fusion(s32[272]{0:T(512)S(1)} %add_add_fusion, s32[80]{0:T(128)S(1)} %iota_add_fusion.1), kind=kLoop, calls=%fused_computation.51 | loop fusion | flops 304640 | bytes 175488 | tf_op jit(solution)/shard_map/cos | solution.py:25
  12.4 0.0 copy-done
  12.4 1.2 %select_add_fusion.coef_ref = f32[6,256,128]{2,1,0:T(8,128)} fusion(s32[6,256,128]{2,1,0:T(8,128)S(1)} %copy-done), kind=kLoop, calls=%fused_computation.24 | loop fusion | flops 2162688 | bytes 1572864 | tf_op jit(solution)/shard_map/add | solution.py:31
  13.6 37.7 %shard_map.69 = (f32[16,64,128]{2,1,0:T(8,128)}, f32[2,42,8,128]{3,2,1,0:T(8,128)}, f32[2,42,8,272]{3,2,1,0:T(8,128)}) custom-call(f32[64,128]{1,0:T(8,128)} %shard_map.68.x_ref, f32[3,6,256,128]{3,2,1,0:T(8,128)} %e_ref.3, f32[3,6,256,128]{3,2,1,0:T(8,128)} %h_ref.3, f32[6,256,128]{2,1,0:T(8,128)} %select_add_fusion.coef_ref), custom_call_target="tpu_custom_call" | custom-call | tf_op jit(solution)/shard_map/pallas_call | solution.py:180
  51.4 1.4 %copy.50 = f32[2,8,64,128]{3,1,2,0:T(8,128)S(1)} copy(f32[2,8,64,128]{3,2,1,0:T(8,128)} %bitcast.72) | data formatting | bytes 1048576
  52.7 0.0 copy-start.3
  52.7 0.0 copy-start.4
  52.7 0.0 copy-start.5
  52.7 0.0 copy-start.6
  52.8 0.5 reshape.368
  53.4 0.2 copy-done.3
  53.5 0.0 copy-done.4
  53.5 0.0 copy-done.5
  53.5 0.0 copy-done.6
  53.5 0.3 multiply_add_fusion.1
  53.9 0.4 maximum_bitcast_fusion.2
  54.3 4.7 %fusion.17 = f32[2,80,144]{1,2,0:T(8,128)S(1)} fusion(f32[16,1,48,2,144]{4,2,0,1,3:T(8,128)S(1)} %get-tuple-element.11, f32[16,1,48,2,144]{4,2,0,1,3:T(8,128)S(1)} %get-tuple-element.10, f32[16,2,80,48]{3,2,1,0:T(8,128)S(1)} %reshape.368), kind=kOutput, calls=%fused_computation.17 | convolution fusion | flops 212779008 | bytes 2353152 | tf_op jit(solution)/shard_map/cauv,cavoy->ouy/dot_general | solution.py:282
  59.0 0.1 copy.14
  59.1 0.1 reshape.369
  59.3 0.6 pad_bitcast_fusion.x_ref
  59.9 13.8 %shard_map.70 = f32[8,184,128]{2,1,0:T(8,128)} custom-call(f32[184,128]{1,0:T(8,128)} %pad_bitcast_fusion.x_ref), custom_call_target="tpu_custom_call" | custom-call | tf_op jit(solution)/shard_map/pallas_call | solution.py:78
  73.7 1.3 %copy.49 = f32[1,8,184,128]{3,1,2,0:T(8,128)S(1)} copy(f32[1,8,184,128]{3,2,1,0:T(8,128)} %bitcast.69) | data formatting | bytes 1507328
  75.0 0.0 copy-start.1
  75.0 0.0 copy-start.2
  75.0 0.0 copy-start.7
  75.1 0.0 copy-start.8
  75.1 0.9 reshape.372
  76.1 0.0 copy-done.1
  76.1 0.0 copy-done.2
  76.1 0.0 copy-done.7
  76.1 0.0 copy-done.8
  76.1 0.2 multiply_add_fusion
  76.4 0.3 maximum_bitcast_fusion
  76.7 4.1 %fusion.12.plane_ref = f32[2,272,144]{2,1,0:T(8,128)} fusion(f32[8,1,80,2,272]{4,2,0,1,3:T(8,128)S(1)} %get-tuple-element.9, f32[8,1,80,2,272]{4,2,0,1,3:T(8,128)S(1)} %get-tuple-element.8, f32[8,2,80,144]{3,2,1,0:T(8,128)S(1)} %reshape.372), kind=kOutput, calls=%fused_computation.16 | convolution fusion | flops 602316800 | bytes 3835904 | tf_op jit(solution)/shard_map/cauox,cauy->oxy/dot_general | solution.py:289
  80.8 27.3 %shard_map.71 = (f32[3,6,256,128]{3,2,1,0:T(8,128)}, f32[3,6,256,128]{3,2,1,0:T(8,128)}) custom-call(f32[3,6,256,128]{3,2,1,0:T(8,128)} %e_ref.3, f32[3,6,256,128]{3,2,1,0:T(8,128)} %h_ref.3, f32[6,256,128]{2,1,0:T(8,128)} %select_add_fusion.coef_ref, f32[2,272,144]{2,1,0:T(8,128)} %fusion.12.plane_ref, f32[2,42,8,128]{3,2,1,0:T(8,128)} %get-tuple-element.6.frow, ...), custom_call_target="tpu_custom_call" | custom-call | tf_op jit(solution)/shard_map/pallas_call | solution.py:392
  (9 shorter events, 0.1 us)
Async XLA Ops:
  0.6 11.8 %copy-start = (s32[6,256,128]{2,1,0:T(8,128)S(1)}, s32[6,256,128]{2,1,0:T(8,128)}, u32[]{:S(2)}) copy-start(s32[6,256,128]{2,1,0:T(8,128)} %param.7) | copy-start | bytes 2359300
  52.7 0.8 copy-start.3
  52.7 0.8 copy-start.4
  52.7 0.8 copy-start.5
  52.7 0.8 copy-start.6
  75.0 1.1 copy-start.1
  75.0 1.1 copy-start.2
  75.0 1.1 copy-start.7
  75.1 1.1 copy-start.8

commit v10 on v8

--- a/solution.py
+++ b/solution.py
@@ -111,19 +111,18 @@
             pl.semaphore_signal(barrier, 1, device_id=peer, device_id_type=MESH)
         pl.semaphore_wait(barrier, n + 1)
 
-        def part_of(h):
-            comp = h // layers
-            z = h % layers
-            field = jnp.where(comp < 3, e_ref[comp % 3, z], h_ref[comp % 3, z])
-            return jnp.where(comp < 6, field, coef_ref[z])
-
-        def fill_rows(h, carry):
-            part = part_of(h)
-            srow[0, h] = part[0:depth]
-            srow[1, h] = part[cells_x - depth:cells_x]
-            return carry
-
-        lax.fori_loop(0, n_parts, fill_rows, 0)
+        def part_ref(h):
+            comp, z = divmod(h, layers)
+            if comp < 3:
+                return e_ref.at[comp, z]
+            if comp < 6:
+                return h_ref.at[comp - 3, z]
+            return coef_ref.at[z]
+
+        for h in range(n_parts):
+            src_ref = part_ref(h)
+            srow[0, h] = src_ref[0:depth]
+            srow[1, h] = src_ref[cells_x - depth:cells_x]
         row_copies = [
             pltpu.make_async_remote_copy(
                 src_ref=srow.at[0], dst_ref=rrow.at[0], send_sem=hsend.at[0], recv_sem=hrecv.at[0],
@@ -149,16 +148,13 @@
         for copy in row_copies:
             copy.wait()
 
-        def fill_cols(h, carry):
-            tmp[0:cells_x] = part_of(h)
+        for h in range(n_parts):
+            tmp[0:cells_x] = part_ref(h)[...]
             tmp[cells_x:cells_x + depth] = rrow[0, h]
             tmp[cells_x + depth:rows] = rrow[1, h]
             t = tmp[...].T
             scol[0, h] = t[0:depth]
             scol[1, h] = t[cells_y - depth:cells_y]
-            return carry
-
-        lax.fori_loop(0, n_parts, fill_cols, 0)
         col_copies = [
             pltpu.make_async_remote_copy(
                 src_ref=scol.at[0], dst_ref=rcol.at[0], send_sem=hsend.at[2], recv_sem=hrecv.at[2],
@@ -330,11 +326,11 @@
     def place_fields(h, carry):
         comp = h // layers
         z = h % layers
-        own = jnp.where(comp < 3, e_ref[comp % 3, z], h_ref[comp % 3, z])
-        place_part(ext, comp * slab + z + 1, own, h)
+        place_part(ext, comp * slab + z + 1, e_ref[comp, z], h)
+        place_part(ext, (comp + 3) * slab + z + 1, h_ref[comp, z], h + 3 * layers)
         return carry
 
-    lax.fori_loop(0, n_field, place_fields, 0)
+    lax.fori_loop(0, 3 * layers, place_fields, 0)
     for z in range(layers):
         place_part(cp, z, coef_ref[z], n_field + z)
     zero = jnp.zeros((rows, lanes), jnp.float32)

time: 108 us -> 103 us (0.954)
  Pallas kernels: 83.6 us -> 78.5 us
    pallas_call x1, Pallas kernels: 37.7 us -> 33.4 us  [gather_with_halo(): pl.pallas_call(kernel, out_shape=(jax.ShapeDtypeStruct((n,) + block.shape...]
    pallas_call x1, Pallas kernels: 27.3 us -> 24.8 us  [per_device(): pl.pallas_call(yee_kernel, out_shape=(out, out), in_specs=[VMEM_SPEC] * 6...]
    pallas_call x1, Pallas kernels: 13.8 us -> 15.5 us  [gather_along(): pl.pallas_call(kernel, out_shape=jax.ShapeDtypeStruct((n,) + block.shape,...]
where the time goes in v10:
time: 103 us; the launch traced here: 102 us
  Pallas kernels  78.5 us (76%)
  matrix products  9.72 us (9%)
  local copies, waits for them, and re-layouts  7.08 us (7%)
  other arithmetic  5.93 us (6%)
    pallas_call x1, Pallas kernels, gather_with_halo(): pl.pallas_call(kernel, out_shape=(jax.ShapeDtypeStruct((n,) + block.shape...  33.4 us
    pallas_call x1, Pallas kernels, per_device(): pl.pallas_call(yee_kernel, out_shape=(out, out), in_specs=[VMEM_SPEC] * 6...  24.8 us
    pallas_call x1, Pallas kernels, gather_along(): pl.pallas_call(kernel, out_shape=jax.ShapeDtypeStruct((n,) + block.shape,...  15.5 us
    pallas_call x1, Pallas kernels, summed_over_pair(): pl.pallas_call(kernel, out_shape=jax.ShapeDtypeStruct(block.shape, block....  4.81 us
    cos x4, other arithmetic, phase_tables(): return (jnp.cos(angle), jnp.sin(angle))  3.66 us
    unnamed x20, local copies, waits for them, and re-layouts  2.85 us

profile of v10, /device:TPU:1, one launch (start us, length us, event | category | flops | bytes accessed | tf_op | source)
XLA Modules:
  0.0 102.2 jit_solution(18073758836831689531)
XLA Ops:
  0.6 0.0 copy-start.2
  0.7 0.1 add_add_fusion.1
  0.8 0.8 slice_bitcast_fusion.12
  1.6 0.1 add_add_fusion
  1.6 0.7 fusion.66
  2.4 0.8 fusion.64
  3.2 0.9 fusion.56
  4.1 1.2 %convolution_bitcast_fusion.4 = f32[4,2,80,32]{2,3,0,1:T(8,128)S(1)} fusion(f32[4,2,64,32]{2,3,1,0:T(8,128)} %param.5, s32[4]{0:T(128)S(1)} %get-tuple-element.17), kind=kOutput, calls=%fused_computation.6 | convolution fusion | flops 15790080 | bytes 147472 | tf_op jit(solution)/shard_map/puk,prkj->pruj/dot_general | solution.py:269
  5.2 0.3 convolution_bitcast_fusion.5
  5.5 0.1 reshape.323
  5.6 0.6 pad_bitcast_fusion.1.x_ref
  6.3 4.8 %shard_map.68.x_ref = f32[64,128]{1,0:T(8,128)} custom-call(f32[64,128]{1,0:T(8,128)} %pad_bitcast_fusion.1.x_ref), custom_call_target="tpu_custom_call" | custom-call | tf_op jit(solution)/shard_map/pallas_call | solution.py:215
  11.1 1.3 %fusion.49 = (f32[80,272]{1,0:T(8,128)}, f32[80,272]{1,0:T(8,128)}) fusion(s32[272]{0:T(512)S(1)} %add_add_fusion, s32[80]{0:T(128)S(1)} %iota_add_fusion.1), kind=kLoop, calls=%fused_computation.83 | loop fusion | flops 304640 | bytes 175488 | tf_op jit(solution)/shard_map/cos | solution.py:25
  12.3 0.0 copy-done.2
  12.3 1.2 %select_add_fusion.coef_ref = f32[6,256,128]{2,1,0:T(8,128)} fusion(s32[6,256,128]{2,1,0:T(8,128)S(1)} %copy-done.2), kind=kLoop, calls=%fused_computation.20 | loop fusion | flops 2162688 | bytes 1572864 | tf_op jit(solution)/shard_map/add | solution.py:31
  13.6 33.4 %shard_map.69 = (f32[16,64,128]{2,1,0:T(8,128)}, f32[2,42,8,128]{3,2,1,0:T(8,128)}, f32[2,42,8,272]{3,2,1,0:T(8,128)}) custom-call(f32[64,128]{1,0:T(8,128)} %shard_map.68.x_ref, f32[3,6,256,128]{3,2,1,0:T(8,128)} %e_ref.3, f32[3,6,256,128]{3,2,1,0:T(8,128)} %h_ref.3, f32[6,256,128]{2,1,0:T(8,128)} %select_add_fusion.coef_ref), custom_call_target="tpu_custom_call" | custom-call | tf_op jit(solution)/shard_map/pallas_call | solution.py:176
  46.9 1.4 %copy.43 = f32[2,8,64,128]{3,1,2,0:T(8,128)S(1)} copy(f32[2,8,64,128]{3,2,1,0:T(8,128)} %bitcast.90) | data formatting | bytes 1048576
  48.3 0.0 copy-start.5
  48.3 0.0 copy-start.6
  48.3 0.0 copy-start.7
  48.3 0.0 copy-start.8
  48.3 0.5 reshape.326
  48.9 0.2 copy-done.5
  49.1 0.0 copy-done.6
  49.1 0.0 copy-done.7
  49.1 0.0 copy-done.8
  49.1 1.3 %convolution_bitcast_fusion.6 = f32[80,144]{0,1:T(8,128)S(1)} fusion(f32[16,2,80,48]{3,2,1,0:T(8,128)S(1)} %reshape.326, f32[48,144]{1,0:T(8,128)S(1)} %copy-done.6, f32[16,144]{1,0:T(8,128)S(1)} %copy-done.8, f32[48,144]{1,0:T(8,128)S(1)} %copy-done.5, f32[16,144]{1,0:T(8,128)S(1)} %copy-done.7), kind=kOutput, calls=%fused_computation.8 | convolution fusion | flops 53415936 | bytes 832512 | tf_op jit(solution)/shard_map/cuv,cvy->uy/dot_general | solution.py:282
  50.4 1.3 %fusion.5 = f32[1,80,144]{1,2,0:T(8,128)S(1)} fusion(f32[80,144]{0,1:T(8,128)S(1)} %convolution_bitcast_fusion.6, f32[16,2,80,48]{3,2,1,0:T(8,128)S(1)} %reshape.326, f32[48,144]{1,0:T(8,128)S(1)} %copy-done.6, f32[16,144]{1,0:T(8,128)S(1)} %copy-done.8, f32[48,144]{1,0:T(8,128)S(1)} %copy-done.5, f32[16,144]{1,0:T(8,128)S(1)} %copy-done.7), kind=kOutput, calls=%fused_computation.15 | convolution fusion | flops 53427456 | bytes 906240 | tf_op jit(solution)/shard_map/cuv,cvy->uy/dot_general | solution.py:282
  51.7 1.3 %convolution_bitcast_fusion.8 = f32[80,144]{0,1:T(8,128)S(1)} fusion(f32[16,2,80,48]{3,2,1,0:T(8,128)S(1)} %reshape.326, f32[48,144]{1,0:T(8,128)S(1)} %copy-done.6, f32[16,144]{1,0:T(8,128)S(1)} %copy-done.8, f32[48,144]{1,0:T(8,128)S(1)} %copy-done.5, f32[16,144]{1,0:T(8,128)S(1)} %copy-done.7), kind=kOutput, calls=%fused_computation.10 | convolution fusion | flops 53415936 | bytes 832512 | tf_op jit(solution)/shard_map/cuv,cvy->uy/dot_general | solution.py:279
  53.0 1.3 %fusion.3 = f32[1,80,144]{1,2,0:T(8,128)S(1)} fusion(f32[80,144]{0,1:T(8,128)S(1)} %convolution_bitcast_fusion.8, f32[16,2,80,48]{3,2,1,0:T(8,128)S(1)} %reshape.326, f32[48,144]{1,0:T(8,128)S(1)} %copy-done.6, f32[16,144]{1,0:T(8,128)S(1)} %copy-done.8, f32[48,144]{1,0:T(8,128)S(1)} %copy-done.5, f32[16,144]{1,0:T(8,128)S(1)} %copy-done.7), kind=kOutput, calls=%fused_computation.13 | convolution fusion | flops 53427456 | bytes 906240 | tf_op jit(solution)/shard_map/cuv,cvy->uy/dot_general | solution.py:279
  54.4 0.1 copy.25
  54.5 0.1 reshape.327
  54.6 0.6 pad_bitcast_fusion.x_ref
  55.3 15.5 %shard_map.70 = f32[8,184,128]{2,1,0:T(8,128)} custom-call(f32[184,128]{1,0:T(8,128)} %pad_bitcast_fusion.x_ref), custom_call_target="tpu_custom_call" | custom-call | tf_op jit(solution)/shard_map/pallas_call | solution.py:78
  70.8 1.3 %copy.42 = f32[1,8,184,128]{3,1,2,0:T(8,128)S(1)} copy(f32[1,8,184,128]{3,2,1,0:T(8,128)} %bitcast.85) | data formatting | bytes 1507328
  72.1 0.0 copy-start
  72.2 0.0 copy-start.1
  72.2 0.0 copy-start.3
  72.2 0.0 copy-start.4
  72.2 0.9 reshape.330
  73.1 0.0 copy-done
  73.2 0.0 copy-done.1
  73.2 0.0 copy-done.3
  73.2 0.0 copy-done.4
  73.2 0.8 convolution_bitcast_fusion
  73.9 0.8 fusion.1
  74.7 0.1 copy.29
  74.9 0.8 convolution_bitcast_fusion.2
  75.6 0.8 fusion
  76.4 0.1 copy.28
  76.5 0.9 pad_maximum_fusion.plane_ref
  77.4 24.8 %shard_map.71 = (f32[3,6,256,128]{3,2,1,0:T(8,128)}, f32[3,6,256,128]{3,2,1,0:T(8,128)}) custom-call(f32[3,6,256,128]{3,2,1,0:T(8,128)} %e_ref.3, f32[3,6,256,128]{3,2,1,0:T(8,128)} %h_ref.3, f32[6,256,128]{2,1,0:T(8,128)} %select_add_fusion.coef_ref, f32[2,272,144]{2,1,0:T(8,128)} %pad_maximum_fusion.plane_ref, f32[2,42,8,128]{3,2,1,0:T(8,128)} %get-tuple-element.6.frow, ...), custom_call_target="tpu_custom_call" | custom-call | tf_op jit(solution)/shard_map/pallas_call | solution.py:401
  (10 shorter events, 0.1 us)
Async XLA Ops:
  0.6 11.7 %copy-start.2 = (s32[6,256,128]{2,1,0:T(8,128)S(1)}, s32[6,256,128]{2,1,0:T(8,128)}, u32[]{:S(2)}) copy-start(s32[6,256,128]{2,1,0:T(8,128)} %param.7) | copy-start | bytes 2359300
  48.3 0.8 copy-start.5
  48.3 0.8 copy-start.6
  48.3 0.8 copy-start.7
  48.3 0.8 copy-start.8
  72.1 1.0 copy-start
  72.2 1.0 copy-start.1
  72.2 1.0 copy-start.3
  72.2 1.0 copy-start.4

commit v11 on v10

--- a/solution.py
+++ b/solution.py
@@ -145,16 +145,16 @@
             )
             copy.start()
             gathers.append(copy)
+        for h in range(n_parts):
+            t = part_ref(h)[...].T
+            scol[0, h, :, 0:cells_x] = t[0:depth]
+            scol[1, h, :, 0:cells_x] = t[cells_y - depth:cells_y]
         for copy in row_copies:
             copy.wait()
-
         for h in range(n_parts):
-            tmp[0:cells_x] = part_ref(h)[...]
-            tmp[cells_x:cells_x + depth] = rrow[0, h]
-            tmp[cells_x + depth:rows] = rrow[1, h]
-            t = tmp[...].T
-            scol[0, h] = t[0:depth]
-            scol[1, h] = t[cells_y - depth:cells_y]
+            t = jnp.concatenate([rrow[0, h], rrow[1, h]], 0).T
+            scol[0, h, :, cells_x:rows] = t[0:depth]
+            scol[1, h, :, cells_x:rows] = t[cells_y - depth:cells_y]
         col_copies = [
             pltpu.make_async_remote_copy(
                 src_ref=scol.at[0], dst_ref=rcol.at[0], send_sem=hsend.at[2], recv_sem=hrecv.at[2],

time: 103 us -> 103 us (level)
    pallas_call x1, Pallas kernels: 15.5 us -> 16.7 us  [gather_along(): pl.pallas_call(kernel, out_shape=jax.ShapeDtypeStruct((n,) + block.shape,...]
    pallas_call x1, Pallas kernels: 33.4 us -> 32.1 us  [gather_with_halo(): pl.pallas_call(kernel, out_shape=(jax.ShapeDtypeStruct((n,) + block.shape...]
where the time goes in v11:
time: 103 us; the launch traced here: 102 us
  Pallas kernels  78.5 us (76%)
  matrix products  9.72 us (9%)
  local copies, waits for them, and re-layouts  7.08 us (7%)
  other arithmetic  5.93 us (6%)
    pallas_call x1, Pallas kernels, gather_with_halo(): pl.pallas_call(kernel, out_shape=(jax.ShapeDtypeStruct((n,) + block.shape...  32.1 us
    pallas_call x1, Pallas kernels, per_device(): pl.pallas_call(yee_kernel, out_shape=(out, out), in_specs=[VMEM_SPEC] * 6...  24.8 us
    pallas_call x1, Pallas kernels, gather_along(): pl.pallas_call(kernel, out_shape=jax.ShapeDtypeStruct((n,) + block.shape,...  16.7 us
    pallas_call x1, Pallas kernels, summed_over_pair(): pl.pallas_call(kernel, out_shape=jax.ShapeDtypeStruct(block.shape, block....  4.81 us
    cos x4, other arithmetic, phase_tables(): return (jnp.cos(angle), jnp.sin(angle))  3.66 us
    unnamed x20, local copies, waits for them, and re-layouts  2.85 us

profile of v11, /device:TPU:1, one launch (start us, length us, event | category | flops | bytes accessed | tf_op | source)
XLA Modules:
  0.0 102.2 jit_solution(12095026778279902973)
XLA Ops:
  0.6 0.0 copy-start.2
  0.7 0.1 add_add_fusion.1
  0.8 0.8 slice_bitcast_fusion.12
  1.6 0.1 add_add_fusion
  1.6 0.7 fusion.66
  2.4 0.8 fusion.64
  3.2 0.9 fusion.56
  4.1 1.2 %convolution_bitcast_fusion.4 = f32[4,2,80,32]{2,3,0,1:T(8,128)S(1)} fusion(f32[4,2,64,32]{2,3,1,0:T(8,128)} %param.5, s32[4]{0:T(128)S(1)} %get-tuple-element.17), kind=kOutput, calls=%fused_computation.6 | convolution fusion | flops 15790080 | bytes 147472 | tf_op jit(solution)/shard_map/puk,prkj->pruj/dot_general | solution.py:269
  5.2 0.3 convolution_bitcast_fusion.5
  5.5 0.1 reshape.323
  5.6 0.6 pad_bitcast_fusion.1.x_ref
  6.3 4.8 %shard_map.68.x_ref = f32[64,128]{1,0:T(8,128)} custom-call(f32[64,128]{1,0:T(8,128)} %pad_bitcast_fusion.1.x_ref), custom_call_target="tpu_custom_call" | custom-call | tf_op jit(solution)/shard_map/pallas_call | solution.py:215
  11.1 1.3 %fusion.49 = (f32[80,272]{1,0:T(8,128)}, f32[80,272]{1,0:T(8,128)}) fusion(s32[272]{0:T(512)S(1)} %add_add_fusion, s32[80]{0:T(128)S(1)} %iota_add_fusion.1), kind=kLoop, calls=%fused_computation.83 | loop fusion | flops 304640 | bytes 175488 | tf_op jit(solution)/shard_map/cos | solution.py:25
  12.3 0.0 copy-done.2
  12.3 1.2 %select_add_fusion.coef_ref = f32[6,256,128]{2,1,0:T(8,128)} fusion(s32[6,256,128]{2,1,0:T(8,128)S(1)} %copy-done.2), kind=kLoop, calls=%fused_computation.20 | loop fusion | flops 2162688 | bytes 1572864 | tf_op jit(solution)/shard_map/add | solution.py:31
  13.6 32.1 %shard_map.69 = (f32[16,64,128]{2,1,0:T(8,128)}, f32[2,42,8,128]{3,2,1,0:T(8,128)}, f32[2,42,8,272]{3,2,1,0:T(8,128)}) custom-call(f32[64,128]{1,0:T(8,128)} %shard_map.68.x_ref, f32[3,6,256,128]{3,2,1,0:T(8,128)} %e_ref.3, f32[3,6,256,128]{3,2,1,0:T(8,128)} %h_ref.3, f32[6,256,128]{2,1,0:T(8,128)} %select_add_fusion.coef_ref), custom_call_target="tpu_custom_call" | custom-call | tf_op jit(solution)/shard_map/pallas_call | solution.py:176
  45.7 1.4 %copy.43 = f32[2,8,64,128]{3,1,2,0:T(8,128)S(1)} copy(f32[2,8,64,128]{3,2,1,0:T(8,128)} %bitcast.90) | data formatting | bytes 1048576
  47.1 0.0 copy-start.5
  47.1 0.0 copy-start.6
  47.1 0.0 copy-start.7
  47.1 0.0 copy-start.8
  47.1 0.5 reshape.326
  47.7 0.2 copy-done.5
  47.9 0.0 copy-done.6
  47.9 0.0 copy-done.7
  47.9 0.0 copy-done.8
  47.9 1.3 %convolution_bitcast_fusion.6 = f32[80,144]{0,1:T(8,128)S(1)} fusion(f32[16,2,80,48]{3,2,1,0:T(8,128)S(1)} %reshape.326, f32[48,144]{1,0:T(8,128)S(1)} %copy-done.6, f32[16,144]{1,0:T(8,128)S(1)} %copy-done.8, f32[48,144]{1,0:T(8,128)S(1)} %copy-done.5, f32[16,144]{1,0:T(8,128)S(1)} %copy-done.7), kind=kOutput, calls=%fused_computation.8 | convolution fusion | flops 53415936 | bytes 832512 | tf_op jit(solution)/shard_map/cuv,cvy->uy/dot_general | solution.py:282
  49.2 1.3 %fusion.5 = f32[1,80,144]{1,2,0:T(8,128)S(1)} fusion(f32[80,144]{0,1:T(8,128)S(1)} %convolution_bitcast_fusion.6, f32[16,2,80,48]{3,2,1,0:T(8,128)S(1)} %reshape.326, f32[48,144]{1,0:T(8,128)S(1)} %copy-done.6, f32[16,144]{1,0:T(8,128)S(1)} %copy-done.8, f32[48,144]{1,0:T(8,128)S(1)} %copy-done.5, f32[16,144]{1,0:T(8,128)S(1)} %copy-done.7), kind=kOutput, calls=%fused_computation.15 | convolution fusion | flops 53427456 | bytes 906240 | tf_op jit(solution)/shard_map/cuv,cvy->uy/dot_general | solution.py:282
  50.5 1.3 %convolution_bitcast_fusion.8 = f32[80,144]{0,1:T(8,128)S(1)} fusion(f32[16,2,80,48]{3,2,1,0:T(8,128)S(1)} %reshape.326, f32[48,144]{1,0:T(8,128)S(1)} %copy-done.6, f32[16,144]{1,0:T(8,128)S(1)} %copy-done.8, f32[48,144]{1,0:T(8,128)S(1)} %copy-done.5, f32[16,144]{1,0:T(8,128)S(1)} %copy-done.7), kind=kOutput, calls=%fused_computation.10 | convolution fusion | flops 53415936 | bytes 832512 | tf_op jit(solution)/shard_map/cuv,cvy->uy/dot_general | solution.py:279
  51.8 1.3 %fusion.3 = f32[1,80,144]{1,2,0:T(8,128)S(1)} fusion(f32[80,144]{0,1:T(8,128)S(1)} %convolution_bitcast_fusion.8, f32[16,2,80,48]{3,2,1,0:T(8,128)S(1)} %reshape.326, f32[48,144]{1,0:T(8,128)S(1)} %copy-done.6, f32[16,144]{1,0:T(8,128)S(1)} %copy-done.8, f32[48,144]{1,0:T(8,128)S(1)} %copy-done.5, f32[16,144]{1,0:T(8,128)S(1)} %copy-done.7), kind=kOutput, calls=%fused_computation.13 | convolution fusion | flops 53427456 | bytes 906240 | tf_op jit(solution)/shard_map/cuv,cvy->uy/dot_general | solution.py:279
  53.2 0.1 copy.25
  53.3 0.1 reshape.327
  53.4 0.6 pad_bitcast_fusion.x_ref
  54.1 16.7 %shard_map.70 = f32[8,184,128]{2,1,0:T(8,128)} custom-call(f32[184,128]{1,0:T(8,128)} %pad_bitcast_fusion.x_ref), custom_call_target="tpu_custom_call" | custom-call | tf_op jit(solution)/shard_map/pallas_call | solution.py:78
  70.8 1.3 %copy.42 = f32[1,8,184,128]{3,1,2,0:T(8,128)S(1)} copy(f32[1,8,184,128]{3,2,1,0:T(8,128)} %bitcast.85) | data formatting | bytes 1507328
  72.1 0.0 copy-start
  72.2 0.0 copy-start.1
  72.2 0.0 copy-start.3
  72.2 0.0 copy-start.4
  72.2 0.9 reshape.330
  73.1 0.0 copy-done
  73.2 0.0 copy-done.1
  73.2 0.0 copy-done.3
  73.2 0.0 copy-done.4
  73.2 0.8 convolution_bitcast_fusion
  73.9 0.8 fusion.1
  74.7 0.1 copy.29
  74.9 0.8 convolution_bitcast_fusion.2
  75.6 0.8 fusion
  76.4 0.1 copy.28
  76.5 0.9 pad_maximum_fusion.plane_ref
  77.4 24.8 %shard_map.71 = (f32[3,6,256,128]{3,2,1,0:T(8,128)}, f32[3,6,256,128]{3,2,1,0:T(8,128)}) custom-call(f32[3,6,256,128]{3,2,1,0:T(8,128)} %e_ref.3, f32[3,6,256,128]{3,2,1,0:T(8,128)} %h_ref.3, f32[6,256,128]{2,1,0:T(8,128)} %select_add_fusion.coef_ref, f32[2,272,144]{2,1,0:T(8,128)} %pad_maximum_fusion.plane_ref, f32[2,42,8,128]{3,2,1,0:T(8,128)} %get-tuple-element.6.frow, ...), custom_call_target="tpu_custom_call" | custom-call | tf_op jit(solution)/shard_map/pallas_call | solution.py:401
  (10 shorter events, 0.1 us)
Async XLA Ops:
  0.6 11.7 %copy-start.2 = (s32[6,256,128]{2,1,0:T(8,128)S(1)}, s32[6,256,128]{2,1,0:T(8,128)}, u32[]{:S(2)}) copy-start(s32[6,256,128]{2,1,0:T(8,128)} %param.7) | copy-start | bytes 2359300
  47.1 0.8 copy-start.5
  47.1 0.8 copy-start.6
  47.1 0.8 copy-start.7
  47.1 0.8 copy-start.8
  72.1 1.0 copy-start
  72.2 1.0 copy-start.1
  72.2 1.0 copy-start.3
  72.2 1.0 copy-start.4

commit v12 on v10

--- a/solution.py
+++ b/solution.py
@@ -374,8 +374,8 @@
             ext[ez_ + s] = ext[ez_ + s] + c * ((h_y - behind_x(h_y)) - (h_x - behind_y(h_x)))
             return carry
 
-        lax.fori_loop(0, layers, h_update, 0)
-        lax.fori_loop(0, layers, e_update, 0)
+        lax.fori_loop(0, layers, h_update, 0, unroll=True)
+        lax.fori_loop(0, layers, e_update, 0, unroll=True)
         cosine = math.cos(OMEGA * (step + 1))
         sine = math.sin(OMEGA * (step + 1))
         p_re = cp[layers]

time: 103 us -> 99.6 us (0.967)
  Pallas kernels: 78.5 us -> 75.5 us
    pallas_call x1, Pallas kernels: 24.8 us -> 21.8 us  [per_device(): pl.pallas_call(yee_kernel, out_shape=(out, out), in_specs=[VMEM_SPEC] * 6...]
where the time goes in v12:
time: 99.6 us; the launch traced here: 99.2 us
  Pallas kernels  75.5 us (76%)
  matrix products  9.72 us (10%)
  local copies, waits for them, and re-layouts  7.08 us (7%)
  other arithmetic  5.93 us (6%)
    pallas_call x1, Pallas kernels, gather_with_halo(): pl.pallas_call(kernel, out_shape=(jax.ShapeDtypeStruct((n,) + block.shape...  33.4 us
    pallas_call x1, Pallas kernels, per_device(): pl.pallas_call(yee_kernel, out_shape=(out, out), in_specs=[VMEM_SPEC] * 6...  21.8 us
    pallas_call x1, Pallas kernels, gather_along(): pl.pallas_call(kernel, out_shape=jax.ShapeDtypeStruct((n,) + block.shape,...  15.5 us
    pallas_call x1, Pallas kernels, summed_over_pair(): pl.pallas_call(kernel, out_shape=jax.ShapeDtypeStruct(block.shape, block....  4.81 us
    cos x4, other arithmetic, phase_tables(): return (jnp.cos(angle), jnp.sin(angle))  3.66 us
    unnamed x20, local copies, waits for them, and re-layouts  2.85 us

profile of v12, /device:TPU:1, one launch (start us, length us, event | category | flops | bytes accessed | tf_op | source)
XLA Modules:
  0.0 99.2 jit_solution(17406540601131544452)
XLA Ops:
  0.6 0.0 copy-start.2
  0.7 0.1 add_add_fusion.1
  0.8 0.8 slice_bitcast_fusion.12
  1.6 0.1 add_add_fusion
  1.6 0.7 fusion.66
  2.4 0.8 fusion.64
  3.2 0.9 fusion.56
  4.1 1.2 %convolution_bitcast_fusion.4 = f32[4,2,80,32]{2,3,0,1:T(8,128)S(1)} fusion(f32[4,2,64,32]{2,3,1,0:T(8,128)} %param.5, s32[4]{0:T(128)S(1)} %get-tuple-element.17), kind=kOutput, calls=%fused_computation.6 | convolution fusion | flops 15790080 | bytes 147472 | tf_op jit(solution)/shard_map/puk,prkj->pruj/dot_general | solution.py:269
  5.2 0.3 convolution_bitcast_fusion.5
  5.5 0.1 reshape.323
  5.6 0.6 pad_bitcast_fusion.1.x_ref
  6.3 4.8 %shard_map.68.x_ref = f32[64,128]{1,0:T(8,128)} custom-call(f32[64,128]{1,0:T(8,128)} %pad_bitcast_fusion.1.x_ref), custom_call_target="tpu_custom_call" | custom-call | tf_op jit(solution)/shard_map/pallas_call | solution.py:215
  11.1 1.3 %fusion.49 = (f32[80,272]{1,0:T(8,128)}, f32[80,272]{1,0:T(8,128)}) fusion(s32[272]{0:T(512)S(1)} %add_add_fusion, s32[80]{0:T(128)S(1)} %iota_add_fusion.1), kind=kLoop, calls=%fused_computation.83 | loop fusion | flops 304640 | bytes 175488 | tf_op jit(solution)/shard_map/cos | solution.py:25
  12.3 0.0 copy-done.2
  12.3 1.2 %select_add_fusion.coef_ref = f32[6,256,128]{2,1,0:T(8,128)} fusion(s32[6,256,128]{2,1,0:T(8,128)S(1)} %copy-done.2), kind=kLoop, calls=%fused_computation.20 | loop fusion | flops 2162688 | bytes 1572864 | tf_op jit(solution)/shard_map/add | solution.py:31
  13.6 33.4 %shard_map.69 = (f32[16,64,128]{2,1,0:T(8,128)}, f32[2,42,8,128]{3,2,1,0:T(8,128)}, f32[2,42,8,272]{3,2,1,0:T(8,128)}) custom-call(f32[64,128]{1,0:T(8,128)} %shard_map.68.x_ref, f32[3,6,256,128]{3,2,1,0:T(8,128)} %e_ref.3, f32[3,6,256,128]{3,2,1,0:T(8,128)} %h_ref.3, f32[6,256,128]{2,1,0:T(8,128)} %select_add_fusion.coef_ref), custom_call_target="tpu_custom_call" | custom-call | tf_op jit(solution)/shard_map/pallas_call | solution.py:176
  46.9 1.4 %copy.43 = f32[2,8,64,128]{3,1,2,0:T(8,128)S(1)} copy(f32[2,8,64,128]{3,2,1,0:T(8,128)} %bitcast.90) | data formatting | bytes 1048576
  48.3 0.0 copy-start.5
  48.3 0.0 copy-start.6
  48.3 0.0 copy-start.7
  48.3 0.0 copy-start.8
  48.3 0.5 reshape.326
  48.9 0.2 copy-done.5
  49.1 0.0 copy-done.6
  49.1 0.0 copy-done.7
  49.1 0.0 copy-done.8
  49.1 1.3 %convolution_bitcast_fusion.6 = f32[80,144]{0,1:T(8,128)S(1)} fusion(f32[16,2,80,48]{3,2,1,0:T(8,128)S(1)} %reshape.326, f32[48,144]{1,0:T(8,128)S(1)} %copy-done.6, f32[16,144]{1,0:T(8,128)S(1)} %copy-done.8, f32[48,144]{1,0:T(8,128)S(1)} %copy-done.5, f32[16,144]{1,0:T(8,128)S(1)} %copy-done.7), kind=kOutput, calls=%fused_computation.8 | convolution fusion | flops 53415936 | bytes 832512 | tf_op jit(solution)/shard_map/cuv,cvy->uy/dot_general | solution.py:282
  50.4 1.3 %fusion.5 = f32[1,80,144]{1,2,0:T(8,128)S(1)} fusion(f32[80,144]{0,1:T(8,128)S(1)} %convolution_bitcast_fusion.6, f32[16,2,80,48]{3,2,1,0:T(8,128)S(1)} %reshape.326, f32[48,144]{1,0:T(8,128)S(1)} %copy-done.6, f32[16,144]{1,0:T(8,128)S(1)} %copy-done.8, f32[48,144]{1,0:T(8,128)S(1)} %copy-done.5, f32[16,144]{1,0:T(8,128)S(1)} %copy-done.7), kind=kOutput, calls=%fused_computation.15 | convolution fusion | flops 53427456 | bytes 906240 | tf_op jit(solution)/shard_map/cuv,cvy->uy/dot_general | solution.py:282
  51.7 1.3 %convolution_bitcast_fusion.8 = f32[80,144]{0,1:T(8,128)S(1)} fusion(f32[16,2,80,48]{3,2,1,0:T(8,128)S(1)} %reshape.326, f32[48,144]{1,0:T(8,128)S(1)} %copy-done.6, f32[16,144]{1,0:T(8,128)S(1)} %copy-done.8, f32[48,144]{1,0:T(8,128)S(1)} %copy-done.5, f32[16,144]{1,0:T(8,128)S(1)} %copy-done.7), kind=kOutput, calls=%fused_computation.10 | convolution fusion | flops 53415936 | bytes 832512 | tf_op jit(solution)/shard_map/cuv,cvy->uy/dot_general | solution.py:279
  53.0 1.3 %fusion.3 = f32[1,80,144]{1,2,0:T(8,128)S(1)} fusion(f32[80,144]{0,1:T(8,128)S(1)} %convolution_bitcast_fusion.8, f32[16,2,80,48]{3,2,1,0:T(8,128)S(1)} %reshape.326, f32[48,144]{1,0:T(8,128)S(1)} %copy-done.6, f32[16,144]{1,0:T(8,128)S(1)} %copy-done.8, f32[48,144]{1,0:T(8,128)S(1)} %copy-done.5, f32[16,144]{1,0:T(8,128)S(1)} %copy-done.7), kind=kOutput, calls=%fused_computation.13 | convolution fusion | flops 53427456 | bytes 906240 | tf_op jit(solution)/shard_map/cuv,cvy->uy/dot_general | solution.py:279
  54.4 0.1 copy.25
  54.5 0.1 reshape.327
  54.6 0.6 pad_bitcast_fusion.x_ref
  55.3 15.5 %shard_map.70 = f32[8,184,128]{2,1,0:T(8,128)} custom-call(f32[184,128]{1,0:T(8,128)} %pad_bitcast_fusion.x_ref), custom_call_target="tpu_custom_call" | custom-call | tf_op jit(solution)/shard_map/pallas_call | solution.py:78
  70.8 1.3 %copy.42 = f32[1,8,184,128]{3,1,2,0:T(8,128)S(1)} copy(f32[1,8,184,128]{3,2,1,0:T(8,128)} %bitcast.85) | data formatting | bytes 1507328
  72.1 0.0 copy-start
  72.2 0.0 copy-start.1
  72.2 0.0 copy-start.3
  72.2 0.0 copy-start.4
  72.2 0.9 reshape.330
  73.1 0.0 copy-done
  73.2 0.0 copy-done.1
  73.2 0.0 copy-done.3
  73.2 0.0 copy-done.4
  73.2 0.8 convolution_bitcast_fusion
  73.9 0.8 fusion.1
  74.7 0.1 copy.29
  74.9 0.8 convolution_bitcast_fusion.2
  75.6 0.8 fusion
  76.4 0.1 copy.28
  76.5 0.9 pad_maximum_fusion.plane_ref
  77.4 21.8 %shard_map.71 = (f32[3,6,256,128]{3,2,1,0:T(8,128)}, f32[3,6,256,128]{3,2,1,0:T(8,128)}) custom-call(f32[3,6,256,128]{3,2,1,0:T(8,128)} %e_ref.3, f32[3,6,256,128]{3,2,1,0:T(8,128)} %h_ref.3, f32[6,256,128]{2,1,0:T(8,128)} %select_add_fusion.coef_ref, f32[2,272,144]{2,1,0:T(8,128)} %pad_maximum_fusion.plane_ref, f32[2,42,8,128]{3,2,1,0:T(8,128)} %get-tuple-element.6.frow, ...), custom_call_target="tpu_custom_call" | custom-call | tf_op jit(solution)/shard_map/pallas_call | solution.py:401
  (10 shorter events, 0.1 us)
Async XLA Ops:
  0.6 11.7 %copy-start.2 = (s32[6,256,128]{2,1,0:T(8,128)S(1)}, s32[6,256,128]{2,1,0:T(8,128)}, u32[]{:S(2)}) copy-start(s32[6,256,128]{2,1,0:T(8,128)} %param.7) | copy-start | bytes 2359300
  48.3 0.8 copy-start.5
  48.3 0.8 copy-start.6
  48.3 0.8 copy-start.7
  48.3 0.8 copy-start.8
  72.1 1.0 %copy-start = (f32[80,272]{1,0:T(8,128)S(1)}, f32[80,272]{1,0:T(8,128)}, u32[]{:S(2)}) copy-start(f32[80,272]{1,0:T(8,128)} %get-tuple-element.10) | copy-start | bytes 261124
  72.2 1.0 %copy-start.1 = (f32[80,272]{1,0:T(8,128)S(1)}, f32[80,272]{1,0:T(8,128)}, u32[]{:S(2)}) copy-start(f32[80,272]{1,0:T(8,128)} %get-tuple-element.11) | copy-start | bytes 261124
  72.2 1.0 %copy-start.3 = (f32[8,272]{1,0:T(8,128)S(1)}, f32[8,272]{1,0:T(8,128)}, u32[]{:S(2)}) copy-start(f32[8,272]{1,0:T(8,128)} %get-tuple-element.8) | copy-start | bytes 26116
  72.2 1.0 %copy-start.4 = (f32[8,272]{1,0:T(8,128)S(1)}, f32[8,272]{1,0:T(8,128)}, u32[]{:S(2)}) copy-start(f32[8,272]{1,0:T(8,128)} %get-tuple-element.9) | copy-start | bytes 26116

commit v13 on v12

--- a/solution.py
+++ b/solution.py
@@ -330,7 +330,7 @@
         place_part(ext, (comp + 3) * slab + z + 1, h_ref[comp, z], h + 3 * layers)
         return carry
 
-    lax.fori_loop(0, 3 * layers, place_fields, 0)
+    lax.fori_loop(0, 3 * layers, place_fields, 0, unroll=True)
     for z in range(layers):
         place_part(cp, z, coef_ref[z], n_field + z)
     zero = jnp.zeros((rows, lanes), jnp.float32)

time: 99.6 us -> 98.1 us (0.985)
  Pallas kernels: 75.5 us -> 74.1 us
    pallas_call x1, Pallas kernels: 21.8 us -> 20.4 us  [per_device(): pl.pallas_call(yee_kernel, out_shape=(out, out), in_specs=[VMEM_SPEC] * 6...]
where the time goes in v13:
time: 98.1 us; the launch traced here: 97.7 us
  Pallas kernels  74.1 us (76%)
  matrix products  9.72 us (10%)
  local copies, waits for them, and re-layouts  7.08 us (7%)
  other arithmetic  5.93 us (6%)
    pallas_call x1, Pallas kernels, gather_with_halo(): pl.pallas_call(kernel, out_shape=(jax.ShapeDtypeStruct((n,) + block.shape...  33.3 us
    pallas_call x1, Pallas kernels, per_device(): pl.pallas_call(yee_kernel, out_shape=(out, out), in_specs=[VMEM_SPEC] * 6...  20.4 us
    pallas_call x1, Pallas kernels, gather_along(): pl.pallas_call(kernel, out_shape=jax.ShapeDtypeStruct((n,) + block.shape,...  15.6 us
    pallas_call x1, Pallas kernels, summed_over_pair(): pl.pallas_call(kernel, out_shape=jax.ShapeDtypeStruct(block.shape, block....  4.81 us
    cos x4, other arithmetic, phase_tables(): return (jnp.cos(angle), jnp.sin(angle))  3.66 us
    unnamed x20, local copies, waits for them, and re-layouts  2.85 us

profile of v13, /device:TPU:1, one launch (start us, length us, event | category | flops | bytes accessed | tf_op | source)
XLA Modules:
  0.0 97.7 jit_solution(16734169019741586425)
XLA Ops:
  0.6 0.0 copy-start.2
  0.7 0.1 add_add_fusion.1
  0.8 0.8 slice_bitcast_fusion.12
  1.6 0.1 add_add_fusion
  1.6 0.7 fusion.66
  2.4 0.8 fusion.64
  3.2 0.9 fusion.56
  4.1 1.2 %convolution_bitcast_fusion.4 = f32[4,2,80,32]{2,3,0,1:T(8,128)S(1)} fusion(f32[4,2,64,32]{2,3,1,0:T(8,128)} %param.5, s32[4]{0:T(128)S(1)} %get-tuple-element.17), kind=kOutput, calls=%fused_computation.6 | convolution fusion | flops 15790080 | bytes 147472 | tf_op jit(solution)/shard_map/puk,prkj->pruj/dot_general | solution.py:269
  5.2 0.3 convolution_bitcast_fusion.5
  5.5 0.1 reshape.323
  5.6 0.6 pad_bitcast_fusion.1.x_ref
  6.3 4.8 %shard_map.68.x_ref = f32[64,128]{1,0:T(8,128)} custom-call(f32[64,128]{1,0:T(8,128)} %pad_bitcast_fusion.1.x_ref), custom_call_target="tpu_custom_call" | custom-call | tf_op jit(solution)/shard_map/pallas_call | solution.py:215
  11.1 1.3 %fusion.49 = (f32[80,272]{1,0:T(8,128)}, f32[80,272]{1,0:T(8,128)}) fusion(s32[272]{0:T(512)S(1)} %add_add_fusion, s32[80]{0:T(128)S(1)} %iota_add_fusion.1), kind=kLoop, calls=%fused_computation.83 | loop fusion | flops 304640 | bytes 175488 | tf_op jit(solution)/shard_map/cos | solution.py:25
  12.3 0.0 copy-done.2
  12.3 1.2 %select_add_fusion.coef_ref = f32[6,256,128]{2,1,0:T(8,128)} fusion(s32[6,256,128]{2,1,0:T(8,128)S(1)} %copy-done.2), kind=kLoop, calls=%fused_computation.20 | loop fusion | flops 2162688 | bytes 1572864 | tf_op jit(solution)/shard_map/add | solution.py:31
  13.6 33.3 %shard_map.69 = (f32[16,64,128]{2,1,0:T(8,128)}, f32[2,42,8,128]{3,2,1,0:T(8,128)}, f32[2,42,8,272]{3,2,1,0:T(8,128)}) custom-call(f32[64,128]{1,0:T(8,128)} %shard_map.68.x_ref, f32[3,6,256,128]{3,2,1,0:T(8,128)} %e_ref.3, f32[3,6,256,128]{3,2,1,0:T(8,128)} %h_ref.3, f32[6,256,128]{2,1,0:T(8,128)} %select_add_fusion.coef_ref), custom_call_target="tpu_custom_call" | custom-call | tf_op jit(solution)/shard_map/pallas_call | solution.py:176
  46.8 1.4 %copy.43 = f32[2,8,64,128]{3,1,2,0:T(8,128)S(1)} copy(f32[2,8,64,128]{3,2,1,0:T(8,128)} %bitcast.90) | data formatting | bytes 1048576
  48.2 0.0 copy-start.5
  48.2 0.0 copy-start.6
  48.2 0.0 copy-start.7
  48.2 0.0 copy-start.8
  48.3 0.5 reshape.326
  48.8 0.2 copy-done.5
  49.0 0.0 copy-done.6
  49.0 0.0 copy-done.7
  49.0 0.0 copy-done.8
  49.0 1.3 %convolution_bitcast_fusion.6 = f32[80,144]{0,1:T(8,128)S(1)} fusion(f32[16,2,80,48]{3,2,1,0:T(8,128)S(1)} %reshape.326, f32[48,144]{1,0:T(8,128)S(1)} %copy-done.6, f32[16,144]{1,0:T(8,128)S(1)} %copy-done.8, f32[48,144]{1,0:T(8,128)S(1)} %copy-done.5, f32[16,144]{1,0:T(8,128)S(1)} %copy-done.7), kind=kOutput, calls=%fused_computation.8 | convolution fusion | flops 53415936 | bytes 832512 | tf_op jit(solution)/shard_map/cuv,cvy->uy/dot_general | solution.py:282
  50.3 1.3 %fusion.5 = f32[1,80,144]{1,2,0:T(8,128)S(1)} fusion(f32[80,144]{0,1:T(8,128)S(1)} %convolution_bitcast_fusion.6, f32[16,2,80,48]{3,2,1,0:T(8,128)S(1)} %reshape.326, f32[48,144]{1,0:T(8,128)S(1)} %copy-done.6, f32[16,144]{1,0:T(8,128)S(1)} %copy-done.8, f32[48,144]{1,0:T(8,128)S(1)} %copy-done.5, f32[16,144]{1,0:T(8,128)S(1)} %copy-done.7), kind=kOutput, calls=%fused_computation.15 | convolution fusion | flops 53427456 | bytes 906240 | tf_op jit(solution)/shard_map/cuv,cvy->uy/dot_general | solution.py:282
  51.6 1.3 %convolution_bitcast_fusion.8 = f32[80,144]{0,1:T(8,128)S(1)} fusion(f32[16,2,80,48]{3,2,1,0:T(8,128)S(1)} %reshape.326, f32[48,144]{1,0:T(8,128)S(1)} %copy-done.6, f32[16,144]{1,0:T(8,128)S(1)} %copy-done.8, f32[48,144]{1,0:T(8,128)S(1)} %copy-done.5, f32[16,144]{1,0:T(8,128)S(1)} %copy-done.7), kind=kOutput, calls=%fused_computation.10 | convolution fusion | flops 53415936 | bytes 832512 | tf_op jit(solution)/shard_map/cuv,cvy->uy/dot_general | solution.py:279
  52.9 1.3 %fusion.3 = f32[1,80,144]{1,2,0:T(8,128)S(1)} fusion(f32[80,144]{0,1:T(8,128)S(1)} %convolution_bitcast_fusion.8, f32[16,2,80,48]{3,2,1,0:T(8,128)S(1)} %reshape.326, f32[48,144]{1,0:T(8,128)S(1)} %copy-done.6, f32[16,144]{1,0:T(8,128)S(1)} %copy-done.8, f32[48,144]{1,0:T(8,128)S(1)} %copy-done.5, f32[16,144]{1,0:T(8,128)S(1)} %copy-done.7), kind=kOutput, calls=%fused_computation.13 | convolution fusion | flops 53427456 | bytes 906240 | tf_op jit(solution)/shard_map/cuv,cvy->uy/dot_general | solution.py:279
  54.3 0.1 copy.25
  54.4 0.1 reshape.327
  54.5 0.6 pad_bitcast_fusion.x_ref
  55.2 15.6 %shard_map.70 = f32[8,184,128]{2,1,0:T(8,128)} custom-call(f32[184,128]{1,0:T(8,128)} %pad_bitcast_fusion.x_ref), custom_call_target="tpu_custom_call" | custom-call | tf_op jit(solution)/shard_map/pallas_call | solution.py:78
  70.8 1.3 %copy.42 = f32[1,8,184,128]{3,1,2,0:T(8,128)S(1)} copy(f32[1,8,184,128]{3,2,1,0:T(8,128)} %bitcast.85) | data formatting | bytes 1507328
  72.1 0.0 copy-start
  72.2 0.0 copy-start.1
  72.2 0.0 copy-start.3
  72.2 0.0 copy-start.4
  72.2 0.9 reshape.330
  73.1 0.0 copy-done
  73.1 0.0 copy-done.1
  73.2 0.0 copy-done.3
  73.2 0.0 copy-done.4
  73.2 0.8 convolution_bitcast_fusion
  73.9 0.8 fusion.1
  74.7 0.1 copy.29
  74.8 0.8 convolution_bitcast_fusion.2
  75.6 0.8 fusion
  76.4 0.1 copy.28
  76.5 0.9 pad_maximum_fusion.plane_ref
  77.4 20.4 %shard_map.71 = (f32[3,6,256,128]{3,2,1,0:T(8,128)}, f32[3,6,256,128]{3,2,1,0:T(8,128)}) custom-call(f32[3,6,256,128]{3,2,1,0:T(8,128)} %e_ref.3, f32[3,6,256,128]{3,2,1,0:T(8,128)} %h_ref.3, f32[6,256,128]{2,1,0:T(8,128)} %select_add_fusion.coef_ref, f32[2,272,144]{2,1,0:T(8,128)} %pad_maximum_fusion.plane_ref, f32[2,42,8,128]{3,2,1,0:T(8,128)} %get-tuple-element.6.frow, ...), custom_call_target="tpu_custom_call" | custom-call | tf_op jit(solution)/shard_map/pallas_call | solution.py:401
  (10 shorter events, 0.1 us)
Async XLA Ops:
  0.6 11.7 %copy-start.2 = (s32[6,256,128]{2,1,0:T(8,128)S(1)}, s32[6,256,128]{2,1,0:T(8,128)}, u32[]{:S(2)}) copy-start(s32[6,256,128]{2,1,0:T(8,128)} %param.7) | copy-start | bytes 2359300
  48.2 0.8 copy-start.5
  48.2 0.8 copy-start.6
  48.2 0.8 copy-start.7
  48.2 0.8 copy-start.8
  72.1 1.0 %copy-start = (f32[80,272]{1,0:T(8,128)S(1)}, f32[80,272]{1,0:T(8,128)}, u32[]{:S(2)}) copy-start(f32[80,272]{1,0:T(8,128)} %get-tuple-element.10) | copy-start | bytes 261124
  72.2 1.0 %copy-start.1 = (f32[80,272]{1,0:T(8,128)S(1)}, f32[80,272]{1,0:T(8,128)}, u32[]{:S(2)}) copy-start(f32[80,272]{1,0:T(8,128)} %get-tuple-element.11) | copy-start | bytes 261124
  72.2 1.0 %copy-start.3 = (f32[8,272]{1,0:T(8,128)S(1)}, f32[8,272]{1,0:T(8,128)}, u32[]{:S(2)}) copy-start(f32[8,272]{1,0:T(8,128)} %get-tuple-element.8) | copy-start | bytes 26116
  72.2 1.0 %copy-start.4 = (f32[8,272]{1,0:T(8,128)S(1)}, f32[8,272]{1,0:T(8,128)}, u32[]{:S(2)}) copy-start(f32[8,272]{1,0:T(8,128)} %get-tuple-element.9) | copy-start | bytes 26116
